TPU v7x, 32 devices: a whole 2x2x4 slice. The times are simulated.
32 devices in a mesh: groups: 2 (over y), tile: 8 (over z, x), head: 2 (over core).
Axes of the slice: x: 2, y: 2, z: 4, core: 2. Of those that a mesh axis runs over, the one named last changes fastest.
Arguments:
- tissue_tiles: bfloat16 [128, 32, 32, 128], P(('groups', 'tile', 'head')), parts along dimension 0, may hold values from -64 to 64
- neighbours: int32 [128, 8], P(('groups', 'tile', 'head')), parts along dimension 0, may hold values from -1 to 63, as said below
- conv_weight: bfloat16 [3, 3, 128, 128], replicated, may hold values from -0.1875 to 0.1875
- conv_bias: float32 [128], replicated, may hold values from -2 to 2
- head_weight: float32 [128], replicated, may hold values from -3 to 3
- slide_label: int32 [2], P('groups'), parts along dimension 0, may hold values from 0 to 100
Outputs:
- grad_tiles: float32 [128, 32, 32, 128], P(('groups', 'tile', 'head')), parts along dimension 0
There are 2 independent parts, one for each index of `groups`. A program takes and returns all parts, laid end to end along the dimension named above; an argument that names none is the same for every part. Nothing has to cross between parts.
Inputs may be any that keep to these rules, and one draw needn't show every extreme that they name: `neighbours`: tiles are listed row by row of a strip of the slide 3 tiles wide in which background cells are left out; entry k of a tile is its neighbour in direction k or -1 where that cell is background or outside the strip. Neighbour relations are mutual.
All inputs are finite; a program needn't handle non-finite values.
Results may differ from a plain program's by a relative error of at most 0.0029.
Values may be sent and summed in bfloat16 or wider, within the bound.
No kernel may reach another device: no remote copies, remote signals or barrier semaphores. Data moves between devices by JAX's collectives and lax.ppermute only.
A program may use at most 64 MiB of HBM per device.

v0:
```python
import jax
import jax.numpy as jnp
from jax import lax
from jax.sharding import PartitionSpec as P

DILATION_STEP = 2


def with_halo(shard, sides, width):
    for axis, dim in sides:
        size, length = (lax.axis_size(axis), shard.shape[dim])
        up = [(i, (i + 1) % size) for i in range(size - 1)]
        down = [(j, i) for i, j in up]
        last = lax.slice_in_dim(shard, length - width, length, axis=dim)
        first = lax.slice_in_dim(shard, 0, width, axis=dim)
        before = lax.ppermute(last, axis, up)
        after = lax.ppermute(first, axis, down)
        shard = jnp.concatenate([before, shard, after], axis=dim)
    return shard


def edge_strips(tile_feature_maps):
    tile_count = tile_feature_maps.shape[0]
    side_length = tile_feature_maps.shape[1]
    upper_margin = tile_feature_maps[:, :DILATION_STEP].reshape(tile_count, -1)
    lower_margin = tile_feature_maps[:, side_length - DILATION_STEP :].reshape(tile_count, -1)
    left_margin = tile_feature_maps[:, :, :DILATION_STEP].reshape(tile_count, -1)
    right_margin = tile_feature_maps[:, :, side_length - DILATION_STEP :].reshape(tile_count, -1)
    return (upper_margin, lower_margin, left_margin, right_margin)


def split_four(received):
    width = received.shape[1] // 4
    return tuple((received[:, part_no * width : (part_no + 1) * width] for part_no in range(4)))


def feature_window(tile_feature_maps):
    strips = edge_strips(tile_feature_maps)
    tile_count = tile_feature_maps.shape[0]
    packed = jnp.concatenate(strips, 1)
    received = with_halo(packed, ((("tile", "head"), 0),), tile_count)
    return split_four(received)


def gradient_window(tile_feature_maps):
    strips = edge_strips(tile_feature_maps)
    tile_count = tile_feature_maps.shape[0]
    packed = jnp.concatenate(strips, 1)
    received = with_halo(packed, ((("tile", "head"), 0),), tile_count)
    return split_four(received)


def assemble(tile_feature_maps, window, chooser):
    tile_count, side_length, _, channel_count = tile_feature_maps.shape
    upper_frame, lower_frame, left_window, right_window = window
    flattened_shape = (tile_count, DILATION_STEP, side_length, channel_count)
    stacked_shape = (tile_count, side_length, DILATION_STEP, channel_count)

    def choose_band(strips, direction, shape):
        chosen = jnp.dot(chooser[:, direction, :], strips, preferred_element_type=jnp.float32)
        return chosen.astype(jnp.bfloat16).reshape(shape)

    rows_above_tile = jnp.concatenate(
        [
            choose_band(lower_frame, 0, flattened_shape)[:, :, side_length - DILATION_STEP :],
            choose_band(lower_frame, 1, flattened_shape),
            choose_band(lower_frame, 2, flattened_shape)[:, :, :DILATION_STEP],
        ],
        2,
    )
    middle_rows = jnp.concatenate(
        [
            choose_band(right_window, 3, stacked_shape),
            tile_feature_maps,
            choose_band(left_window, 4, stacked_shape),
        ],
        2,
    )
    rows_below_tile = jnp.concatenate(
        [
            choose_band(upper_frame, 5, flattened_shape)[:, :, side_length - DILATION_STEP :],
            choose_band(upper_frame, 6, flattened_shape),
            choose_band(upper_frame, 7, flattened_shape)[:, :, :DILATION_STEP],
        ],
        2,
    )
    return jnp.concatenate([rows_above_tile, middle_rows, rows_below_tile], 1)


def dilated(padded_maps, kernel_weight):
    return lax.conv_general_dilated(
        padded_maps,
        kernel_weight,
        (1, 1),
        "VALID",
        rhs_dilation=(DILATION_STEP, DILATION_STEP),
        dimension_numbers=("NHWC", "HWIO", "NHWC"),
        preferred_element_type=jnp.float32,
    )


def body(tissue_tiles, neighbours, conv_weight, conv_bias, head_weight, slide_label):
    tile_count, side_length, _, channel_count = tissue_tiles.shape
    start_index = lax.axis_index(("tile", "head")) * tile_count
    slot_ids = jnp.arange(3 * tile_count, dtype=jnp.int32)
    local_ids = neighbours - start_index + tile_count
    chooser = ((local_ids[:, :, None] == slot_ids) & (neighbours[:, :, None] >= 0)).astype(
        jnp.bfloat16
    )
    padded_maps = assemble(tissue_tiles, feature_window(tissue_tiles), chooser)
    pre = dilated(padded_maps, conv_weight) + conv_bias
    sigmoid_pre = jax.nn.sigmoid(pre)
    local_sum = jnp.sum(pre * sigmoid_pre * head_weight)
    total_sum = lax.psum(local_sum, ("tile", "head"))
    all_tiles = tile_count * lax.axis_size(("tile", "head"))
    slide_score = total_sum / (all_tiles * side_length * side_length * channel_count)
    loss_slope = jax.nn.sigmoid(slide_score) - slide_label[0].astype(jnp.float32) / 100.0
    grad_pre = (loss_slope * head_weight * sigmoid_pre * (1.0 + pre * (1.0 - sigmoid_pre))).astype(
        jnp.bfloat16
    )
    grad_padded = assemble(grad_pre, gradient_window(grad_pre), chooser)
    flipped = jnp.transpose(conv_weight[::-1, ::-1], (0, 1, 3, 2))
    return dilated(grad_padded, flipped)


def solution(mesh):
    return jax.shard_map(
        body,
        mesh=mesh,
        in_specs=(
            P(("groups", "tile", "head"), None, None, None),
            P(("groups", "tile", "head"), None),
            P(),
            P(),
            P(),
            P("groups"),
        ),
        out_specs=P(("groups", "tile", "head"), None, None, None),
        check_vma=False,
    )
```

profile of v0, /device:TPU:1, one launch (start us, length us, event | category | flops | bytes accessed | tf_op | source)
XLA Modules:
  0.0 79.9 jit_solution(1276034632636055342)
XLA Ops:
  0.0 0.9 %fusion.45 = (bf16[4,2,32,128]{3,2,1,0:T(8,128)(2,1)S(1)}, bf16[4,2,32,128]{3,2,1,0:T(8,128)(2,1)S(1)}) fusion(bf16[4,32,32,128]{3,2,1,0:T(8,128)(2,1)} %param.6), kind=kLoop, calls=%fused_computation.92 | loop fusion | bytes 262144 | tf_op jit(solution)/shard_map/slice | solution.py:26
  0.9 1.1 %fusion.44 = (bf16[4,32,2,128]{3,2,1,0:T(2,128)(2,1)S(1)}, bf16[4,32,2,128]{3,2,1,0:T(2,128)(2,1)S(1)}) fusion(bf16[4,32,32,128]{3,2,1,0:T(8,128)(2,1)} %param.6), kind=kLoop, calls=%fused_computation.91 | loop fusion | bytes 262144 | tf_op jit(solution)/shard_map/slice | solution.py:28
  2.1 0.1 bitcast_dynamic-update-slice_fusion.3
  2.2 0.1 bitcast_dynamic-update-slice_fusion.2
  2.3 4.5 %collective-permute-start = (bf16[4,32768]{1,0:T(4,128)(2,1)S(1)}, bf16[4,32768]{1,0:T(4,128)(2,1)S(1)}, u32[]{:S(2)}, u32[]{:S(2)}) collective-permute-start(bf16[4,32768]{1,0:T(4,128)(2,1)S(1)} %constant_dynamic-update-slice_fusion), channel_id=1, source_target_pairs={{0,1},{1,2},{2,3},{3,4},{4,5},{5,6},{6,7},{7,8},{8,9},{9,10},{10,1... | collective-permute-start | bytes 786440 | tf_op jit(solution)/shard_map/ppermute | solution.py:16
  6.8 1.9 %collective-permute-start.1 = (bf16[4,32768]{1,0:T(4,128)(2,1)S(1)}, bf16[4,32768]{1,0:T(4,128)(2,1)S(1)}, u32[]{:S(2)}, u32[]{:S(2)}) collective-permute-start(bf16[4,32768]{1,0:T(4,128)(2,1)S(1)} %constant_dynamic-update-slice_fusion), channel_id=1, source_target_pairs={{1,0},{2,1},{3,2},{4,3},{5,4},{6,5},{7,6},{8,7},{9,8},{10,9},{11,1... | collective-permute-start | bytes 786440 | tf_op jit(solution)/shard_map/ppermute | solution.py:17
  8.8 0.7 subtract_add_fusion
  9.5 0.7 broadcast_compare_fusion
  10.2 0.1 copy.11
  10.2 0.1 copy.12
  11.0 0.1 fusion.41
  11.1 3.4 %collective-permute-done.1 = bf16[4,32768]{1,0:T(4,128)(2,1)S(1)} collective-permute-done((bf16[4,32768]{1,0:T(4,128)(2,1)S(1)}, bf16[4,32768]{1,0:T(4,128)(2,1)S(1)}, u32[]{:S(2)}, u32[]{:S(2)}) %collective-permute-start.1) | collective-permute-done | bytes 262176 | tf_op jit(solution)/shard_map/ppermute | solution.py:17
  14.5 0.4 pad_maximum_fusion
  15.0 0.2 fusion.13
  15.2 0.2 fusion.15
  15.3 0.2 fusion.16
  15.5 0.2 fusion.18
  15.7 0.2 fusion.14
  15.8 0.2 fusion.17
  16.0 0.2 convolution_convert_fusion.12
  16.2 0.2 convolution_convert_fusion.11
  16.5 0.1 reshape.88
  16.6 0.1 reshape.89
  16.7 1.0 %maximum_bitcast_fusion = bf16[36,4,36,128]{3,2,0,1:T(8,128)(2,1)S(1)} fusion(bf16[4,2,2,128]{3,2,1,0:T(2,128)(2,1)S(1)} %slice.159, bf16[4,2,32,128]{3,2,1,0:T(8,128)(2,1)S(1)} %bitcast.136, bf16[4,2,2,128]{3,2,1,0:T(2,128)(2,1)S(1)} %slice.156, bf16[4,32,2,128]{3,2,1,0:T(2,128)(2,1)S(1)} %reshape.89, bf16[4,32,32,128]{3,2,1,0:T(8,128)(2,1)S(1)} %copy-done.1, ...), kind=kLoop, calls=%fused_computation.33 | loop fusion | flops 11943936 | bytes 2654208 | tf_op jit(solution)/shard_map/concatenate | solution.py:87
  17.7 0.7 copy.38
  18.4 0.5 pad.clone
  18.9 0.4 slice.160
  19.3 1.1 %fusion.2 = bf16[36,4,8,9,128]{4,1,3,2,0:T(4,128)(2,1)S(1)} fusion(bf16[36,4,7,4,128]{4,1,3,2,0:T(4,128)(2,1)S(1)} %slice.160, bf16[36,4,8,5,128]{4,1,3,2,0:T(4,128)(2,1)S(1)} %bitcast.130), kind=kLoop, calls=%fused_computation.19 | loop fusion | flops 7962624 | bytes 5160960 | tf_op jit(solution)/shard_map/conv_general_dilated | solution.py:91
  20.5 4.3 %select_reduce_fusion = (f32[]{:T(128)}, f32[32,32,5,128]{3,1,2,0:T(8,128)S(1)}) fusion(f32[128]{0:T(128)S(1)} %copy-done.4, f32[128]{0:T(128)S(1)} %copy-done.3, pred[32,5]{0,1:T(8,128)(4,1)S(1)} %copy-done.2, bf16[3,3,128,128]{3,2,1,0:T(8,128)(2,1)S(1)} %copy-done, bf16[36,4,8,9,128]{4,1,3,2,0:T(4,128)(2,1)S(1)} %fusion.2), kind=kOutput, calls=%fused_computation.28 | convolution fusion | flops 1515847680 | bytes 5571748 | tf_op jit(solution)/shard_map/conv_general_dilated | solution.py:91
  24.8 28.4 %psum.7 = f32[]{:T(128)} all-reduce(f32[]{:T(128)} %get-tuple-element.13), channel_id=1, replica_groups=mesh['groups'=2,'tile'=8,'head'=2] {'tile','head'}, use_global_device_ids=true, to_apply=%region_1.0 | all-reduce | flops 1 | bytes 8 | tf_op jit(solution)/shard_map/psum | solution.py:114
  54.0 1.1 %multiply_convert_fusion = bf16[32,32,5,128]{3,1,2,0:T(8,128)(2,1)S(1)} fusion(f32[32,32,5,128]{3,1,2,0:T(8,128)S(1)} %get-tuple-element.14, f32[128]{0:T(128)S(1)} %broadcast_multiply_fusion, f32[128]{0:T(128)S(1)} %copy-done.3, pred[32,5]{0,1:T(8,128)(4,1)S(1)} %copy-done.2), kind=kLoop, calls=%fused_computation.27 | loop fusion | flops 7208960 | bytes 3933344 | tf_op jit(solution)/shard_map/convert_element_type | solution.py:118
  55.1 0.5 copy.19
  55.6 0.1 slice_bitcast_fusion.1
  55.7 0.1 copy.20
  55.8 0.1 copy.15
  55.9 0.1 bitcast_dynamic-update-slice_fusion.1
  56.0 0.1 copy.17
  56.2 0.1 copy.21
  56.2 0.1 bitcast_dynamic-update-slice_fusion
  56.4 2.1 %collective-permute-start.2 = (bf16[4,32768]{1,0:T(4,128)(2,1)S(1)}, bf16[4,32768]{1,0:T(4,128)(2,1)S(1)}, u32[]{:S(2)}, u32[]{:S(2)}) collective-permute-start(bf16[4,32768]{1,0:T(4,128)(2,1)S(1)} %constant_dynamic-update-slice_fusion.2), channel_id=1, source_target_pairs={{0,1},{1,2},{2,3},{3,4},{4,5},{5,6},{6,7},{7,8},{8,9},{9,10},{10,1... | collective-permute-start | bytes 786440 | tf_op jit(solution)/shard_map/ppermute | solution.py:16
  58.5 3.5 %collective-permute-start.3 = (bf16[4,32768]{1,0:T(4,128)(2,1)S(1)}, bf16[4,32768]{1,0:T(4,128)(2,1)S(1)}, u32[]{:S(2)}, u32[]{:S(2)}) collective-permute-start(bf16[4,32768]{1,0:T(4,128)(2,1)S(1)} %constant_dynamic-update-slice_fusion.2), channel_id=1, source_target_pairs={{1,0},{2,1},{3,2},{4,3},{5,4},{6,5},{7,6},{8,7},{9,8},{10,9},{11,1... | collective-permute-start | bytes 786440 | tf_op jit(solution)/shard_map/ppermute | solution.py:17
  62.0 4.2 %collective-permute-done.3 = bf16[4,32768]{1,0:T(4,128)(2,1)S(1)} collective-permute-done((bf16[4,32768]{1,0:T(4,128)(2,1)S(1)}, bf16[4,32768]{1,0:T(4,128)(2,1)S(1)}, u32[]{:S(2)}, u32[]{:S(2)}) %collective-permute-start.3) | collective-permute-done | bytes 262176 | tf_op jit(solution)/shard_map/ppermute | solution.py:17
  66.2 0.4 pad_maximum_fusion.1
  66.6 0.2 fusion.20
  66.8 0.2 convolution_convert_fusion.4
  67.0 0.2 convolution_convert_fusion.3
  67.1 0.2 fusion.23
  67.3 0.2 fusion.19
  67.5 0.2 fusion.21
  67.6 0.2 fusion.22
  67.8 0.2 fusion.24
  68.0 0.1 copy.24
  68.1 0.1 reshape.100
  68.2 0.1 reshape.101
  68.3 0.1 copy.29
  68.6 1.0 %maximum_bitcast_fusion.1 = bf16[36,4,36,128]{3,0,2,1:T(8,128)(2,1)S(1)} fusion(bf16[4,2,2,128]{3,1,2,0:T(2,128)(2,1)S(1)} %copy.37, bf16[4,2,32,128]{3,1,2,0:T(2,128)(2,1)S(1)} %copy.29, bf16[4,2,2,128]{3,1,2,0:T(2,128)(2,1)S(1)} %copy.36, bf16[4,32,2,128]{3,1,2,0:T(8,128)(2,1)S(1)} %copy.26, bf16[4,32,32,128]{3,1,2,0:T(8,128)(2,1)S(1)} %slice_bitcast_fusion.1, ...), kind=kLoop, calls=%fused_computation.34 | loop fusion | flops 11943936 | bytes 2654208 | tf_op jit(solution)/shard_map/concatenate | solution.py:87
  69.6 0.7 copy.39
  70.3 0.5 pad.2.clone
  70.8 0.4 slice.176
  71.2 1.1 %fusion.3 = bf16[36,4,8,9,128]{4,1,3,2,0:T(4,128)(2,1)S(1)} fusion(bf16[36,4,7,4,128]{4,1,3,2,0:T(4,128)(2,1)S(1)} %slice.176, bf16[36,4,8,5,128]{4,1,3,2,0:T(4,128)(2,1)S(1)} %bitcast.128), kind=kLoop, calls=%fused_computation.20 | loop fusion | flops 7962624 | bytes 5160960 | tf_op jit(solution)/shard_map/conv_general_dilated | solution.py:91
  72.3 3.3 %fusion.10 = f32[32,32,5,128]{3,1,2,0:T(8,128)S(1)} fusion(bf16[3,3,128,128]{3,2,1,0:T(8,128)(2,1)S(1)} %copy-done, bf16[36,4,8,9,128]{4,1,3,2,0:T(4,128)(2,1)S(1)} %fusion.3, pred[32,5]{0,1:T(8,128)(4,1)S(1)} %copy-done.2), kind=kOutput, calls=%fused_computation.32 | convolution fusion | flops 1510604800 | bytes 5570720 | tf_op jit(solution)/shard_map/conv_general_dilated | solution.py:91
  75.6 1.5 %copy.32 = f32[32,32,5,128]{3,0,2,1:T(8,128)S(1)} copy(f32[32,32,5,128]{3,1,2,0:T(8,128)S(1)} %fusion.10) | data formatting | bytes 5242880 | tf_op jit(solution)/shard_map/conv_general_dilated | solution.py:91
  77.1 0.2 slice_bitcast_fusion
  77.3 2.5 %copy.33 = f32[4,32,32,128]{3,2,1,0:T(8,128)} copy(f32[4,32,32,128]{3,1,2,0:T(8,128)S(1)} %slice_bitcast_fusion) | data formatting | bytes 4194304 | tf_op jit(solution)/shard_map/conv_general_dilated | solution.py:91
  (53 shorter events, 0.7 us)
Async XLA Ops:
  0.0 20.5 %copy-start = (bf16[3,3,128,128]{3,2,1,0:T(8,128)(2,1)S(1)}, bf16[3,3,128,128]{3,2,1,0:T(8,128)(2,1)}, u32[]{:S(2)}) copy-start(bf16[3,3,128,128]{3,2,1,0:T(8,128)(2,1)} %param.8) | copy-start | bytes 884740
  2.3 8.7 %collective-permute-start = (bf16[4,32768]{1,0:T(4,128)(2,1)S(1)}, bf16[4,32768]{1,0:T(4,128)(2,1)S(1)}, u32[]{:S(2)}, u32[]{:S(2)}) collective-permute-start(bf16[4,32768]{1,0:T(4,128)(2,1)S(1)} %constant_dynamic-update-slice_fusion), channel_id=1, source_target_pairs={{0,1},{1,2},{2,3},{3,4},{4,5},{5,6},{6,7},{7,8},{8,9},{9,10},{10,1... | collective-permute-start | bytes 786440 | tf_op jit(solution)/shard_map/ppermute | solution.py:16
  6.8 7.7 %collective-permute-start.1 = (bf16[4,32768]{1,0:T(4,128)(2,1)S(1)}, bf16[4,32768]{1,0:T(4,128)(2,1)S(1)}, u32[]{:S(2)}, u32[]{:S(2)}) collective-permute-start(bf16[4,32768]{1,0:T(4,128)(2,1)S(1)} %constant_dynamic-update-slice_fusion), channel_id=1, source_target_pairs={{1,0},{2,1},{3,2},{4,3},{5,4},{6,5},{7,6},{8,7},{9,8},{10,9},{11,1... | collective-permute-start | bytes 786440 | tf_op jit(solution)/shard_map/ppermute | solution.py:17
  11.1 5.6 %copy-start.1 = (bf16[4,32,32,128]{3,2,1,0:T(8,128)(2,1)S(1)}, bf16[4,32,32,128]{3,2,1,0:T(8,128)(2,1)}, u32[]{:S(2)}) copy-start(bf16[4,32,32,128]{3,2,1,0:T(8,128)(2,1)} %param.6) | copy-start | bytes 3145732
  19.3 1.2 %copy-start.2 = (pred[32,5]{0,1:T(8,128)(4,1)S(1)}, pred[32,5]{0,1:T(8,128)(4,1)}, u32[]{:S(2)}) copy-start(pred[32,5]{0,1:T(8,128)(4,1)} %constant.39) | copy-start | bytes 484
  19.3 1.2 %copy-start.3 = (f32[128]{0:T(128)S(1)}, f32[128]{0:T(128)}, u32[]{:S(2)}) copy-start(f32[128]{0:T(128)} %param.9) | copy-start | bytes 1540
  19.3 1.2 %copy-start.4 = (f32[128]{0:T(128)S(1)}, f32[128]{0:T(128)}, u32[]{:S(2)}) copy-start(f32[128]{0:T(128)} %param.10) | copy-start | bytes 1540
  56.4 5.6 %collective-permute-start.2 = (bf16[4,32768]{1,0:T(4,128)(2,1)S(1)}, bf16[4,32768]{1,0:T(4,128)(2,1)S(1)}, u32[]{:S(2)}, u32[]{:S(2)}) collective-permute-start(bf16[4,32768]{1,0:T(4,128)(2,1)S(1)} %constant_dynamic-update-slice_fusion.2), channel_id=1, source_target_pairs={{0,1},{1,2},{2,3},{3,4},{4,5},{5,6},{6,7},{7,8},{8,9},{9,10},{10,1... | collective-permute-start | bytes 786440 | tf_op jit(solution)/shard_map/ppermute | solution.py:16
  58.5 7.7 %collective-permute-start.3 = (bf16[4,32768]{1,0:T(4,128)(2,1)S(1)}, bf16[4,32768]{1,0:T(4,128)(2,1)S(1)}, u32[]{:S(2)}, u32[]{:S(2)}) collective-permute-start(bf16[4,32768]{1,0:T(4,128)(2,1)S(1)} %constant_dynamic-update-slice_fusion.2), channel_id=1, source_target_pairs={{1,0},{2,1},{3,2},{4,3},{5,4},{6,5},{7,6},{8,7},{9,8},{10,9},{11,1... | collective-permute-start | bytes 786440 | tf_op jit(solution)/shard_map/ppermute | solution.py:17
where the time goes:
time: 80.2 us; the launch traced here: 79.9 us
  blocking collectives  28.4 us (35%)
  starting transfers between devices  12 us (15%)
  local copies, waits for them, and re-layouts  11.7 us (15%)
  matrix products  10.2 us (13%)
  other arithmetic  7.7 us (10%)
  waiting for transfers between devices  7.63 us (10%)
  between operations  2.18 us (3%)
    psum x1, blocking collectives, body(): total_sum = lax.psum(local_sum, ('tile', 'head'))  28.4 us
    ppermute x2, waiting for transfers between devices, with_halo(): after = lax.ppermute(first, axis, down)  7.63 us
    conv_general_dilated x2, matrix products, dilated(): lax.conv_general_dilated(padded_maps, kernel_weight, (1, 1), 'VALID', rhs...  7.61 us
    ppermute x2, starting transfers between devices, with_halo(): before = lax.ppermute(last, axis, up)  6.6 us
    ppermute x2, starting transfers between devices, with_halo(): after = lax.ppermute(first, axis, down)  5.41 us
    conv_general_dilated x5, local copies, waits for them, and re-layouts, dilated(): lax.conv_general_dilated(padded_maps, kernel_weight, (1, 1), 'VALID', rhs...  4.94 us
    dot_general x16, matrix products, choose_band(): jnp.dot(chooser[:, direction, :], strips, preferred_element_type=jnp.floa...  2.58 us
    conv_general_dilated x2, other arithmetic, dilated(): lax.conv_general_dilated(padded_maps, kernel_weight, (1, 1), 'VALID', rhs...  2.27 us
  transfers between devices with their start and end apart: 4, of which 2 were waited for; matrix products, arithmetic and copies ran while one was open for 2% of the time, Pallas kernels for 0%

commit v1 on v0

v1 whole, which is shorter than its diff:
```python
import functools

import jax
import jax.numpy as jnp
from jax import lax
from jax.experimental import pallas as pl
from jax.experimental.pallas import tpu as pltpu
from jax.sharding import PartitionSpec as P

D = 2
GROUP = ("tile", "head")
BF = jnp.bfloat16
F32 = jnp.float32
VMEM = pl.BlockSpec(memory_space=pltpu.VMEM)
SMEM = pl.BlockSpec(memory_space=pltpu.SMEM)


def strips_kernel(top_ref, bottom_ref, left_ref, right_ref, up_ref, down_ref):
    t = top_ref.shape[0]
    s = left_ref.shape[1]
    up_ref[0:t] = top_ref[...]
    down_ref[0:t] = bottom_ref[...]
    per = up_ref.shape[2] // D
    for i in range(s):
        at = pl.ds((i % per) * D, D)
        up_ref[t, i // per, at, :] = left_ref[0, i, 0:D, :]
        down_ref[t, i // per, at, :] = right_ref[0, i, right_ref.shape[2] - D :, :]


def make_strips(maps):
    t, s, _, c = maps.shape
    edge = 16
    out = jax.ShapeDtypeStruct((t + 1, D, s, c), maps.dtype)
    return pl.pallas_call(
        strips_kernel,
        grid=(1,),
        out_shape=(out, out),
        in_specs=[
            pl.BlockSpec((t, D, s, c), lambda i: (0, 0, 0, 0)),
            pl.BlockSpec((t, D, s, c), lambda i: (0, s // D - 1, 0, 0)),
            pl.BlockSpec((1, s, edge, c), lambda i: (0, 0, 0, 0)),
            pl.BlockSpec((1, s, edge, c), lambda i: (t - 1, 0, s // edge - 1, 0)),
        ],
        out_specs=(pl.BlockSpec(out.shape, lambda i: (0, 0, 0, 0)),) * 2,
        name="strips",
    )(maps, maps, maps, maps)


def exchange(up, down):
    size = lax.axis_size(GROUP)
    forward = [(i, i + 1) for i in range(size - 1)]
    return (
        lax.ppermute(down, GROUP, forward),
        lax.ppermute(up, GROUP, [(j, i) for i, j in forward]),
    )


def weights_kernel(w_ref, first_ref, second_ref):
    c = w_ref.shape[2]
    blank = jnp.zeros((c, c), BF)
    for b in range(3):
        for m in range(4):
            rows = pl.ds((m * 3 + b) * c, c)
            for half in range(2):
                a = m - half
                cols = pl.ds(half * c, c)
                if 0 <= a < 3:
                    first_ref[rows, cols] = w_ref[a, b]
                    second_ref[rows, cols] = w_ref[2 - a, 2 - b].T
                else:
                    first_ref[rows, cols] = blank
                    second_ref[rows, cols] = blank


def make_weights(w):
    c = w.shape[2]
    out = jax.ShapeDtypeStruct((12 * c, 2 * c), BF)
    return pl.pallas_call(
        weights_kernel,
        out_shape=(out, out),
        in_specs=[VMEM],
        out_specs=(VMEM, VMEM),
        cost_estimate=pl.CostEstimate(flops=0, bytes_accessed=2 << 20, transcendentals=0),
        name="weights",
    )(w)


def fill_window(near_ref, start_ref, src_ref, prev_ref, next_ref, win_ref, low_ref, high_ref):
    t, s, _, c = src_ref.shape
    start = start_ref[0]
    low_ref[0:t] = prev_ref[0:t]
    low_ref[t : 2 * t] = src_ref[:, s - D :]
    low_ref[2 * t] = jnp.zeros(low_ref.shape[1:], BF)
    high_ref[0:t] = src_ref[:, 0:D]
    high_ref[t : 2 * t] = next_ref[0:t]
    high_ref[2 * t] = jnp.zeros(low_ref.shape[1:], BF)

    def pick(ref, tile, k, base):
        there = near_ref[tile, k]
        local = jnp.where(there < 0, 2 * t, jnp.clip(there - base, 0, 2 * t - 1))
        return ref[local]

    per = s // D
    for i in range(t):
        v = src_ref[i]
        win_ref[0, i, D : D + s, D:] = v[:, : s - D]
        win_ref[1, i, D : D + s] = v
        win_ref[2, i, D : D + s, : s - D] = v[:, D:]
        has_left = (near_ref[i, 3] >= 0).astype(F32).astype(BF)
        has_right = (near_ref[i, 4] >= 0).astype(F32).astype(BF)
        if i > 0:
            win_ref[0, i, D : D + s, :D] = src_ref[i - 1, :, s - D :] * has_left
        else:
            for r in range(s):
                win_ref[0, i, D + r, :D] = (
                    prev_ref[t, r // per, pl.ds((r % per) * D, D), :] * has_left
                )
        if i < t - 1:
            win_ref[2, i, D : D + s, s - D :] = src_ref[i + 1, :, :D] * has_right
        else:
            for r in range(s):
                win_ref[2, i, D + r, s - D :] = (
                    next_ref[t, r // per, pl.ds((r % per) * D, D), :] * has_right
                )
        for ref, k, base, row in ((low_ref, 0, start - t, 0), (high_ref, 5, start, D + s)):
            rows = slice(row, row + D)
            middle = pick(ref, i, k + 1, base)
            win_ref[0, i, rows, D:] = middle[:, : s - D]
            win_ref[0, i, rows, :D] = pick(ref, i, k, base)[:, s - D :]
            win_ref[1, i, rows] = middle
            win_ref[2, i, rows, : s - D] = middle[:, D:]
            win_ref[2, i, rows, s - D :] = pick(ref, i, k + 2, base)[:, :D]


def band(win_ref, tile, group, groups):
    s, c = win_ref.shape[3:]
    pieces = []
    for m in range(4):
        for b in range(3):
            pair = [
                win_ref[b, tile, pl.ds(4 * g + D * m, D)]
                for g in range(group, group + groups)
            ]
            pieces.append(jnp.concatenate(pair, 0).reshape(groups * D * s, c))
    return jnp.concatenate(pieces, 1)


def first_kernel(
    groups, near_ref, start_ref, x_ref, prev_ref, next_ref, w_ref, bias_ref, head_ref,
    u_ref, up_ref, down_ref, sum_ref, win_ref, low_ref, high_ref,
):
    fill_window(near_ref, start_ref, x_ref, prev_ref, next_ref, win_ref, low_ref, high_ref)
    t, s, _, c = x_ref.shape
    bias = bias_ref[...]
    head = head_ref[...]
    total = jnp.zeros((8, c), F32)
    for tile in range(t):
        for group in range(0, s // 4, groups):
            both = jnp.dot(
                band(win_ref, tile, group, groups), w_ref[...], preferred_element_type=F32
            )
            for half in range(2):
                pre = both[:, half * c : (half + 1) * c] + bias
                sig = 0.5 + 0.5 * jnp.tanh(0.5 * pre)
                silu = pre * sig
                total = total + jnp.sum(silu.reshape(-1, 8, c), 0)
                grad = (head * (sig + silu * (1.0 - sig))).astype(BF)
                grad = grad.reshape(groups, D, s, c)
                for g in range(groups):
                    u_ref[tile, pl.ds(4 * (group + g) + D * half, D)] = grad[g]
    sum_ref[...] = total * head
    per = s // D
    up_ref[0:t] = u_ref[:, 0:D]
    down_ref[0:t] = u_ref[:, s - D :]
    for i in range(s):
        at = pl.ds((i % per) * D, D)
        up_ref[t, i // per, at, :] = u_ref[0, i, 0:D, :]
        down_ref[t, i // per, at, :] = u_ref[t - 1, i, s - D :, :]


def window_scratch(t, s, c):
    return [
        pltpu.VMEM((3, t, s + 2 * D, s, c), BF),
        pltpu.VMEM((2 * t + 1, D, s, c), BF),
        pltpu.VMEM((2 * t + 1, D, s, c), BF),
    ]


def first_stage(near, start, x, before, after, w, bias, head, groups=8):
    t, s, _, c = x.shape
    strip = jax.ShapeDtypeStruct((t + 1, D, s, c), BF)
    return pl.pallas_call(
        functools.partial(first_kernel, groups),
        out_shape=(
            jax.ShapeDtypeStruct(x.shape, BF),
            strip,
            strip,
            jax.ShapeDtypeStruct((8, c), F32),
        ),
        in_specs=[SMEM, SMEM] + [VMEM] * 6,
        out_specs=(VMEM,) * 4,
        scratch_shapes=window_scratch(t, s, c),
        cost_estimate=pl.CostEstimate(
            flops=2 * 9 * t * s * s * c * c, bytes_accessed=4 << 20, transcendentals=t * s * s * c
        ),
        name="first",
    )(near, start, x, before, after, w, bias, head)


def second_kernel(
    groups, near_ref, start_ref, u_ref, prev_ref, next_ref, w_ref, o_ref, win_ref, low_ref, high_ref
):
    fill_window(near_ref, start_ref, u_ref, prev_ref, next_ref, win_ref, low_ref, high_ref)
    t, s, _, c = u_ref.shape
    for tile in range(t):
        for group in range(0, s // 4, groups):
            both = jnp.dot(
                band(win_ref, tile, group, groups), w_ref[...], preferred_element_type=F32
            )
            for half in range(2):
                part = both[:, half * c : (half + 1) * c].reshape(groups, D, s, c)
                for g in range(groups):
                    o_ref[tile, pl.ds(4 * (group + g) + D * half, D)] = part[g]


def second_stage(near, start, u, before, after, w, groups=8):
    t, s, _, c = u.shape
    return pl.pallas_call(
        functools.partial(second_kernel, groups),
        out_shape=jax.ShapeDtypeStruct(u.shape, F32),
        in_specs=[SMEM, SMEM] + [VMEM] * 4,
        out_specs=VMEM,
        scratch_shapes=window_scratch(t, s, c),
        cost_estimate=pl.CostEstimate(
            flops=2 * 9 * t * s * s * c * c, bytes_accessed=4 << 20, transcendentals=0
        ),
        name="second",
    )(near, start, u, before, after, w)


def scale_kernel(count, label_ref, sum_ref, v_ref, o_ref):
    score = jnp.sum(sum_ref[...], axis=(0, 1), keepdims=True) / count
    label = label_ref[0].astype(F32) / 100.0
    slope = jax.nn.sigmoid(score) - label
    o_ref[...] = v_ref[...] * slope.reshape(1, 1, 1, 1)


def scale(label, total, v, count):
    t, s, _, c = v.shape
    rows = 8
    block = pl.BlockSpec((1, rows, s, c), lambda i, j: (i, j, 0, 0))
    return pl.pallas_call(
        functools.partial(scale_kernel, count),
        grid=(t, s // rows),
        out_shape=jax.ShapeDtypeStruct(v.shape, F32),
        in_specs=[SMEM, pl.BlockSpec(total.shape, lambda i, j: (0, 0)), block],
        out_specs=block,
        name="scale",
    )(label, total, v)


def group_sum(part):
    size = lax.axis_size(GROUP)
    if size & (size - 1):
        return lax.psum(part, GROUP)
    step = 1
    while step < size:
        part = part + lax.ppermute(part, GROUP, [(i, i ^ step) for i in range(size)])
        step *= 2
    return part


def body(tissue_tiles, neighbours, conv_weight, conv_bias, head_weight, slide_label):
    t, s, _, c = tissue_tiles.shape
    start = (lax.axis_index(GROUP) * t).astype(jnp.int32).reshape(1)
    before, after = exchange(*make_strips(tissue_tiles))
    w_first, w_second = make_weights(conv_weight)
    u, up, down, part = first_stage(
        neighbours, start, tissue_tiles, before, after, w_first,
        conv_bias.reshape(1, c), head_weight.reshape(1, c),
    )
    total = group_sum(part)
    before, after = exchange(up, down)
    v = second_stage(neighbours, start, u, before, after, w_second)
    return scale(slide_label, total, v, float(t * lax.axis_size(GROUP) * s * s * c))


def solution(mesh):
    return jax.shard_map(
        body,
        mesh=mesh,
        in_specs=(
            P(("groups", "tile", "head"), None, None, None),
            P(("groups", "tile", "head"), None),
            P(),
            P(),
            P(),
            P("groups"),
        ),
        out_specs=P(("groups", "tile", "head"), None, None, None),
        check_vma=False,
    )
```

time: 80.2 us -> 54.8 us (0.68)
  the two profiles are of different devices: /device:TPU:1 before, /device:TPU:0 now
where the time goes in v1:
time: 54.8 us; the launch traced here: 54.2 us
  Pallas kernels  24.3 us (44%)
  starting transfers between devices  19.7 us (36%)
  waiting for transfers between devices  6.92 us (13%)
  local copies, waits for them, and re-layouts  1.28 us (2%)
  other arithmetic  1.27 us (2%)
  between operations  0.71 us (1%)
    pallas_call x1, Pallas kernels, scale(): pl.pallas_call(functools.partial(scale_kernel, count), grid=(t, s // rows...  10.2 us
    ppermute x4, starting transfers between devices, group_sum(): lax.ppermute(part, GROUP, [(i, i ^ step) for i in range(size)])  9.72 us
    ppermute x2, starting transfers between devices, exchange(): lax.ppermute(down, GROUP, forward)  7.37 us
    pallas_call x1, Pallas kernels, first_stage(): pl.pallas_call(functools.partial(first_kernel, groups), out_shape=(jax.Sh...  5.19 us
    ppermute x4, waiting for transfers between devices, group_sum(): lax.ppermute(part, GROUP, [(i, i ^ step) for i in range(size)])  5.13 us
    pallas_call x1, Pallas kernels, second_stage(): pl.pallas_call(functools.partial(second_kernel, groups), out_shape=jax.Sh...  4.81 us
    ppermute x2, starting transfers between devices, exchange(): lax.ppermute(up, GROUP, [(j, i) for i, j in forward])  2.58 us
    pallas_call x1, Pallas kernels, make_weights(): pl.pallas_call(weights_kernel, out_shape=(out, out), in_specs=[VMEM], out...  2.38 us
  transfers between devices with their start and end apart: 8, of which 5 were waited for; matrix products, arithmetic and copies ran while one was open for 2% of the time, Pallas kernels for 4%

profile of v1, /device:TPU:0, one launch (start us, length us, event | category | flops | bytes accessed | tf_op | source)
XLA Modules:
  0.0 54.2 jit_solution(7728444972844496804)
XLA Ops:
  0.0 1.7 %strips.1 = (bf16[5,2,32,128]{3,2,1,0:T(8,128)(2,1)}, bf16[5,2,32,128]{3,2,1,0:T(8,128)(2,1)}) custom-call(bf16[4,32,32,128]{3,2,1,0:T(8,128)(2,1)} %x_ref.1, bf16[4,32,32,128]{3,2,1,0:T(8,128)(2,1)} %x_ref.1, bf16[4,32,32,128]{3,2,1,0:T(8,128)(2,1)} %x_ref.1, bf16[4,32,32,128]{3,2,1,0:T(8,128)(2,1)} %x_ref.1), custom_call_target="tpu_custom_call" | custom-call | tf_op jit(solution)/shard_map/strips/pallas_call | solution.py:34
  1.7 2.4 %collective-permute-start = (bf16[5,2,32,128]{3,2,1,0:T(8,128)(2,1)}, bf16[5,2,32,128]{3,2,1,0:T(8,128)(2,1)S(1)}, u32[]{:S(2)}, u32[]{:S(2)}) collective-permute-start(bf16[5,2,32,128]{3,2,1,0:T(8,128)(2,1)} %get-tuple-element.13), channel_id=1, source_target_pairs={{0,1},{1,2},{2,3},{3,4},{4,5},{5,6},{6,7},{7,8},{8,9},{9,10},{10,1... | collective-permute-start | bytes 245768 | tf_op jit(solution)/shard_map/ppermute | solution.py:53
  4.1 1.3 %collective-permute-start.1 = (bf16[5,2,32,128]{3,2,1,0:T(8,128)(2,1)}, bf16[5,2,32,128]{3,2,1,0:T(8,128)(2,1)S(1)}, u32[]{:S(2)}, u32[]{:S(2)}) collective-permute-start(bf16[5,2,32,128]{3,2,1,0:T(8,128)(2,1)} %get-tuple-element.14), channel_id=1, source_target_pairs={{1,0},{2,1},{3,2},{4,3},{5,4},{6,5},{7,6},{8,7},{9,8},{10,9},{11,1... | collective-permute-start | bytes 245768 | tf_op jit(solution)/shard_map/ppermute | solution.py:54
  5.4 2.4 %weights.1 = (bf16[1536,256]{1,0:T(8,128)(2,1)}, bf16[1536,256]{1,0:T(8,128)(2,1)}) custom-call(bf16[3,3,128,128]{3,2,1,0:T(8,128)(2,1)} %w_ref.1), custom_call_target="tpu_custom_call" | custom-call | bytes 2097152 | tf_op jit(solution)/shard_map/weights/pallas_call | solution.py:78
  7.8 0.0 collective-permute-done.prev_ref
  7.8 0.0 copy-start.2
  7.8 1.8 %collective-permute-done.1.next_ref = bf16[5,2,32,128]{3,2,1,0:T(8,128)(2,1)S(1)} collective-permute-done((bf16[5,2,32,128]{3,2,1,0:T(8,128)(2,1)}, bf16[5,2,32,128]{3,2,1,0:T(8,128)(2,1)S(1)}, u32[]{:S(2)}, u32[]{:S(2)}) %collective-permute-start.1) | collective-permute-done | bytes 81952 | tf_op jit(solution)/shard_map/ppermute | solution.py:54
  9.6 0.0 copy-start.3
  9.6 0.0 copy-done.2
  9.6 0.6 %copy-done.3 = bf16[5,2,32,128]{3,2,1,0:T(8,128)(2,1)} copy-done((bf16[5,2,32,128]{3,2,1,0:T(8,128)(2,1)}, bf16[5,2,32,128]{3,2,1,0:T(8,128)(2,1)S(1)}, u32[]{:S(2)}) %copy-start.3) | copy-done | bytes 81944
  10.2 5.2 %first.1 = (bf16[4,32,32,128]{3,2,1,0:T(8,128)(2,1)}, bf16[5,2,32,128]{3,2,1,0:T(8,128)(2,1)}, bf16[5,2,32,128]{3,2,1,0:T(8,128)(2,1)}, f32[8,128]{1,0:T(8,128)}) custom-call(s32[4,8]{1,0:T(4,128)} %near_ref.3, s32[1]{0:T(128)} %bitcast.start_ref, bf16[4,32,32,128]{3,2,1,0:T(8,128)(2,1)} %x_ref.1, bf16[5,2,32,128]{3,2,1,0:T(8,128)(2,1)} %copy-done.2, ...), custom_call_target="tpu_custom_call" | custom-call | flops 1207959552 | bytes 4194304 | tf_op jit(solution)/shard_map/first/pallas_call | solution.py:192
  15.4 5.0 %collective-permute-start.6 = (bf16[5,2,32,128]{3,2,1,0:T(8,128)(2,1)}, bf16[5,2,32,128]{3,2,1,0:T(8,128)(2,1)S(1)}, u32[]{:S(2)}, u32[]{:S(2)}) collective-permute-start(bf16[5,2,32,128]{3,2,1,0:T(8,128)(2,1)} %get-tuple-element.18), channel_id=1, source_target_pairs={{0,1},{1,2},{2,3},{3,4},{4,5},{5,6},{6,7},{7,8},{8,9},{9,10},{10,1... | collective-permute-start | bytes 245768 | tf_op jit(solution)/shard_map/ppermute | solution.py:53
  20.4 1.3 %collective-permute-start.7 = (bf16[5,2,32,128]{3,2,1,0:T(8,128)(2,1)}, bf16[5,2,32,128]{3,2,1,0:T(8,128)(2,1)S(1)}, u32[]{:S(2)}, u32[]{:S(2)}) collective-permute-start(bf16[5,2,32,128]{3,2,1,0:T(8,128)(2,1)} %get-tuple-element.19), channel_id=1, source_target_pairs={{1,0},{2,1},{3,2},{4,3},{5,4},{6,5},{7,6},{8,7},{9,8},{10,9},{11,1... | collective-permute-start | bytes 245768 | tf_op jit(solution)/shard_map/ppermute | solution.py:54
  21.7 1.2 %collective-permute-start.2 = (f32[8,128]{1,0:T(8,128)}, f32[8,128]{1,0:T(8,128)S(1)}, u32[]{:S(2)}, u32[]{:S(2)}) collective-permute-start(f32[8,128]{1,0:T(8,128)} %get-tuple-element.16), channel_id=1, source_target_pairs={{0,1},{1,0},{2,3},{3,2},{4,5},{5,4},{6,7},{7,6},{8,9},{9,8},{10,11... | collective-permute-start | bytes 12296 | tf_op jit(solution)/shard_map/ppermute | solution.py:268
  22.9 1.0 %collective-permute-done.2 = f32[8,128]{1,0:T(8,128)S(1)} collective-permute-done((f32[8,128]{1,0:T(8,128)}, f32[8,128]{1,0:T(8,128)S(1)}, u32[]{:S(2)}, u32[]{:S(2)}) %collective-permute-start.2) | collective-permute-done | bytes 4128 | tf_op jit(solution)/shard_map/ppermute | solution.py:268
  23.9 0.7 %add.16 = f32[8,128]{1,0:T(8,128)S(1)} add(f32[8,128]{1,0:T(8,128)} %get-tuple-element.16, f32[8,128]{1,0:T(8,128)S(1)} %collective-permute-done.2) | non-fusion elementwise | flops 1024 | bytes 12288 | tf_op jit(solution)/shard_map/add | solution.py:268
  24.6 2.4 %collective-permute-start.3 = (f32[8,128]{1,0:T(8,128)S(1)}, f32[8,128]{1,0:T(8,128)S(1)}, u32[]{:S(2)}, u32[]{:S(2)}) collective-permute-start(f32[8,128]{1,0:T(8,128)S(1)} %add.16), channel_id=1, source_target_pairs={{0,2},{1,3},{2,0},{3,1},{4,6},{5,7},{6,4},{7,5},{8,10},{9,11},{10,... | collective-permute-start | bytes 12296 | tf_op jit(solution)/shard_map/ppermute | solution.py:268
  27.1 1.6 %collective-permute-done.3 = f32[8,128]{1,0:T(8,128)S(1)} collective-permute-done((f32[8,128]{1,0:T(8,128)S(1)}, f32[8,128]{1,0:T(8,128)S(1)}, u32[]{:S(2)}, u32[]{:S(2)}) %collective-permute-start.3) | collective-permute-done | bytes 4128 | tf_op jit(solution)/shard_map/ppermute | solution.py:268
  28.6 3.0 %collective-permute-start.4 = (f32[8,128]{1,0:T(8,128)S(1)}, f32[8,128]{1,0:T(8,128)S(1)}, u32[]{:S(2)}, u32[]{:S(2)}) collective-permute-start(f32[8,128]{1,0:T(8,128)S(1)} %add.17), channel_id=1, source_target_pairs={{0,4},{1,5},{2,6},{3,7},{4,0},{5,1},{6,2},{7,3},{8,12},{9,13},{10,... | collective-permute-start | bytes 12296 | tf_op jit(solution)/shard_map/ppermute | solution.py:268
  31.7 1.6 %collective-permute-done.4 = f32[8,128]{1,0:T(8,128)S(1)} collective-permute-done((f32[8,128]{1,0:T(8,128)S(1)}, f32[8,128]{1,0:T(8,128)S(1)}, u32[]{:S(2)}, u32[]{:S(2)}) %collective-permute-start.4) | collective-permute-done | bytes 4128 | tf_op jit(solution)/shard_map/ppermute | solution.py:268
  33.3 3.0 %collective-permute-start.5 = (f32[8,128]{1,0:T(8,128)S(1)}, f32[8,128]{1,0:T(8,128)S(1)}, u32[]{:S(2)}, u32[]{:S(2)}) collective-permute-start(f32[8,128]{1,0:T(8,128)S(1)} %add.18), channel_id=1, source_target_pairs={{0,8},{1,9},{2,10},{3,11},{4,12},{5,13},{6,14},{7,15},{8,0},{9,1},... | collective-permute-start | bytes 12296 | tf_op jit(solution)/shard_map/ppermute | solution.py:268
  37.0 0.9 %collective-permute-done.5 = f32[8,128]{1,0:T(8,128)S(1)} collective-permute-done((f32[8,128]{1,0:T(8,128)S(1)}, f32[8,128]{1,0:T(8,128)S(1)}, u32[]{:S(2)}, u32[]{:S(2)}) %collective-permute-start.5) | collective-permute-done | bytes 4128 | tf_op jit(solution)/shard_map/ppermute | solution.py:268
  37.9 0.6 %add.19.sum_ref = f32[8,128]{1,0:T(8,128)} add(f32[8,128]{1,0:T(8,128)S(1)} %add.18, f32[8,128]{1,0:T(8,128)S(1)} %collective-permute-done.5) | non-fusion elementwise | flops 1024 | bytes 12288 | tf_op jit(solution)/shard_map/add | solution.py:268
  38.5 0.0 collective-permute-done.6.prev_ref
  38.5 0.0 copy-start
  38.5 0.0 collective-permute-done.7.next_ref
  38.5 0.0 copy-start.1
  38.5 0.6 %copy-done = bf16[5,2,32,128]{3,2,1,0:T(8,128)(2,1)} copy-done((bf16[5,2,32,128]{3,2,1,0:T(8,128)(2,1)}, bf16[5,2,32,128]{3,2,1,0:T(8,128)(2,1)S(1)}, u32[]{:S(2)}) %copy-start) | copy-done | bytes 81944
  39.1 0.0 copy-done.1
  39.2 4.8 %second.1.v_ref = f32[4,32,32,128]{3,2,1,0:T(8,128)} custom-call(s32[4,8]{1,0:T(4,128)} %near_ref.3, s32[1]{0:T(128)} %bitcast.start_ref, bf16[4,32,32,128]{3,2,1,0:T(8,128)(2,1)} %get-tuple-element.17.u_ref, bf16[5,2,32,128]{3,2,1,0:T(8,128)(2,1)} %copy-done, bf16[5,2,32,128]{3,2,1,0:T(8,128)(2,1)} %copy-done.1, bf16[1536,256]{1,0:T(8,128)(2,1)} %get-tuple-element.20.w_ref), custom_call_target="tpu_custom_call" | custom-call | flops 1207959552 | bytes 4194304 | tf_op jit(solution)/shard_map/second/pallas_call | solution.py:228
  44.0 10.2 %scale.1 = f32[4,32,32,128]{3,2,1,0:T(8,128)} custom-call(s32[1]{0:T(128)S(6)} %copy.7.label_ref, f32[8,128]{1,0:T(8,128)} %add.19.sum_ref, f32[4,32,32,128]{3,2,1,0:T(8,128)} %second.1.v_ref), custom_call_target="tpu_custom_call" | custom-call | tf_op jit(solution)/shard_map/scale/pallas_call | solution.py:252
  (2 shorter events, 0.0 us)
Async XLA Ops:
  1.7 6.1 %collective-permute-start = (bf16[5,2,32,128]{3,2,1,0:T(8,128)(2,1)}, bf16[5,2,32,128]{3,2,1,0:T(8,128)(2,1)S(1)}, u32[]{:S(2)}, u32[]{:S(2)}) collective-permute-start(bf16[5,2,32,128]{3,2,1,0:T(8,128)(2,1)} %get-tuple-element.13), channel_id=1, source_target_pairs={{0,1},{1,2},{2,3},{3,4},{4,5},{5,6},{6,7},{7,8},{8,9},{9,10},{10,1... | collective-permute-start | bytes 245768 | tf_op jit(solution)/shard_map/ppermute | solution.py:53
  4.1 5.5 %collective-permute-start.1 = (bf16[5,2,32,128]{3,2,1,0:T(8,128)(2,1)}, bf16[5,2,32,128]{3,2,1,0:T(8,128)(2,1)S(1)}, u32[]{:S(2)}, u32[]{:S(2)}) collective-permute-start(bf16[5,2,32,128]{3,2,1,0:T(8,128)(2,1)} %get-tuple-element.14), channel_id=1, source_target_pairs={{1,0},{2,1},{3,2},{4,3},{5,4},{6,5},{7,6},{8,7},{9,8},{10,9},{11,1... | collective-permute-start | bytes 245768 | tf_op jit(solution)/shard_map/ppermute | solution.py:54
  7.8 1.8 %copy-start.2 = (bf16[5,2,32,128]{3,2,1,0:T(8,128)(2,1)}, bf16[5,2,32,128]{3,2,1,0:T(8,128)(2,1)S(1)}, u32[]{:S(2)}) copy-start(bf16[5,2,32,128]{3,2,1,0:T(8,128)(2,1)S(1)} %collective-permute-done.prev_ref) | copy-start | bytes 245764
  9.6 0.6 %copy-start.3 = (bf16[5,2,32,128]{3,2,1,0:T(8,128)(2,1)}, bf16[5,2,32,128]{3,2,1,0:T(8,128)(2,1)S(1)}, u32[]{:S(2)}) copy-start(bf16[5,2,32,128]{3,2,1,0:T(8,128)(2,1)S(1)} %collective-permute-done.1.next_ref) | copy-start | bytes 245764
  15.4 23.1 %collective-permute-start.6 = (bf16[5,2,32,128]{3,2,1,0:T(8,128)(2,1)}, bf16[5,2,32,128]{3,2,1,0:T(8,128)(2,1)S(1)}, u32[]{:S(2)}, u32[]{:S(2)}) collective-permute-start(bf16[5,2,32,128]{3,2,1,0:T(8,128)(2,1)} %get-tuple-element.18), channel_id=1, source_target_pairs={{0,1},{1,2},{2,3},{3,4},{4,5},{5,6},{6,7},{7,8},{8,9},{9,10},{10,1... | collective-permute-start | bytes 245768 | tf_op jit(solution)/shard_map/ppermute | solution.py:53
  20.4 18.1 %collective-permute-start.7 = (bf16[5,2,32,128]{3,2,1,0:T(8,128)(2,1)}, bf16[5,2,32,128]{3,2,1,0:T(8,128)(2,1)S(1)}, u32[]{:S(2)}, u32[]{:S(2)}) collective-permute-start(bf16[5,2,32,128]{3,2,1,0:T(8,128)(2,1)} %get-tuple-element.19), channel_id=1, source_target_pairs={{1,0},{2,1},{3,2},{4,3},{5,4},{6,5},{7,6},{8,7},{9,8},{10,9},{11,1... | collective-permute-start | bytes 245768 | tf_op jit(solution)/shard_map/ppermute | solution.py:54
  21.7 2.2 %collective-permute-start.2 = (f32[8,128]{1,0:T(8,128)}, f32[8,128]{1,0:T(8,128)S(1)}, u32[]{:S(2)}, u32[]{:S(2)}) collective-permute-start(f32[8,128]{1,0:T(8,128)} %get-tuple-element.16), channel_id=1, source_target_pairs={{0,1},{1,0},{2,3},{3,2},{4,5},{5,4},{6,7},{7,6},{8,9},{9,8},{10,11... | collective-permute-start | bytes 12296 | tf_op jit(solution)/shard_map/ppermute | solution.py:268
  24.6 4.0 %collective-permute-start.3 = (f32[8,128]{1,0:T(8,128)S(1)}, f32[8,128]{1,0:T(8,128)S(1)}, u32[]{:S(2)}, u32[]{:S(2)}) collective-permute-start(f32[8,128]{1,0:T(8,128)S(1)} %add.16), channel_id=1, source_target_pairs={{0,2},{1,3},{2,0},{3,1},{4,6},{5,7},{6,4},{7,5},{8,10},{9,11},{10,... | collective-permute-start | bytes 12296 | tf_op jit(solution)/shard_map/ppermute | solution.py:268
  28.6 4.6 %collective-permute-start.4 = (f32[8,128]{1,0:T(8,128)S(1)}, f32[8,128]{1,0:T(8,128)S(1)}, u32[]{:S(2)}, u32[]{:S(2)}) collective-permute-start(f32[8,128]{1,0:T(8,128)S(1)} %add.17), channel_id=1, source_target_pairs={{0,4},{1,5},{2,6},{3,7},{4,0},{5,1},{6,2},{7,3},{8,12},{9,13},{10,... | collective-permute-start | bytes 12296 | tf_op jit(solution)/shard_map/ppermute | solution.py:268
  33.3 4.6 %collective-permute-start.5 = (f32[8,128]{1,0:T(8,128)S(1)}, f32[8,128]{1,0:T(8,128)S(1)}, u32[]{:S(2)}, u32[]{:S(2)}) collective-permute-start(f32[8,128]{1,0:T(8,128)S(1)} %add.18), channel_id=1, source_target_pairs={{0,8},{1,9},{2,10},{3,11},{4,12},{5,13},{6,14},{7,15},{8,0},{9,1},... | collective-permute-start | bytes 12296 | tf_op jit(solution)/shard_map/ppermute | solution.py:268
  38.5 0.6 %copy-start = (bf16[5,2,32,128]{3,2,1,0:T(8,128)(2,1)}, bf16[5,2,32,128]{3,2,1,0:T(8,128)(2,1)S(1)}, u32[]{:S(2)}) copy-start(bf16[5,2,32,128]{3,2,1,0:T(8,128)(2,1)S(1)} %collective-permute-done.6.prev_ref) | copy-start | bytes 245764
  38.5 0.7 %copy-start.1 = (bf16[5,2,32,128]{3,2,1,0:T(8,128)(2,1)}, bf16[5,2,32,128]{3,2,1,0:T(8,128)(2,1)S(1)}, u32[]{:S(2)}) copy-start(bf16[5,2,32,128]{3,2,1,0:T(8,128)(2,1)S(1)} %collective-permute-done.7.next_ref) | copy-start | bytes 245764

commit v2 on v1

v2 whole, which is shorter than its diff:
```python
import functools

import jax
import jax.numpy as jnp
from jax import lax
from jax.experimental import pallas as pl
from jax.experimental.pallas import tpu as pltpu
from jax.sharding import PartitionSpec as P

D = 2
GROUP = ("tile", "head")
BF = jnp.bfloat16
F32 = jnp.float32
VMEM = pl.BlockSpec(memory_space=pltpu.VMEM)
SMEM = pl.BlockSpec(memory_space=pltpu.SMEM)


LIMIT = 24 << 20


def params(limit=LIMIT):
    return pltpu.CompilerParams(vmem_limit_bytes=limit)


def put_strips(parity, src_ref, mate_ref, other_ref):
    t, s, _, c = src_ref.shape
    per = s // D

    def put(ref, last):
        ref[0:t] = src_ref[:, s - D :] if last else src_ref[:, 0:D]
        for i in range(s):
            at = pl.ds((i % per) * D, D)
            ref[t, i // per, at, :] = (
                src_ref[t - 1, i, s - D :, :] if last else src_ref[0, i, 0:D, :]
            )

    @pl.when(parity == 0)
    def _():
        put(mate_ref, True)
        put(other_ref, False)

    @pl.when(parity == 1)
    def _():
        put(mate_ref, False)
        put(other_ref, True)


def strips_kernel(place_ref, x_ref, mate_ref, other_ref, keep_ref):
    keep_ref[...] = x_ref[...]
    put_strips(place_ref[1], x_ref, mate_ref, other_ref)


def make_strips(place, x):
    t, s, _, c = x.shape
    out = jax.ShapeDtypeStruct((t + 1, D, s, c), BF)
    return pl.pallas_call(
        strips_kernel,
        out_shape=(out, out, jax.ShapeDtypeStruct(x.shape, BF)),
        in_specs=[SMEM, VMEM],
        out_specs=(VMEM,) * 3,
        compiler_params=params(),
        name="strips",
    )(place, x)


def swap(mate, other):
    size = lax.axis_size(GROUP)
    mates = [(i, i ^ 1) for i in range(size) if i ^ 1 < size]
    others = [(i, j) for i in range(size) for j in [(i + 1 ^ 1) - 1] if 0 <= j < size]
    return lax.ppermute(mate, GROUP, mates), lax.ppermute(other, GROUP, others)


def weights_kernel(w_ref, head_ref, first_ref, second_ref):
    c = w_ref.shape[2]
    blank = jnp.zeros((c, c), BF)
    head = head_ref[...]
    for b in range(3):
        for m in range(4):
            rows = pl.ds((m * 3 + b) * c, c)
            for half in range(2):
                a = m - half
                first_ref[rows, pl.ds(half * c, c)] = w_ref[a, b] if 0 <= a < 3 else blank
        for a in range(3):
            rows = pl.ds((a * 3 + b) * c, c)
            turned = (w_ref[2 - a, 2 - b].astype(F32) * head).T
            high = turned.astype(BF)
            second_ref[rows, 0:c] = high
            second_ref[rows, c : 2 * c] = (turned - high.astype(F32)).astype(BF)


def make_weights(w, head):
    c = w.shape[2]
    return pl.pallas_call(
        weights_kernel,
        out_shape=(
            jax.ShapeDtypeStruct((12 * c, 2 * c), BF),
            jax.ShapeDtypeStruct((9 * c, 2 * c), BF),
        ),
        in_specs=[VMEM, VMEM],
        out_specs=(VMEM, VMEM),
        compiler_params=params(),
        cost_estimate=pl.CostEstimate(flops=0, bytes_accessed=4 << 20, transcendentals=0),
        name="weights",
    )(w, head)


def fill_window(tiles, near_ref, place_ref, src_ref, mate_ref, other_ref, win_ref, strip_ref):
    t, s, _, c = src_ref.shape
    start, parity = place_ref[0], place_ref[1]
    strip_ref[0 : t + 1] = mate_ref[0 : t + 1]
    strip_ref[t + 1 : 2 * t + 2] = other_ref[0 : t + 1]
    strip_ref[2 * t + 2 : 3 * t + 2] = src_ref[:, s - D :]
    strip_ref[3 * t + 2 : 4 * t + 2] = src_ref[:, 0:D]
    strip_ref[4 * t + 2] = jnp.zeros((D, s, c), BF)
    before = (1 - parity) * (t + 1)
    after = parity * (t + 1)

    def pick(tile, k):
        there = near_ref[tile, k]
        local = there - start
        if k < 3:
            local = jnp.clip(local, -t, t - 1)
            slot = jnp.where(local < 0, before + t + local, 2 * t + 2 + local)
        else:
            local = jnp.clip(local, 0, 2 * t - 1)
            slot = jnp.where(local >= t, after - t + local, 3 * t + 2 + local)
        return strip_ref[jnp.where(there < 0, 4 * t + 2, slot)]

    per = s // D
    for j, i in enumerate(tiles):
        v = src_ref[i]
        win_ref[0, j, D : D + s, D:] = v[:, : s - D]
        win_ref[1, j, D : D + s] = v
        win_ref[2, j, D : D + s, : s - D] = v[:, D:]
        has_left = (near_ref[i, 3] >= 0).astype(F32).astype(BF)
        has_right = (near_ref[i, 4] >= 0).astype(F32).astype(BF)
        if i > 0:
            win_ref[0, j, D : D + s, :D] = src_ref[i - 1, :, s - D :] * has_left
        else:
            for r in range(s):
                at = pl.ds((r % per) * D, D)
                win_ref[0, j, D + r, :D] = strip_ref[before + t, r // per, at, :] * has_left
        if i < t - 1:
            win_ref[2, j, D : D + s, s - D :] = src_ref[i + 1, :, :D] * has_right
        else:
            for r in range(s):
                at = pl.ds((r % per) * D, D)
                win_ref[2, j, D + r, s - D :] = strip_ref[after + t, r // per, at, :] * has_right
        for k, row in ((0, 0), (5, D + s)):
            rows = slice(row, row + D)
            middle = pick(i, k + 1)
            win_ref[0, j, rows, D:] = middle[:, : s - D]
            win_ref[0, j, rows, :D] = pick(i, k)[:, s - D :]
            win_ref[1, j, rows] = middle
            win_ref[2, j, rows, : s - D] = middle[:, D:]
            win_ref[2, j, rows, s - D :] = pick(i, k + 2)[:, :D]


def window_scratch(n, t, s, c):
    return [
        pltpu.VMEM((3, n, s + 2 * D, s, c), BF),
        pltpu.VMEM((4 * t + 3, D, s, c), BF),
    ]


def band(win_ref, tile, group, groups):
    s, c = win_ref.shape[3:]
    pieces = []
    for m in range(4):
        for b in range(3):
            pair = [
                win_ref[b, tile, pl.ds(4 * g + D * m, D)]
                for g in range(group, group + groups)
            ]
            pieces.append(jnp.concatenate(pair, 0).reshape(groups * D * s, c))
    return jnp.concatenate(pieces, 1)


def first_kernel(
    groups, near_ref, place_ref, x_ref, mate_ref, other_ref, w_ref, bias_ref, head_ref,
    u_ref, to_mate_ref, to_other_ref, sum_ref, win_ref, strip_ref,
):
    t, s, _, c = x_ref.shape
    fill_window(
        range(t), near_ref, place_ref, x_ref, mate_ref, other_ref, win_ref, strip_ref
    )
    bias = bias_ref[...]
    total = jnp.zeros((16, c), F32)
    for tile in range(t):
        for group in range(0, s // 4, groups):
            both = jnp.dot(
                band(win_ref, tile, group, groups), w_ref[...], preferred_element_type=F32
            )
            for half in range(2):
                pre = both[:, half * c : (half + 1) * c] + bias
                sig = 0.5 + 0.5 * jnp.tanh(0.5 * pre)
                silu = pre * sig
                total = total + jnp.sum(silu.reshape(-1, 16, c), 0)
                grad = (sig + silu * (1.0 - sig)).astype(BF)
                grad = grad.reshape(groups, D, s, c)
                for g in range(groups):
                    u_ref[tile, pl.ds(4 * (group + g) + D * half, D)] = grad[g]
    total = total * head_ref[...]
    sum_ref[...] = total
    put_strips(place_ref[1], u_ref, to_mate_ref, to_other_ref)
    high = total.astype(BF)
    rest = total - high.astype(F32)
    middle = rest.astype(BF)
    to_mate_ref[t + 1, 0, 0:16] = high
    to_mate_ref[t + 1, 0, 16:32] = middle
    to_mate_ref[t + 1, 1, 0:16] = (rest - middle.astype(F32)).astype(BF)
    to_mate_ref[t + 1, 1, 16:32] = jnp.zeros((16, c), BF)


def first_stage(near, place, x, mate, other, w, bias, head, groups=8):
    t, s, _, c = x.shape
    return pl.pallas_call(
        functools.partial(first_kernel, groups),
        out_shape=(
            jax.ShapeDtypeStruct(x.shape, BF),
            jax.ShapeDtypeStruct((t + 2, D, s, c), BF),
            jax.ShapeDtypeStruct((t + 1, D, s, c), BF),
            jax.ShapeDtypeStruct((16, c), F32),
        ),
        in_specs=[SMEM, SMEM] + [VMEM] * 6,
        out_specs=(VMEM,) * 4,
        scratch_shapes=window_scratch(t, t, s, c),
        compiler_params=params(),
        cost_estimate=pl.CostEstimate(
            flops=2 * 9 * t * s * s * c * c, bytes_accessed=4 << 20, transcendentals=t * s * s * c
        ),
        name="first",
    )(near, place, x, mate, other, w, bias, head)


def second_kernel(
    tiles, near_ref, place_ref, u_ref, mate_ref, other_ref, w_ref, o_ref, win_ref, strip_ref
):
    t, s, _, c = u_ref.shape
    fill_window(tiles, near_ref, place_ref, u_ref, mate_ref, other_ref, win_ref, strip_ref)
    for j in range(len(tiles)):
        taken = jnp.concatenate(
            [
                win_ref[b, j, D * a : D * a + s].reshape(s * s, c)
                for a in range(3)
                for b in range(3)
            ],
            1,
        )
        both = jnp.dot(taken, w_ref[...], preferred_element_type=F32)
        o_ref[j] = (both[:, :c] + both[:, c:]).reshape(s, s, c)


def second_stage(tiles, near, place, u, mate, other, w):
    t, s, _, c = u.shape
    n = len(tiles)
    return pl.pallas_call(
        functools.partial(second_kernel, tiles),
        out_shape=jax.ShapeDtypeStruct((n, s, s, c), F32),
        in_specs=[SMEM, SMEM] + [VMEM] * 4,
        out_specs=VMEM,
        scratch_shapes=window_scratch(n, t, s, c),
        compiler_params=params(),
        cost_estimate=pl.CostEstimate(
            flops=2 * 9 * n * s * s * c * c, bytes_accessed=n << 21, transcendentals=0
        ),
        name="second",
    )(near, place, u, mate, other, w)


def scale_kernel(count, n, label_ref, mine_ref, theirs_ref, *refs):
    parts, o_ref, stage_ref, sems = refs[:n], *refs[n:]
    score = jnp.sum(mine_ref[...] + theirs_ref[...], axis=(0, 1), keepdims=True) / count
    slope = jax.nn.sigmoid(score) - label_ref[0].astype(F32) / 100.0
    copies = []
    at = 0
    half = parts[0].shape[1] // 2
    for part in parts:
        for i in range(part.shape[0]):
            for h in range(2):
                rows = pl.ds(h * half, half)
                stage_ref[at, rows] = part[i, rows] * slope.reshape(1, 1, 1)
                copy = pltpu.make_async_copy(
                    stage_ref.at[at, rows], o_ref.at[at, rows], sems.at[at, h]
                )
                copy.start()
                copies.append(copy)
            at += 1
    for copy in copies:
        copy.wait()


def scale(label, mine, theirs, parts, count):
    t = sum(p.shape[0] for p in parts)
    s, _, c = parts[0].shape[1:]
    return pl.pallas_call(
        functools.partial(scale_kernel, count, len(parts)),
        out_shape=jax.ShapeDtypeStruct((t, s, s, c), F32),
        in_specs=[SMEM] + [VMEM] * (2 + len(parts)),
        out_specs=pl.BlockSpec(memory_space=pl.ANY),
        scratch_shapes=[pltpu.VMEM((t, s, s, c), F32), pltpu.SemaphoreType.DMA((t, 2))],
        compiler_params=params(),
        name="scale",
    )(label, mine, theirs, *parts)


def pieces(t):
    return [tuple(range(i, i + 1)) for i in range(t)]


def body(tissue_tiles, neighbours, conv_weight, conv_bias, head_weight, slide_label):
    t, s, _, c = tissue_tiles.shape
    size = lax.axis_size(GROUP)
    index = lax.axis_index(GROUP).astype(jnp.int32)
    place = jnp.stack([index * t, index % 2])
    head = head_weight.reshape(1, c)
    mate, other, x = make_strips(place, tissue_tiles)
    mate, other = swap(mate, other)
    w_first, w_second = make_weights(conv_weight, head)
    u, mate, other, mine = first_stage(
        neighbours, place, x, mate, other, w_first, conv_bias.reshape(1, c), head
    )
    mate, other = swap(mate, other)
    got = mate[t + 1].astype(F32)
    theirs = got[0, 0:16] + got[0, 16:32] + got[1, 0:16]
    if size & (size - 1):
        mine, theirs = lax.psum(mine, GROUP), jnp.zeros_like(mine)
    step = 2
    while step < size and not size & (size - 1):
        mine = mine + theirs
        theirs = lax.ppermute(mine, GROUP, [(i, i ^ step) for i in range(size)])
        step *= 2
    parts = [
        second_stage(tiles, neighbours, place, u, mate, other, w_second) for tiles in pieces(t)
    ]
    return scale(slide_label, mine, theirs, parts, float(t * size * s * s * c))


def solution(mesh):
    return jax.shard_map(
        body,
        mesh=mesh,
        in_specs=(
            P(("groups", "tile", "head"), None, None, None),
            P(("groups", "tile", "head"), None),
            P(),
            P(),
            P(),
            P("groups"),
        ),
        out_specs=P(("groups", "tile", "head"), None, None, None),
        check_vma=False,
    )
```

time: 54.8 us -> 36 us (0.66)
  Pallas kernels: 24.3 us -> 11.4 us
  waiting for transfers between devices: 6.92 us -> 0.38 us
  local copies, waits for them, and re-layouts: 1.28 us -> 4.82 us
  starting transfers between devices: 19.7 us -> 18.2 us
  other arithmetic: 1.27 us -> 0.09 us
    pallas_call x4 -> x7, Pallas kernels: 19.1 us -> 8.26 us  [the longest x4 5.79 us: second_stage(): pl.pallas_call(functools.partial(second_kernel, tiles), out_shape=jax.Sha...]
    ppermute x8 -> x7, waiting for transfers between devices: 6.92 us -> 0.38 us  [the longest x3 0.37 us: body(): theirs = lax.ppermute(mine, GROUP, [(i, i ^ step) for i in range(size)])]
    unnamed x8 -> x12, local copies, waits for them, and re-layouts: 1.28 us -> 4.82 us
    pallas_call x1, Pallas kernels: 5.19 us -> 3.19 us  [first_stage(): pl.pallas_call(functools.partial(first_kernel, groups), out_shape=(jax.Sh...]
    ppermute x8 -> x7, starting transfers between devices: 19.7 us -> 18.2 us  [the longest x3 12.2 us: body(): theirs = lax.ppermute(mine, GROUP, [(i, i ^ step) for i in range(size)])]
    add x4 -> x3, other arithmetic: 1.27 us -> 0.01 us  [body(): mine = mine + theirs]
  transfers between devices with their start and end apart: 8 -> 7, of which waited for: 5 -> 2; matrix products, arithmetic and copies ran while one was open for 2% -> 0% of each run, Pallas kernels for 4% -> 17%
where the time goes in v2:
time: 36 us; the launch traced here: 35.7 us
  starting transfers between devices  18.2 us (51%)
  Pallas kernels  11.4 us (32%)
  local copies, waits for them, and re-layouts  4.82 us (13%)
  between operations  0.79 us (2%)
  waiting for transfers between devices  0.38 us (1%)
    ppermute x3, starting transfers between devices, body(): theirs = lax.ppermute(mine, GROUP, [(i, i ^ step) for i in range(size)])  12.2 us
    pallas_call x4, Pallas kernels, second_stage(): pl.pallas_call(functools.partial(second_kernel, tiles), out_shape=jax.Sha...  5.79 us
    unnamed x12, local copies, waits for them, and re-layouts  4.82 us
    ppermute x2, starting transfers between devices, swap(): lax.ppermute(mate, GROUP, mates)  4.64 us
    pallas_call x1, Pallas kernels, first_stage(): pl.pallas_call(functools.partial(first_kernel, groups), out_shape=(jax.Sh...  3.19 us
    pallas_call x1, Pallas kernels, scale(): pl.pallas_call(functools.partial(scale_kernel, count, len(parts)), out_sh...  1.52 us
    ppermute x2, starting transfers between devices, swap(): lax.ppermute(other, GROUP, others)  1.32 us
  transfers between devices with their start and end apart: 7, of which 2 were waited for; matrix products, arithmetic and copies ran while one was open for 0% of the time, Pallas kernels for 17%

profile of v2, /device:TPU:0, one launch (start us, length us, event | category | flops | bytes accessed | tf_op | source)
XLA Modules:
  0.0 35.7 jit_solution(2831481578187899813)
XLA Ops:
  0.0 0.1 pad_add_fusion.place_ref
  0.1 0.0 copy-start
  0.1 1.2 %copy-done = bf16[4,32,32,128]{3,2,1,0:T(8,128)(2,1)S(1)} copy-done((bf16[4,32,32,128]{3,2,1,0:T(8,128)(2,1)S(1)}, bf16[4,32,32,128]{3,2,1,0:T(8,128)(2,1)}, u32[]{:S(2)}) %copy-start) | copy-done | bytes 1048600
  1.3 0.6 %strips.1 = (bf16[5,2,32,128]{3,2,1,0:T(8,128)(2,1)S(1)}, bf16[5,2,32,128]{3,2,1,0:T(8,128)(2,1)S(1)}, bf16[4,32,32,128]{3,2,1,0:T(8,128)(2,1)S(1)}) custom-call(s32[2]{0:T(128)S(1)} %pad_add_fusion.place_ref, bf16[4,32,32,128]{3,2,1,0:T(8,128)(2,1)S(1)} %copy-done), custom_call_target="tpu_custom_call" | custom-call | tf_op jit(solution)/shard_map/strips/pallas_call | solution.py:56
  2.0 0.6 %collective-permute-start = (bf16[5,2,32,128]{3,2,1,0:T(8,128)(2,1)S(1)}, bf16[5,2,32,128]{3,2,1,0:T(8,128)(2,1)S(1)}, u32[]{:S(2)}, u32[]{:S(2)}) collective-permute-start(bf16[5,2,32,128]{3,2,1,0:T(8,128)(2,1)S(1)} %get-tuple-element.15), channel_id=1, source_target_pairs={{0,1},{1,0},{2,3},{3,2},{4,5},{5,4},{6,7},{7,6},{8,9},{9,8},{10,11... | collective-permute-start | bytes 245768 | tf_op jit(solution)/shard_map/ppermute | solution.py:70
  2.5 0.7 %collective-permute-start.1 = (bf16[5,2,32,128]{3,2,1,0:T(8,128)(2,1)S(1)}, bf16[5,2,32,128]{3,2,1,0:T(8,128)(2,1)S(1)}, u32[]{:S(2)}, u32[]{:S(2)}) collective-permute-start(bf16[5,2,32,128]{3,2,1,0:T(8,128)(2,1)S(1)} %get-tuple-element.16), channel_id=1, source_target_pairs={{1,2},{2,1},{3,4},{4,3},{5,6},{6,5},{7,8},{8,7},{9,10},{10,9},{11,... | collective-permute-start | bytes 245768 | tf_op jit(solution)/shard_map/ppermute | solution.py:70
  3.2 0.0 copy-start.1
  3.2 1.0 %copy-done.1 = bf16[3,3,128,128]{3,2,1,0:T(8,128)(2,1)S(1)} copy-done((bf16[3,3,128,128]{3,2,1,0:T(8,128)(2,1)S(1)}, bf16[3,3,128,128]{3,2,1,0:T(8,128)(2,1)}, u32[]{:S(2)}) %copy-start.1) | copy-done | bytes 294936
  4.1 0.0 copy-start.3
  4.1 0.7 %copy-done.3 = f32[128]{0:T(128)S(1)} copy-done((f32[128]{0:T(128)S(1)}, f32[128]{0:T(128)}, u32[]{:S(2)}) %copy-start.3) | copy-done | bytes 536
  4.8 0.3 weights.1
  5.1 0.0 collective-permute-done.mate_ref
  5.1 0.0 collective-permute-done.1.other_ref
  5.1 0.0 copy-start.2
  5.1 0.7 %copy-done.2 = s32[4,8]{1,0:T(4,128)S(1)} copy-done((s32[4,8]{1,0:T(4,128)S(1)}, s32[4,8]{1,0:T(4,128)}, u32[]{:S(2)}) %copy-start.2) | copy-done | bytes 152
  5.8 0.0 copy-start.4
  5.8 0.7 %copy-done.4 = f32[128]{0:T(128)S(1)} copy-done((f32[128]{0:T(128)S(1)}, f32[128]{0:T(128)}, u32[]{:S(2)}) %copy-start.4) | copy-done | bytes 536
  6.5 0.0 copy-start.5
  6.5 0.7 %copy-done.5 = f32[128]{0:T(128)S(1)} copy-done((f32[128]{0:T(128)S(1)}, f32[128]{0:T(128)}, u32[]{:S(2)}) %copy-start.5) | copy-done | bytes 536
  7.1 3.2 %first.1 = (bf16[4,32,32,128]{3,2,1,0:T(8,128)(2,1)S(1)}, bf16[6,2,32,128]{3,2,1,0:T(8,128)(2,1)S(1)}, bf16[5,2,32,128]{3,2,1,0:T(8,128)(2,1)S(1)}, f32[16,128]{1,0:T(8,128)S(1)}) custom-call(s32[4,8]{1,0:T(4,128)S(1)} %copy-done.2, s32[2]{0:T(128)S(1)} %pad_add_fusion.place_ref, bf16[4,32,32,128]{3,2,1,0:T(8,128)(2,1)S(1)} %get-tuple-element.14.x_ref, ...), custom_call_target="tpu_custom_call" | custom-call | flops 1207959552 | bytes 4194304 | tf_op jit(solution)/shard_map/first/pallas_call | solution.py:217
  10.3 4.1 %collective-permute-start.2 = (bf16[6,2,32,128]{3,2,1,0:T(8,128)(2,1)S(1)}, bf16[6,2,32,128]{3,2,1,0:T(8,128)(2,1)S(1)}, u32[]{:S(2)}, u32[]{:S(2)}) collective-permute-start(bf16[6,2,32,128]{3,2,1,0:T(8,128)(2,1)S(1)} %get-tuple-element.19), channel_id=1, source_target_pairs={{0,1},{1,0},{2,3},{3,2},{4,5},{5,4},{6,7},{7,6},{8,9},{9,8},{10,11... | collective-permute-start | bytes 294920 | tf_op jit(solution)/shard_map/ppermute | solution.py:70
  15.1 0.7 %collective-permute-start.6 = (bf16[5,2,32,128]{3,2,1,0:T(8,128)(2,1)S(1)}, bf16[5,2,32,128]{3,2,1,0:T(8,128)(2,1)S(1)}, u32[]{:S(2)}, u32[]{:S(2)}) collective-permute-start(bf16[5,2,32,128]{3,2,1,0:T(8,128)(2,1)S(1)} %get-tuple-element.21), channel_id=1, source_target_pairs={{1,2},{2,1},{3,4},{4,3},{5,6},{6,5},{7,8},{8,7},{9,10},{10,9},{11,... | collective-permute-start | bytes 245768 | tf_op jit(solution)/shard_map/ppermute | solution.py:70
  15.7 0.0 collective-permute-done.2.mate_ref
  15.8 4.3 %collective-permute-start.3 = (f32[16,128]{1,0:T(8,128)S(1)}, f32[16,128]{1,0:T(8,128)S(1)}, u32[]{:S(2)}, u32[]{:S(2)}) collective-permute-start(f32[16,128]{1,0:T(8,128)S(1)} %fusion.2), channel_id=1, source_target_pairs={{0,2},{1,3},{2,0},{3,1},{4,6},{5,7},{6,4},{7,5},{8,10},{9,11},{10,... | collective-permute-start | bytes 24584 | tf_op jit(solution)/shard_map/ppermute | solution.py:331
  20.1 0.0 collective-permute-done.6.other_ref
  20.1 1.5 %second.7.refs_3_ = f32[1,32,32,128]{3,2,1,0:T(8,128)S(1)} custom-call(s32[4,8]{1,0:T(4,128)S(1)} %copy-done.2, s32[2]{0:T(128)S(1)} %pad_add_fusion.place_ref, bf16[4,32,32,128]{3,2,1,0:T(8,128)(2,1)S(1)} %get-tuple-element.20.u_ref, bf16[6,2,32,128]{3,2,1,0:T(8,128)(2,1)S(1)} %collective-permute-done.2.mate_ref, ...), custom_call_target="tpu_custom_call" | custom-call | flops 301989888 | bytes 2097152 | tf_op jit(solution)/shard_map/second/pallas_call | solution.py:257
  21.6 1.4 %second.6.refs_2_ = f32[1,32,32,128]{3,2,1,0:T(8,128)S(1)} custom-call(s32[4,8]{1,0:T(4,128)S(1)} %copy-done.2, s32[2]{0:T(128)S(1)} %pad_add_fusion.place_ref, bf16[4,32,32,128]{3,2,1,0:T(8,128)(2,1)S(1)} %get-tuple-element.20.u_ref, bf16[6,2,32,128]{3,2,1,0:T(8,128)(2,1)S(1)} %collective-permute-done.2.mate_ref, ...), custom_call_target="tpu_custom_call" | custom-call | flops 301989888 | bytes 2097152 | tf_op jit(solution)/shard_map/second/pallas_call | solution.py:257
  23.0 0.0 collective-permute-done.3
  23.0 4.8 %collective-permute-start.4 = (f32[16,128]{1,0:T(8,128)S(1)}, f32[16,128]{1,0:T(8,128)S(1)}, u32[]{:S(2)}, u32[]{:S(2)}) collective-permute-start(f32[16,128]{1,0:T(8,128)S(1)} %add.32), channel_id=1, source_target_pairs={{0,4},{1,5},{2,6},{3,7},{4,0},{5,1},{6,2},{7,3},{8,12},{9,13},{10,... | collective-permute-start | bytes 24584 | tf_op jit(solution)/shard_map/ppermute | solution.py:331
  27.9 1.4 %second.5.refs_1_ = f32[1,32,32,128]{3,2,1,0:T(8,128)S(1)} custom-call(s32[4,8]{1,0:T(4,128)S(1)} %copy-done.2, s32[2]{0:T(128)S(1)} %pad_add_fusion.place_ref, bf16[4,32,32,128]{3,2,1,0:T(8,128)(2,1)S(1)} %get-tuple-element.20.u_ref, bf16[6,2,32,128]{3,2,1,0:T(8,128)(2,1)S(1)} %collective-permute-done.2.mate_ref, ...), custom_call_target="tpu_custom_call" | custom-call | flops 301989888 | bytes 2097152 | tf_op jit(solution)/shard_map/second/pallas_call | solution.py:257
  29.3 0.2 collective-permute-done.4
  29.5 3.0 %collective-permute-start.5 = (f32[16,128]{1,0:T(8,128)S(1)}, f32[16,128]{1,0:T(8,128)S(1)}, u32[]{:S(2)}, u32[]{:S(2)}) collective-permute-start(f32[16,128]{1,0:T(8,128)S(1)} %add.33.mine_ref), channel_id=1, source_target_pairs={{0,8},{1,9},{2,10},{3,11},{4,12},{5,13},{6,14},{7,15},{8,0},{9,1},... | collective-permute-start | bytes 24584 | tf_op jit(solution)/shard_map/ppermute | solution.py:331
  32.6 1.4 %second.4.refs_0_ = f32[1,32,32,128]{3,2,1,0:T(8,128)S(1)} custom-call(s32[4,8]{1,0:T(4,128)S(1)} %copy-done.2, s32[2]{0:T(128)S(1)} %pad_add_fusion.place_ref, bf16[4,32,32,128]{3,2,1,0:T(8,128)(2,1)S(1)} %get-tuple-element.20.u_ref, bf16[6,2,32,128]{3,2,1,0:T(8,128)(2,1)S(1)} %collective-permute-done.2.mate_ref, ...), custom_call_target="tpu_custom_call" | custom-call | flops 301989888 | bytes 2097152 | tf_op jit(solution)/shard_map/second/pallas_call | solution.py:257
  34.0 0.2 collective-permute-done.5.theirs_ref
  34.2 1.5 %scale.1 = f32[4,32,32,128]{3,2,1,0:T(8,128)} custom-call(s32[1]{0:T(128)S(6)} %copy.7.label_ref, f32[16,128]{1,0:T(8,128)S(1)} %add.33.mine_ref, f32[16,128]{1,0:T(8,128)S(1)} %collective-permute-done.5.theirs_ref, f32[1,32,32,128]{3,2,1,0:T(8,128)S(1)} %second.4.refs_0_, f32[1,32,32,128]{3,2,1,0:T(8,128)S(1)} %second.5.refs_1_, ...), custom_call_target="tpu_custom_call" | custom-call | tf_op jit(solution)/shard_map/scale/pallas_call | solution.py:296
  (4 shorter events, 0.0 us)
Async XLA Ops:
  0.1 1.2 %copy-start = (bf16[4,32,32,128]{3,2,1,0:T(8,128)(2,1)S(1)}, bf16[4,32,32,128]{3,2,1,0:T(8,128)(2,1)}, u32[]{:S(2)}) copy-start(bf16[4,32,32,128]{3,2,1,0:T(8,128)(2,1)} %x_ref.1) | copy-start | bytes 3145732
  2.0 3.1 %collective-permute-start = (bf16[5,2,32,128]{3,2,1,0:T(8,128)(2,1)S(1)}, bf16[5,2,32,128]{3,2,1,0:T(8,128)(2,1)S(1)}, u32[]{:S(2)}, u32[]{:S(2)}) collective-permute-start(bf16[5,2,32,128]{3,2,1,0:T(8,128)(2,1)S(1)} %get-tuple-element.15), channel_id=1, source_target_pairs={{0,1},{1,0},{2,3},{3,2},{4,5},{5,4},{6,7},{7,6},{8,9},{9,8},{10,11... | collective-permute-start | bytes 245768 | tf_op jit(solution)/shard_map/ppermute | solution.py:70
  2.5 2.6 %collective-permute-start.1 = (bf16[5,2,32,128]{3,2,1,0:T(8,128)(2,1)S(1)}, bf16[5,2,32,128]{3,2,1,0:T(8,128)(2,1)S(1)}, u32[]{:S(2)}, u32[]{:S(2)}) collective-permute-start(bf16[5,2,32,128]{3,2,1,0:T(8,128)(2,1)S(1)} %get-tuple-element.16), channel_id=1, source_target_pairs={{1,2},{2,1},{3,4},{4,3},{5,6},{6,5},{7,8},{8,7},{9,10},{10,9},{11,... | collective-permute-start | bytes 245768 | tf_op jit(solution)/shard_map/ppermute | solution.py:70
  3.2 1.0 %copy-start.1 = (bf16[3,3,128,128]{3,2,1,0:T(8,128)(2,1)S(1)}, bf16[3,3,128,128]{3,2,1,0:T(8,128)(2,1)}, u32[]{:S(2)}) copy-start(bf16[3,3,128,128]{3,2,1,0:T(8,128)(2,1)} %w_ref.1) | copy-start | bytes 884740
  4.1 0.7 %copy-start.3 = (f32[128]{0:T(128)S(1)}, f32[128]{0:T(128)}, u32[]{:S(2)}) copy-start(f32[128]{0:T(128)} %param.10) | copy-start | bytes 1540
  5.1 0.7 %copy-start.2 = (s32[4,8]{1,0:T(4,128)S(1)}, s32[4,8]{1,0:T(4,128)}, u32[]{:S(2)}) copy-start(s32[4,8]{1,0:T(4,128)} %near_ref.9) | copy-start | bytes 388
  5.8 0.7 %copy-start.4 = (f32[128]{0:T(128)S(1)}, f32[128]{0:T(128)}, u32[]{:S(2)}) copy-start(f32[128]{0:T(128)} %param.10) | copy-start | bytes 1540
  6.5 0.7 %copy-start.5 = (f32[128]{0:T(128)S(1)}, f32[128]{0:T(128)}, u32[]{:S(2)}) copy-start(f32[128]{0:T(128)} %param.9) | copy-start | bytes 1540
  10.3 5.4 %collective-permute-start.2 = (bf16[6,2,32,128]{3,2,1,0:T(8,128)(2,1)S(1)}, bf16[6,2,32,128]{3,2,1,0:T(8,128)(2,1)S(1)}, u32[]{:S(2)}, u32[]{:S(2)}) collective-permute-start(bf16[6,2,32,128]{3,2,1,0:T(8,128)(2,1)S(1)} %get-tuple-element.19), channel_id=1, source_target_pairs={{0,1},{1,0},{2,3},{3,2},{4,5},{5,4},{6,7},{7,6},{8,9},{9,8},{10,11... | collective-permute-start | bytes 294920 | tf_op jit(solution)/shard_map/ppermute | solution.py:70
  15.1 5.0 %collective-permute-start.6 = (bf16[5,2,32,128]{3,2,1,0:T(8,128)(2,1)S(1)}, bf16[5,2,32,128]{3,2,1,0:T(8,128)(2,1)S(1)}, u32[]{:S(2)}, u32[]{:S(2)}) collective-permute-start(bf16[5,2,32,128]{3,2,1,0:T(8,128)(2,1)S(1)} %get-tuple-element.21), channel_id=1, source_target_pairs={{1,2},{2,1},{3,4},{4,3},{5,6},{6,5},{7,8},{8,7},{9,10},{10,9},{11,... | collective-permute-start | bytes 245768 | tf_op jit(solution)/shard_map/ppermute | solution.py:70
  15.8 7.3 %collective-permute-start.3 = (f32[16,128]{1,0:T(8,128)S(1)}, f32[16,128]{1,0:T(8,128)S(1)}, u32[]{:S(2)}, u32[]{:S(2)}) collective-permute-start(f32[16,128]{1,0:T(8,128)S(1)} %fusion.2), channel_id=1, source_target_pairs={{0,2},{1,3},{2,0},{3,1},{4,6},{5,7},{6,4},{7,5},{8,10},{9,11},{10,... | collective-permute-start | bytes 24584 | tf_op jit(solution)/shard_map/ppermute | solution.py:331
  23.0 6.5 %collective-permute-start.4 = (f32[16,128]{1,0:T(8,128)S(1)}, f32[16,128]{1,0:T(8,128)S(1)}, u32[]{:S(2)}, u32[]{:S(2)}) collective-permute-start(f32[16,128]{1,0:T(8,128)S(1)} %add.32), channel_id=1, source_target_pairs={{0,4},{1,5},{2,6},{3,7},{4,0},{5,1},{6,2},{7,3},{8,12},{9,13},{10,... | collective-permute-start | bytes 24584 | tf_op jit(solution)/shard_map/ppermute | solution.py:331
  29.5 4.7 %collective-permute-start.5 = (f32[16,128]{1,0:T(8,128)S(1)}, f32[16,128]{1,0:T(8,128)S(1)}, u32[]{:S(2)}, u32[]{:S(2)}) collective-permute-start(f32[16,128]{1,0:T(8,128)S(1)} %add.33.mine_ref), channel_id=1, source_target_pairs={{0,8},{1,9},{2,10},{3,11},{4,12},{5,13},{6,14},{7,15},{8,0},{9,1},... | collective-permute-start | bytes 24584 | tf_op jit(solution)/shard_map/ppermute | solution.py:331

commit v3 on v0

v3 whole, which is shorter than its diff:
```python
import functools

import jax
import jax.numpy as jnp
from jax import lax
from jax.experimental import pallas as pl
from jax.experimental.pallas import tpu as pltpu
from jax.sharding import PartitionSpec as P

D = 2
GROUP = ("tile", "head")
BF = jnp.bfloat16
F32 = jnp.float32
VMEM = pl.BlockSpec(memory_space=pltpu.VMEM)
HBM = pl.BlockSpec(memory_space=pltpu.HBM)
KEPT = 0.90625
REACH = (4, 3, 2)


def params(limit=24 << 20):
    return pltpu.CompilerParams(vmem_limit_bytes=limit)


def in_hbm(*arrays):
    return [pltpu.with_memory_space_constraint(a, pltpu.HBM) for a in arrays]


def my_index():
    return lax.axis_index("tile") * lax.axis_size("head") + lax.axis_index("head")


def put_strips(top, bottom, left, right, mate_ref, other_ref):
    t, _, s, _ = top.shape
    per = s // D
    parity = my_index() % 2

    def put(ref, rows, columns, at_end):
        ref[0:t] = rows[...]
        first = columns.shape[1] - D if at_end else 0
        for i in range(s):
            ref[t, i // per, pl.ds((i % per) * D, D), :] = columns[i, first : first + D, :]

    @pl.when(parity == 0)
    def _():
        put(mate_ref, bottom, right, True)
        put(other_ref, top, left, False)

    @pl.when(parity == 1)
    def _():
        put(mate_ref, top, left, False)
        put(other_ref, bottom, right, True)


def strips_kernel(x_ref, mate_ref, other_ref, top, bottom, left, right, sems):
    t, s = x_ref.shape[:2]
    e = left.shape[1]
    copies = [
        pltpu.make_async_copy(x_ref.at[0, :, 0:e], left, sems.at[0]),
        pltpu.make_async_copy(x_ref.at[t - 1, :, s - e : s], right, sems.at[1]),
        pltpu.make_async_copy(x_ref.at[:, 0:D], top, sems.at[2]),
        pltpu.make_async_copy(x_ref.at[:, s - D : s], bottom, sems.at[3]),
    ]
    for copy in copies:
        copy.start()
    for copy in copies:
        copy.wait()
    put_strips(top, bottom, left, right, mate_ref, other_ref)


def make_strips(x):
    t, s, _, c = x.shape
    out = jax.ShapeDtypeStruct((t + 1, D, s, c), BF)
    return pl.pallas_call(
        strips_kernel,
        out_shape=(out, out),
        in_specs=[HBM],
        out_specs=(VMEM,) * 2,
        scratch_shapes=[pltpu.VMEM((t, D, s, c), BF)] * 2
        + [pltpu.VMEM((s, 16, c), BF)] * 2
        + [pltpu.SemaphoreType.DMA((4,))],
        compiler_params=params(),
        name="strips",
    )(*in_hbm(x))


def swap(mate, other):
    size = lax.axis_size(GROUP)
    mates = [(i, i ^ 1) for i in range(size) if i ^ 1 < size]
    others = [(i, j) for i in range(size) for j in [(i + 1 ^ 1) - 1] if 0 <= j < size]
    return lax.ppermute(mate, GROUP, mates), lax.ppermute(other, GROUP, others)


def regions(t, s):
    inner, outer = [], []
    h = s // 2
    for i in range(t):
        first, last = i == 0, i == t - 1
        outer += [(i, 0, 4, 0, s), (i, s - 4, 4, 0, s)]
        for column in (0, h):
            alone = not (first and column == 0) and not (last and column == h)
            (inner if alone else outer).append((i, 4, s - 8, column, h))
    return inner, outer


def fill_own(tiles, src_ref, win_ref):
    s = src_ref.shape[1]
    for i in tiles:
        v = src_ref[i]
        win_ref[0, i, D : D + s, D:] = v[:, : s - D]
        win_ref[1, i, D : D + s] = v
        win_ref[2, i, D : D + s, : s - D] = v[:, D:]


def fill_beside(tiles, beside_ref, src_ref, win_ref):
    t, s, _, c = src_ref.shape
    for i in tiles:
        if i > 0:
            there = beside_ref[i, 0, 0:D].reshape(1, D, c)
            win_ref[0, i, D : D + s, :D] = src_ref[i - 1, :, s - D :] * there
        if i < t - 1:
            there = beside_ref[i, 1, 0:D].reshape(1, D, c)
            win_ref[2, i, D : D + s, s - D :] = src_ref[i + 1, :, :D] * there


def fill_border(beside_ref, mask_ref, mate_ref, other_ref, win_ref, both_ref):
    t, s, c = win_ref.shape[1], win_ref.shape[3], win_ref.shape[4]
    parity = my_index() % 2
    both_ref[0] = mate_ref[0 : t + 1]
    both_ref[1] = other_ref[0 : t + 1]
    prev_ref, next_ref = both_ref.at[1 - parity], both_ref.at[parity]

    def low(i):
        return prev_ref[t + i] if i < 0 else win_ref[1, i, s : s + D]

    def high(i):
        return next_ref[i - t] if i >= t else win_ref[1, i, D : 2 * D]

    per = s // D
    has_left = beside_ref[0, 0, 0:D]
    has_right = beside_ref[t - 1, 1, 0:D]
    for r in range(s):
        at = pl.ds((r % per) * D, D)
        win_ref[0, 0, D + r, :D] = prev_ref[t, r // per, at, :] * has_left
        win_ref[2, t - 1, D + r, s - D :] = next_ref[t, r // per, at, :] * has_right

    def pick(strip, i, side, kind, columns):
        total = None
        for step in range(1, REACH[kind] + 1):
            rows = strip(i - step if side == 0 else i + step)[:, columns]
            n = rows.shape[1] // 16
            mask = mask_ref[i, side, sum(REACH[:kind]) + step - 1]
            term = rows.reshape(D, n, 16, c) * mask.reshape(1, 1, 16, c)
            total = term if total is None else total + term
        return total.reshape(D, n * 16, c)

    for i in range(t):
        for side, strip, row in ((0, low, 0), (1, high, D + s)):
            rows = slice(row, row + D)
            middle = pick(strip, i, side, 1, slice(0, s))
            left = pick(strip, i, side, 2 * side, slice(s - 16, s))
            right = pick(strip, i, side, 2 - 2 * side, slice(0, 16))
            win_ref[0, i, rows, D:] = middle[:, : s - D]
            win_ref[0, i, rows, :D] = left[:, 16 - D :]
            win_ref[1, i, rows] = middle
            win_ref[2, i, rows, : s - D] = middle[:, D:]
            win_ref[2, i, rows, s - D :] = right[:, :D]


def first_part(places, win_ref, w_ref, bias, u_ref):
    c = w_ref.shape[1] // 2
    pieces = []
    for m in range(4):
        for b in range(3):
            rows = [
                win_ref[b, i, r + D * m : r + D * m + D, q : q + n].reshape(D * n, c)
                for i, row, count, q, n in places
                for r in range(row, row + count, 2 * D)
            ]
            pieces.append(jnp.concatenate(rows, 0))
    both = jnp.dot(jnp.concatenate(pieces, 1), w_ref[...], preferred_element_type=F32)
    total = jnp.zeros((16, c), F32)
    for half in range(2):
        pre = both[:, half * c : (half + 1) * c] + bias
        sig = 0.5 + 0.5 * jnp.tanh(0.5 * pre)
        silu = pre * sig
        total = total + jnp.sum(silu.reshape(-1, 16, c), 0)
        kept = (KEPT * (sig + silu * (1.0 - sig))).astype(BF)
        at = 0
        for i, row, count, q, n in places:
            for r in range(row + D * half, row + count, 2 * D):
                u_ref[i, r : r + D, q : q + n] = kept[at : at + D * n].reshape(D, n, c)
                at += D * n
    return total


def second_part(places, win_ref, w_ref, v_ref):
    c = w_ref.shape[1] // 2
    pieces = []
    for a in range(3):
        for b in range(3):
            rows = [
                win_ref[b, i, r + D * a : r + D * a + count, q : q + n].reshape(count * n, c)
                for i, r, count, q, n in places
            ]
            pieces.append(jnp.concatenate(rows, 0))
    both = jnp.dot(jnp.concatenate(pieces, 1), w_ref[...], preferred_element_type=F32)
    out = both[:, :c] + both[:, c:]
    at = 0
    for i, r, count, q, n in places:
        v_ref[i, r : r + count, q : q + n] = out[at : at + count * n].reshape(count, n, c)
        at += count * n


def inner_kernel(
    x_hbm, w_hbm, near_hbm, bias_hbm, head_hbm, label_hbm,
    u_ref, win_ref, first_ref, second_ref, sum_ref, small_ref, beside_ref, mask_ref,
    x_ref, w_ref, bias_ref, head_ref, near_ref, label_ref, sems,
):
    t, s, _, c = x_ref.shape
    moves = [
        (x_hbm, x_ref), (w_hbm, w_ref), (head_hbm, head_ref), (bias_hbm, bias_ref),
        (near_hbm, near_ref), (label_hbm, label_ref),
    ]
    copies = [pltpu.make_async_copy(a, b, sems.at[i]) for i, (a, b) in enumerate(moves)]
    for copy in copies:
        copy.start()
    for copy in copies[1:]:
        copy.wait()
    small_ref[0:1] = head_ref[...]
    small_ref[1:2] = bias_ref[...]
    small_ref[2:3] = jnp.full((1, c), label_ref[0], jnp.int32).astype(F32)
    start = my_index() * t

    def flag(yes):
        return jnp.full((16, c), jnp.where(yes, 1.0, 0.0), F32).astype(BF)

    for i in range(t):
        beside_ref[i, 0] = flag(near_ref[i, 3] >= 0)
        beside_ref[i, 1] = flag(near_ref[i, 4] >= 0)
        for side in range(2):
            at = 0
            for kind in range(3):
                k = kind if side == 0 else 7 - kind
                for step in range(1, REACH[kind] + 1):
                    there = start + (i - step if side == 0 else i + step)
                    mask_ref[i, side, at] = flag((near_ref[i, k] == there) & (there >= 0))
                    at += 1
    blank = jnp.zeros((c, c), BF)
    head = head_ref[...] * (1.0 / KEPT)
    for b in range(3):
        for m in range(4):
            rows = pl.ds((m * 3 + b) * c, c)
            for half in range(2):
                a = m - half
                first_ref[rows, pl.ds(half * c, c)] = w_ref[a, b] if 0 <= a < 3 else blank
        for a in range(3):
            rows = pl.ds((a * 3 + b) * c, c)
            turned = (w_ref[2 - a, 2 - b].astype(F32) * head).T
            upper = turned.astype(BF)
            second_ref[rows, 0:c] = upper
            second_ref[rows, c : 2 * c] = (turned - upper.astype(F32)).astype(BF)
    copies[0].wait()
    fill_own(range(t), x_ref, win_ref)
    fill_beside(range(t), beside_ref, x_ref, win_ref)
    sum_ref[...] = first_part(regions(t, s)[0], win_ref, first_ref, bias_ref[...], u_ref)


def inner_stage(x, w, near, bias, head, label):
    t, s, _, c = x.shape
    return pl.pallas_call(
        inner_kernel,
        out_shape=(
            jax.ShapeDtypeStruct(x.shape, BF),
            jax.ShapeDtypeStruct((3, t, s + 2 * D, s, c), BF),
            jax.ShapeDtypeStruct((12 * c, 2 * c), BF),
            jax.ShapeDtypeStruct((9 * c, 2 * c), BF),
            jax.ShapeDtypeStruct((16, c), F32),
            jax.ShapeDtypeStruct((3, c), F32),
            jax.ShapeDtypeStruct((t, 2, 16, c), BF),
            jax.ShapeDtypeStruct((t, 2, sum(REACH), 16, c), BF),
        ),
        in_specs=[HBM] * 6,
        out_specs=(VMEM,) * 8,
        scratch_shapes=[
            pltpu.VMEM(x.shape, BF),
            pltpu.VMEM(w.shape, BF),
            pltpu.VMEM((1, c), F32),
            pltpu.VMEM((1, c), F32),
            pltpu.SMEM(near.shape, jnp.int32),
            pltpu.SMEM((1,), jnp.int32),
            pltpu.SemaphoreType.DMA((6,)),
        ],
        compiler_params=params(),
        cost_estimate=pl.CostEstimate(
            flops=9 * t * s * s * c * c, bytes_accessed=6 << 20, transcendentals=t * s * s * c // 2
        ),
        name="inner",
    )(*in_hbm(x, w, near, bias, head), label)


def outer_kernel(
    mate_ref, other_ref, w_ref, small_ref, beside_ref, mask_ref, part_ref, u_in, win_in,
    u_ref, win_ref, to_mate_ref, to_other_ref, sum_ref, both_ref,
):
    del u_in, win_in
    t, s, _, c = u_ref.shape
    fill_border(beside_ref, mask_ref, mate_ref, other_ref, win_ref, both_ref)
    total = part_ref[...] + first_part(
        regions(t, s)[1], win_ref, w_ref, small_ref[1:2], u_ref
    )
    total = total * small_ref[0:1]
    sum_ref[...] = total
    put_strips(
        u_ref.at[:, 0:D], u_ref.at[:, s - D : s],
        u_ref.at[0, :, 0:16], u_ref.at[t - 1, :, s - 16 : s], to_mate_ref, to_other_ref,
    )
    upper = total.astype(BF)
    rest = total - upper.astype(F32)
    middle = rest.astype(BF)
    to_mate_ref[t + 1, 0, 0:16] = upper
    to_mate_ref[t + 1, 0, 16:32] = middle
    to_mate_ref[t + 1, 1, 0:16] = (rest - middle.astype(F32)).astype(BF)
    to_mate_ref[t + 1, 1, 16:32] = jnp.zeros((16, c), BF)


def outer_stage(mate, other, w, small, beside, mask, part, u, win):
    t, s, _, c = u.shape
    return pl.pallas_call(
        outer_kernel,
        out_shape=(
            jax.ShapeDtypeStruct(u.shape, BF),
            jax.ShapeDtypeStruct(win.shape, BF),
            jax.ShapeDtypeStruct((t + 2, D, s, c), BF),
            jax.ShapeDtypeStruct((t + 1, D, s, c), BF),
            jax.ShapeDtypeStruct((16, c), F32),
        ),
        in_specs=[VMEM] * 9,
        out_specs=(VMEM,) * 5,
        input_output_aliases={7: 0, 8: 1},
        scratch_shapes=[pltpu.VMEM((2, t + 1, D, s, c), BF)],
        compiler_params=params(),
        cost_estimate=pl.CostEstimate(
            flops=9 * t * s * s * c * c, bytes_accessed=4 << 20, transcendentals=t * s * s * c // 2
        ),
        name="outer",
    )(mate, other, w, small, beside, mask, part, u, win)


def back_inner_kernel(tiles, u_ref, w_ref, beside_ref, *refs):
    win_ref, v_ref = refs[-2:]
    t, s = u_ref.shape[:2]
    fill_own(tiles, u_ref, win_ref)
    fill_beside(tiles, beside_ref, u_ref, win_ref)
    places = [p for p in regions(t, s)[0] if p[0] in tiles]
    second_part(places, win_ref, w_ref, v_ref)


def back_inner(tiles, u, w, beside, held=()):
    t, s, _, c = u.shape
    return pl.pallas_call(
        functools.partial(back_inner_kernel, tiles),
        out_shape=(
            jax.ShapeDtypeStruct((3, t, s + 2 * D, s, c), BF),
            jax.ShapeDtypeStruct(u.shape, F32),
        ),
        in_specs=[VMEM] * (3 + len(held)),
        out_specs=(VMEM, VMEM),
        input_output_aliases={3: 0, 4: 1} if held else {},
        compiler_params=params(),
        cost_estimate=pl.CostEstimate(
            flops=5 * t * s * s * c * c, bytes_accessed=2 << 20, transcendentals=0
        ),
        name="back_inner",
    )(u, w, beside, *held)


def back_outer_kernel(mate_ref, other_ref, w_ref, beside_ref, mask_ref, win_in, v_in, win_ref, v_ref, both_ref):
    del win_in, v_in
    t, s = v_ref.shape[:2]
    fill_border(beside_ref, mask_ref, mate_ref, other_ref, win_ref, both_ref)
    second_part(regions(t, s)[1], win_ref, w_ref, v_ref)


def back_outer(mate, other, w, beside, mask, win, v):
    t, s, _, c = v.shape
    return pl.pallas_call(
        back_outer_kernel,
        out_shape=(
            jax.ShapeDtypeStruct(win.shape, BF),
            jax.ShapeDtypeStruct(v.shape, F32),
        ),
        in_specs=[VMEM] * 7,
        out_specs=(VMEM, VMEM),
        input_output_aliases={5: 0, 6: 1},
        scratch_shapes=[pltpu.VMEM((2, t + 1, D, s, c), BF)],
        compiler_params=params(),
        cost_estimate=pl.CostEstimate(
            flops=8 * t * s * s * c * c, bytes_accessed=2 << 20, transcendentals=0
        ),
        name="back_outer",
    )(mate, other, w, beside, mask, win, v)[1]


def scale_kernel(count, small_ref, mine_ref, theirs_ref, v_ref, o_ref, stage_ref, sems):
    score = jnp.sum(mine_ref[...] + theirs_ref[...], axis=(0, 1), keepdims=True) / count
    slope = jax.nn.sigmoid(score) - small_ref[2:3, 0:1] / 100.0
    t, s = v_ref.shape[:2]
    copies = []
    for i in range(t):
        for h in range(2):
            rows = pl.ds(h * s // 2, s // 2)
            stage_ref[i, rows] = v_ref[i, rows] * slope.reshape(1, 1, 1)
            copy = pltpu.make_async_copy(stage_ref.at[i, rows], o_ref.at[i, rows], sems.at[i, h])
            copy.start()
            copies.append(copy)
    for copy in copies:
        copy.wait()


def scale(small, mine, theirs, v, count):
    return pl.pallas_call(
        functools.partial(scale_kernel, count),
        out_shape=jax.ShapeDtypeStruct(v.shape, F32),
        in_specs=[VMEM] * 4,
        out_specs=HBM,
        scratch_shapes=[pltpu.VMEM(v.shape, F32), pltpu.SemaphoreType.DMA((v.shape[0], 2))],
        compiler_params=params(),
        name="scale",
    )(small, mine, theirs, v)


def body(tissue_tiles, neighbours, conv_weight, conv_bias, head_weight, slide_label):
    t, s, _, c = tissue_tiles.shape
    size = lax.axis_size(GROUP)
    mate, other = swap(*make_strips(tissue_tiles))
    u, win, w_first, w_second, part, small, beside, mask = inner_stage(
        tissue_tiles, conv_weight, neighbours, conv_bias.reshape(1, c), head_weight.reshape(1, c),
        slide_label,
    )
    u, _, mate, other, mine = outer_stage(
        mate, other, w_first, small, beside, mask, part, u, win
    )
    mate, other = swap(mate, other)
    got = mate[t + 1].astype(F32)
    theirs = got[0, 0:16] + got[0, 16:32] + got[1, 0:16]
    if size & (size - 1):
        mine, theirs = lax.psum(mine, GROUP), jnp.zeros_like(mine)
    step = 2
    while step < size and not size & (size - 1):
        mine = mine + theirs
        theirs = lax.ppermute(mine, GROUP, [(i, i ^ step) for i in range(size)])
        step *= 2
    held = back_inner(tuple(range(1, t - 1)), u, w_second, beside)
    held = back_inner((0, t - 1), u, w_second, beside, held)
    v = back_outer(mate, other, w_second, beside, mask, *held)
    return scale(small, mine, theirs, v, float(t * size * s * s * c))


def solution(mesh):
    return jax.shard_map(
        body,
        mesh=mesh,
        in_specs=(
            P(("groups", "tile", "head"), None, None, None),
            P(("groups", "tile", "head"), None),
            P(),
            P(),
            P(),
            P("groups"),
        ),
        out_specs=P(("groups", "tile", "head"), None, None, None),
        check_vma=False,
    )
```

time: 80.2 us -> 28.3 us (0.35)
  the two profiles are of different devices: /device:TPU:1 before, /device:TPU:0 now
where the time goes in v3:
time: 28.3 us; the launch traced here: 28.1 us
  starting transfers between devices  14.4 us (51%)
  Pallas kernels  10.4 us (37%)
  waiting for transfers between devices  2.52 us (9%)
  between operations  0.72 us (3%)
    ppermute x3, starting transfers between devices, body(): theirs = lax.ppermute(mine, GROUP, [(i, i ^ step) for i in range(size)])  8.62 us
    ppermute x2, starting transfers between devices, swap(): lax.ppermute(mate, GROUP, mates)  4.49 us
    pallas_call x1, Pallas kernels, inner_stage(): pl.pallas_call(inner_kernel, out_shape=(jax.ShapeDtypeStruct(x.shape, BF)...  3.26 us
    ppermute x3, waiting for transfers between devices, body(): theirs = lax.ppermute(mine, GROUP, [(i, i ^ step) for i in range(size)])  2.23 us
    pallas_call x2, Pallas kernels, back_inner(): pl.pallas_call(functools.partial(back_inner_kernel, tiles), out_shape=(ja...  1.98 us
    pallas_call x1, Pallas kernels, scale(): pl.pallas_call(functools.partial(scale_kernel, count), out_shape=jax.Shap...  1.55 us
    pallas_call x1, Pallas kernels, back_outer(): pl.pallas_call(back_outer_kernel, out_shape=(jax.ShapeDtypeStruct(win.sha...  1.41 us
    ppermute x2, starting transfers between devices, swap(): lax.ppermute(other, GROUP, others)  1.31 us
  transfers between devices with their start and end apart: 7, of which 4 were waited for; matrix products, arithmetic and copies ran while one was open for 0% of the time, Pallas kernels for 24%

profile of v3, /device:TPU:0, one launch (start us, length us, event | category | flops | bytes accessed | tf_op | source)
XLA Modules:
  0.0 28.1 jit_solution(5370526921264097530)
XLA Ops:
  0.0 1.1 %strips.1 = (bf16[5,2,32,128]{3,2,1,0:T(8,128)(2,1)S(1)}, bf16[5,2,32,128]{3,2,1,0:T(8,128)(2,1)S(1)}) custom-call(bf16[4,32,32,128]{3,2,1,0:T(8,128)(2,1)} %x_ref.1), custom_call_target="tpu_custom_call" | custom-call | tf_op jit(solution)/shard_map/strips/pallas_call | solution.py:73
  1.1 0.6 %collective-permute-start = (bf16[5,2,32,128]{3,2,1,0:T(8,128)(2,1)S(1)}, bf16[5,2,32,128]{3,2,1,0:T(8,128)(2,1)S(1)}, u32[]{:S(2)}, u32[]{:S(2)}) collective-permute-start(bf16[5,2,32,128]{3,2,1,0:T(8,128)(2,1)S(1)} %get-tuple-element.25), channel_id=1, source_target_pairs={{0,1},{1,0},{2,3},{3,2},{4,5},{5,4},{6,7},{7,6},{8,9},{9,8},{10,11... | collective-permute-start | bytes 245768 | tf_op jit(solution)/shard_map/ppermute | solution.py:90
  1.6 0.7 %collective-permute-start.1 = (bf16[5,2,32,128]{3,2,1,0:T(8,128)(2,1)S(1)}, bf16[5,2,32,128]{3,2,1,0:T(8,128)(2,1)S(1)}, u32[]{:S(2)}, u32[]{:S(2)}) collective-permute-start(bf16[5,2,32,128]{3,2,1,0:T(8,128)(2,1)S(1)} %get-tuple-element.26), channel_id=1, source_target_pairs={{1,2},{2,1},{3,4},{4,3},{5,6},{6,5},{7,8},{8,7},{9,10},{10,9},{11,... | collective-permute-start | bytes 245768 | tf_op jit(solution)/shard_map/ppermute | solution.py:90
  2.9 3.3 %inner.1 = (bf16[4,32,32,128]{3,2,1,0:T(8,128)(2,1)S(1)}, bf16[3,4,36,32,128]{4,3,2,1,0:T(8,128)(2,1)S(1)}, bf16[1536,256]{1,0:T(8,128)(2,1)S(1)}, bf16[1152,256...) custom-call(bf16[4,32,32,128]{3,2,1,0:T(8,128)(2,1)} %x_ref.1, ...), custom_call_target="tpu_custom_call" | custom-call | flops 603979776 | bytes 6291456 | tf_op jit(solution)/shard_map/inner/pallas_call | solution.py:270
  6.2 0.0 collective-permute-done.mate_ref
  6.2 0.0 collective-permute-done.1.other_ref
  6.2 1.2 %outer.1 = (bf16[4,32,32,128]{3,2,1,0:T(8,128)(2,1)S(1)}, bf16[3,4,36,32,128]{4,3,2,1,0:T(8,128)(2,1)S(1)}, bf16[6,2,32,128]{3,2,1,0:T(8,128)(2,1)S(1)}, bf16[5,...) custom-call(bf16[5,2,32,128]{3,2,1,0:T(8,128)(2,1)S(1)} %collective-permute-done.mate_ref, ...), custom_call_target="tpu_custom_call", output_to_operand_aliasing={{0}: (7, {}), {1}: (8, {})} | custom-call | flops 603979776 | bytes 4194304 | tf_op jit(solution)/shard_map/outer/pallas_call | solution.py:328
  7.4 3.9 %collective-permute-start.2 = (bf16[6,2,32,128]{3,2,1,0:T(8,128)(2,1)S(1)}, bf16[6,2,32,128]{3,2,1,0:T(8,128)(2,1)S(1)}, u32[]{:S(2)}, u32[]{:S(2)}) collective-permute-start(bf16[6,2,32,128]{3,2,1,0:T(8,128)(2,1)S(1)} %get-tuple-element.34), channel_id=1, source_target_pairs={{0,1},{1,0},{2,3},{3,2},{4,5},{5,4},{6,7},{7,6},{8,9},{9,8},{10,11... | collective-permute-start | bytes 294920 | tf_op jit(solution)/shard_map/ppermute | solution.py:90
  11.3 0.7 %collective-permute-start.6 = (bf16[5,2,32,128]{3,2,1,0:T(8,128)(2,1)S(1)}, bf16[5,2,32,128]{3,2,1,0:T(8,128)(2,1)S(1)}, u32[]{:S(2)}, u32[]{:S(2)}) collective-permute-start(bf16[5,2,32,128]{3,2,1,0:T(8,128)(2,1)S(1)} %get-tuple-element.35), channel_id=1, source_target_pairs={{1,2},{2,1},{3,4},{4,3},{5,6},{6,5},{7,8},{8,7},{9,10},{10,9},{11,... | collective-permute-start | bytes 245768 | tf_op jit(solution)/shard_map/ppermute | solution.py:90
  12.0 0.3 %collective-permute-done.2.mate_ref = bf16[6,2,32,128]{3,2,1,0:T(8,128)(2,1)S(1)} collective-permute-done((bf16[6,2,32,128]{3,2,1,0:T(8,128)(2,1)S(1)}, bf16[6,2,32,128]{3,2,1,0:T(8,128)(2,1)S(1)}, u32[]{:S(2)}, u32[]{:S(2)}) %collective-permute-start.2) | collective-permute-done | bytes 98336 | tf_op jit(solution)/shard_map/ppermute | solution.py:90
  12.3 2.7 %collective-permute-start.3 = (f32[16,128]{1,0:T(8,128)S(1)}, f32[16,128]{1,0:T(8,128)S(1)}, u32[]{:S(2)}, u32[]{:S(2)}) collective-permute-start(f32[16,128]{1,0:T(8,128)S(1)} %fusion.2), channel_id=1, source_target_pairs={{0,2},{1,3},{2,0},{3,1},{4,6},{5,7},{6,4},{7,5},{8,10},{9,11},{10,... | collective-permute-start | bytes 24584 | tf_op jit(solution)/shard_map/ppermute | solution.py:451
  15.0 1.2 %back_inner.2 = (bf16[3,4,36,32,128]{4,3,2,1,0:T(8,128)(2,1)S(1)}, f32[4,32,32,128]{3,2,1,0:T(8,128)S(1)}) custom-call(bf16[4,32,32,128]{3,2,1,0:T(8,128)(2,1)S(1)} %get-tuple-element.37.u_ref, bf16[1152,256]{1,0:T(8,128)(2,1)S(1)} %get-tuple-element.36.w_ref, bf16[4,2,16,128]{3,2,1,0:T(8,128)(2,1)S(1)} %get-tuple-element.28.beside_ref), custom_call_target="tpu_custom_call" | custom-call | flops 335544320 | bytes 2097152 | tf_op jit(solution)/shard_map/back_inner/pallas_call | solution.py:360
  16.2 1.1 %collective-permute-done.3 = f32[16,128]{1,0:T(8,128)S(1)} collective-permute-done((f32[16,128]{1,0:T(8,128)S(1)}, f32[16,128]{1,0:T(8,128)S(1)}, u32[]{:S(2)}, u32[]{:S(2)}) %collective-permute-start.3) | collective-permute-done | bytes 8224 | tf_op jit(solution)/shard_map/ppermute | solution.py:451
  17.4 2.9 %collective-permute-start.4 = (f32[16,128]{1,0:T(8,128)S(1)}, f32[16,128]{1,0:T(8,128)S(1)}, u32[]{:S(2)}, u32[]{:S(2)}) collective-permute-start(f32[16,128]{1,0:T(8,128)S(1)} %add.23), channel_id=1, source_target_pairs={{0,4},{1,5},{2,6},{3,7},{4,0},{5,1},{6,2},{7,3},{8,12},{9,13},{10,... | collective-permute-start | bytes 24584 | tf_op jit(solution)/shard_map/ppermute | solution.py:451
  20.2 0.7 %back_inner.3 = (bf16[3,4,36,32,128]{4,3,2,1,0:T(8,128)(2,1)S(1)}, f32[4,32,32,128]{3,2,1,0:T(8,128)S(1)}) custom-call(bf16[4,32,32,128]{3,2,1,0:T(8,128)(2,1)S(1)} %get-tuple-element.37.u_ref, bf16[1152,256]{1,0:T(8,128)(2,1)S(1)} %get-tuple-element.36.w_ref, ...), custom_call_target="tpu_custom_call", output_to_operand_aliasing={{0}: (3, {}), {1}: (4, {})} | custom-call | flops 335544320 | bytes 2097152 | tf_op jit(solution)/shard_map/back_inner/pallas_call | solution.py:360
  21.0 0.9 %collective-permute-done.4 = f32[16,128]{1,0:T(8,128)S(1)} collective-permute-done((f32[16,128]{1,0:T(8,128)S(1)}, f32[16,128]{1,0:T(8,128)S(1)}, u32[]{:S(2)}, u32[]{:S(2)}) %collective-permute-start.4) | collective-permute-done | bytes 8224 | tf_op jit(solution)/shard_map/ppermute | solution.py:451
  21.9 3.0 %collective-permute-start.5 = (f32[16,128]{1,0:T(8,128)S(1)}, f32[16,128]{1,0:T(8,128)S(1)}, u32[]{:S(2)}, u32[]{:S(2)}) collective-permute-start(f32[16,128]{1,0:T(8,128)S(1)} %add.24.mine_ref), channel_id=1, source_target_pairs={{0,8},{1,9},{2,10},{3,11},{4,12},{5,13},{6,14},{7,15},{8,0},{9,1},... | collective-permute-start | bytes 24584 | tf_op jit(solution)/shard_map/ppermute | solution.py:451
  24.9 0.0 collective-permute-done.6.other_ref
  24.9 1.4 %back_outer.1 = (bf16[3,4,36,32,128]{4,3,2,1,0:T(8,128)(2,1)S(1)}, f32[4,32,32,128]{3,2,1,0:T(8,128)S(1)}) custom-call(bf16[6,2,32,128]{3,2,1,0:T(8,128)(2,1)S(1)} %collective-permute-done.2.mate_ref, bf16[5,2,32,128]{3,2,1,0:T(8,128)(2,1)S(1)} %collective-permute-done.6.other_ref, ...), custom_call_target="tpu_custom_call", output_to_operand_aliasing={{0}: (5, {}), {1}: (6, {})} | custom-call | flops 536870912 | bytes 2097152 | tf_op jit(solution)/shard_map/back_outer/pallas_call | solution.py:386
  26.3 0.2 collective-permute-done.5.theirs_ref
  26.5 1.6 %scale.1 = f32[4,32,32,128]{3,2,1,0:T(8,128)} custom-call(f32[3,128]{1,0:T(4,128)S(1)} %get-tuple-element.24.small_ref, f32[16,128]{1,0:T(8,128)S(1)} %add.24.mine_ref, f32[16,128]{1,0:T(8,128)S(1)} %collective-permute-done.5.theirs_ref, f32[4,32,32,128]{3,2,1,0:T(8,128)S(1)} %get-tuple-element.42.v_ref), custom_call_target="tpu_custom_call" | custom-call | tf_op jit(solution)/shard_map/scale/pallas_call | solution.py:421
  (4 shorter events, 0.0 us)
Async XLA Ops:
  1.1 5.1 %collective-permute-start = (bf16[5,2,32,128]{3,2,1,0:T(8,128)(2,1)S(1)}, bf16[5,2,32,128]{3,2,1,0:T(8,128)(2,1)S(1)}, u32[]{:S(2)}, u32[]{:S(2)}) collective-permute-start(bf16[5,2,32,128]{3,2,1,0:T(8,128)(2,1)S(1)} %get-tuple-element.25), channel_id=1, source_target_pairs={{0,1},{1,0},{2,3},{3,2},{4,5},{5,4},{6,7},{7,6},{8,9},{9,8},{10,11... | collective-permute-start | bytes 245768 | tf_op jit(solution)/shard_map/ppermute | solution.py:90
  1.6 4.6 %collective-permute-start.1 = (bf16[5,2,32,128]{3,2,1,0:T(8,128)(2,1)S(1)}, bf16[5,2,32,128]{3,2,1,0:T(8,128)(2,1)S(1)}, u32[]{:S(2)}, u32[]{:S(2)}) collective-permute-start(bf16[5,2,32,128]{3,2,1,0:T(8,128)(2,1)S(1)} %get-tuple-element.26), channel_id=1, source_target_pairs={{1,2},{2,1},{3,4},{4,3},{5,6},{6,5},{7,8},{8,7},{9,10},{10,9},{11,... | collective-permute-start | bytes 245768 | tf_op jit(solution)/shard_map/ppermute | solution.py:90
  7.4 4.9 %collective-permute-start.2 = (bf16[6,2,32,128]{3,2,1,0:T(8,128)(2,1)S(1)}, bf16[6,2,32,128]{3,2,1,0:T(8,128)(2,1)S(1)}, u32[]{:S(2)}, u32[]{:S(2)}) collective-permute-start(bf16[6,2,32,128]{3,2,1,0:T(8,128)(2,1)S(1)} %get-tuple-element.34), channel_id=1, source_target_pairs={{0,1},{1,0},{2,3},{3,2},{4,5},{5,4},{6,7},{7,6},{8,9},{9,8},{10,11... | collective-permute-start | bytes 294920 | tf_op jit(solution)/shard_map/ppermute | solution.py:90
  11.3 13.6 %collective-permute-start.6 = (bf16[5,2,32,128]{3,2,1,0:T(8,128)(2,1)S(1)}, bf16[5,2,32,128]{3,2,1,0:T(8,128)(2,1)S(1)}, u32[]{:S(2)}, u32[]{:S(2)}) collective-permute-start(bf16[5,2,32,128]{3,2,1,0:T(8,128)(2,1)S(1)} %get-tuple-element.35), channel_id=1, source_target_pairs={{1,2},{2,1},{3,4},{4,3},{5,6},{6,5},{7,8},{8,7},{9,10},{10,9},{11,... | collective-permute-start | bytes 245768 | tf_op jit(solution)/shard_map/ppermute | solution.py:90
  12.3 5.1 %collective-permute-start.3 = (f32[16,128]{1,0:T(8,128)S(1)}, f32[16,128]{1,0:T(8,128)S(1)}, u32[]{:S(2)}, u32[]{:S(2)}) collective-permute-start(f32[16,128]{1,0:T(8,128)S(1)} %fusion.2), channel_id=1, source_target_pairs={{0,2},{1,3},{2,0},{3,1},{4,6},{5,7},{6,4},{7,5},{8,10},{9,11},{10,... | collective-permute-start | bytes 24584 | tf_op jit(solution)/shard_map/ppermute | solution.py:451
  17.4 4.5 %collective-permute-start.4 = (f32[16,128]{1,0:T(8,128)S(1)}, f32[16,128]{1,0:T(8,128)S(1)}, u32[]{:S(2)}, u32[]{:S(2)}) collective-permute-start(f32[16,128]{1,0:T(8,128)S(1)} %add.23), channel_id=1, source_target_pairs={{0,4},{1,5},{2,6},{3,7},{4,0},{5,1},{6,2},{7,3},{8,12},{9,13},{10,... | collective-permute-start | bytes 24584 | tf_op jit(solution)/shard_map/ppermute | solution.py:451
  21.9 4.7 %collective-permute-start.5 = (f32[16,128]{1,0:T(8,128)S(1)}, f32[16,128]{1,0:T(8,128)S(1)}, u32[]{:S(2)}, u32[]{:S(2)}) collective-permute-start(f32[16,128]{1,0:T(8,128)S(1)} %add.24.mine_ref), channel_id=1, source_target_pairs={{0,8},{1,9},{2,10},{3,11},{4,12},{5,13},{6,14},{7,15},{8,0},{9,1},... | collective-permute-start | bytes 24584 | tf_op jit(solution)/shard_map/ppermute | solution.py:451

commit v4 on v3

--- a/solution.py
+++ b/solution.py
@@ -12,6 +12,7 @@
 BF = jnp.bfloat16
 F32 = jnp.float32
 VMEM = pl.BlockSpec(memory_space=pltpu.VMEM)
+SMEM = pl.BlockSpec(memory_space=pltpu.SMEM)
 HBM = pl.BlockSpec(memory_space=pltpu.HBM)
 KEPT = 0.90625
 REACH = (4, 3, 2)
@@ -34,11 +35,20 @@
     per = s // D
     parity = my_index() % 2
 
-    def put(ref, rows, columns, at_end):
-        ref[0:t] = rows[...]
-        first = columns.shape[1] - D if at_end else 0
+    def put(ref, rows, columns, below):
+        far, near = (0, t - 1) if below else (t - 1, 0)
+        for i in range(t):
+            if i != far:
+                ref[i] = rows[i]
+        first = columns.shape[1] - D if below else 0
+        shared = range(s - D, s) if below else range(D)
         for i in range(s):
-            ref[t, i // per, pl.ds((i % per) * D, D), :] = columns[i, first : first + D, :]
+            at = pl.ds((i % per) * D, D)
+            if i in shared:
+                edge = s - D if below else 0
+                ref[far, i // per, at, :] = rows[far, i - shared[0], edge : edge + D, :]
+            else:
+                ref[far, i // per, at, :] = columns[i, first : first + D, :]
 
     @pl.when(parity == 0)
     def _():
@@ -69,7 +79,7 @@
 
 def make_strips(x):
     t, s, _, c = x.shape
-    out = jax.ShapeDtypeStruct((t + 1, D, s, c), BF)
+    out = jax.ShapeDtypeStruct((t, D, s, c), BF)
     return pl.pallas_call(
         strips_kernel,
         out_shape=(out, out),
@@ -87,7 +97,10 @@
     size = lax.axis_size(GROUP)
     mates = [(i, i ^ 1) for i in range(size) if i ^ 1 < size]
     others = [(i, j) for i in range(size) for j in [(i + 1 ^ 1) - 1] if 0 <= j < size]
-    return lax.ppermute(mate, GROUP, mates), lax.ppermute(other, GROUP, others)
+    return (
+        None if mate is None else lax.ppermute(mate, GROUP, mates),
+        None if other is None else lax.ppermute(other, GROUP, others),
+    )
 
 
 def regions(t, s):
@@ -122,31 +135,48 @@
             win_ref[2, i, D : D + s, s - D :] = src_ref[i + 1, :, :D] * there
 
 
-def fill_border(beside_ref, mask_ref, mate_ref, other_ref, win_ref, both_ref):
+def fill_border(beside_ref, mask_ref, mate_ref, other_ref, win_ref, both_ref, corner_ref):
     t, s, c = win_ref.shape[1], win_ref.shape[3], win_ref.shape[4]
     parity = my_index() % 2
-    both_ref[0] = mate_ref[0 : t + 1]
-    both_ref[1] = other_ref[0 : t + 1]
+    both_ref[0] = mate_ref[0:t]
+    both_ref[1] = other_ref[0:t]
     prev_ref, next_ref = both_ref.at[1 - parity], both_ref.at[parity]
-
-    def low(i):
-        return prev_ref[t + i] if i < 0 else win_ref[1, i, s : s + D]
-
-    def high(i):
-        return next_ref[i - t] if i >= t else win_ref[1, i, D : 2 * D]
-
     per = s // D
+    corner_ref[...] = jnp.zeros(corner_ref.shape, BF)
+    for r in range(D):
+        at = pl.ds((per - D + r) * D, D)
+        corner_ref[0, r, 16 - D :] = prev_ref[0, D - 1, at, :]
+        corner_ref[1, r, :D] = next_ref[t - 1, 0, pl.ds(r * D, D), :]
+
+    def low(i, columns):
+        if i == -t:
+            return corner_ref[0]
+        return prev_ref[t + i, :, columns] if i < 0 else win_ref[1, i, s : s + D, columns]
+
+    def high(i, columns):
+        if i == 2 * t - 1:
+            return corner_ref[1]
+        return next_ref[i - t, :, columns] if i >= t else win_ref[1, i, D : 2 * D, columns]
+
     has_left = beside_ref[0, 0, 0:D]
     has_right = beside_ref[t - 1, 1, 0:D]
     for r in range(s):
         at = pl.ds((r % per) * D, D)
-        win_ref[0, 0, D + r, :D] = prev_ref[t, r // per, at, :] * has_left
-        win_ref[2, t - 1, D + r, s - D :] = next_ref[t, r // per, at, :] * has_right
+        if r < s - D:
+            pixels = prev_ref[0, r // per, at, :]
+        else:
+            pixels = prev_ref[t - 1, r - s + D, s - D :, :]
+        win_ref[0, 0, D + r, :D] = pixels * has_left
+        if r >= D:
+            pixels = next_ref[t - 1, r // per, at, :]
+        else:
+            pixels = next_ref[0, r, :D, :]
+        win_ref[2, t - 1, D + r, s - D :] = pixels * has_right
 
     def pick(strip, i, side, kind, columns):
         total = None
         for step in range(1, REACH[kind] + 1):
-            rows = strip(i - step if side == 0 else i + step)[:, columns]
+            rows = strip(i - step if side == 0 else i + step, columns)
             n = rows.shape[1] // 16
             mask = mask_ref[i, side, sum(REACH[:kind]) + step - 1]
             term = rows.reshape(D, n, 16, c) * mask.reshape(1, 1, 16, c)
@@ -212,14 +242,14 @@
 
 
 def inner_kernel(
-    x_hbm, w_hbm, near_hbm, bias_hbm, head_hbm, label_hbm,
-    u_ref, win_ref, first_ref, second_ref, sum_ref, small_ref, beside_ref, mask_ref,
-    x_ref, w_ref, bias_ref, head_ref, near_ref, label_ref, sems,
+    x_hbm, w_hbm, near_hbm, bias_hbm, head_hbm,
+    u_ref, win_ref, first_ref, sum_ref, small_ref, beside_ref, mask_ref,
+    x_ref, w_ref, bias_ref, head_ref, near_ref, sems,
 ):
     t, s, _, c = x_ref.shape
     moves = [
         (x_hbm, x_ref), (w_hbm, w_ref), (head_hbm, head_ref), (bias_hbm, bias_ref),
-        (near_hbm, near_ref), (label_hbm, label_ref),
+        (near_hbm, near_ref),
     ]
     copies = [pltpu.make_async_copy(a, b, sems.at[i]) for i, (a, b) in enumerate(moves)]
     for copy in copies:
@@ -228,7 +258,6 @@
         copy.wait()
     small_ref[0:1] = head_ref[...]
     small_ref[1:2] = bias_ref[...]
-    small_ref[2:3] = jnp.full((1, c), label_ref[0], jnp.int32).astype(F32)
     start = my_index() * t
 
     def flag(yes):
@@ -246,26 +275,19 @@
                     mask_ref[i, side, at] = flag((near_ref[i, k] == there) & (there >= 0))
                     at += 1
     blank = jnp.zeros((c, c), BF)
-    head = head_ref[...] * (1.0 / KEPT)
     for b in range(3):
         for m in range(4):
             rows = pl.ds((m * 3 + b) * c, c)
             for half in range(2):
                 a = m - half
                 first_ref[rows, pl.ds(half * c, c)] = w_ref[a, b] if 0 <= a < 3 else blank
-        for a in range(3):
-            rows = pl.ds((a * 3 + b) * c, c)
-            turned = (w_ref[2 - a, 2 - b].astype(F32) * head).T
-            upper = turned.astype(BF)
-            second_ref[rows, 0:c] = upper
-            second_ref[rows, c : 2 * c] = (turned - upper.astype(F32)).astype(BF)
     copies[0].wait()
     fill_own(range(t), x_ref, win_ref)
     fill_beside(range(t), beside_ref, x_ref, win_ref)
     sum_ref[...] = first_part(regions(t, s)[0], win_ref, first_ref, bias_ref[...], u_ref)
 
 
-def inner_stage(x, w, near, bias, head, label):
+def inner_stage(x, w, near, bias, head):
     t, s, _, c = x.shape
     return pl.pallas_call(
         inner_kernel,
@@ -273,38 +295,36 @@
             jax.ShapeDtypeStruct(x.shape, BF),
             jax.ShapeDtypeStruct((3, t, s + 2 * D, s, c), BF),
             jax.ShapeDtypeStruct((12 * c, 2 * c), BF),
-            jax.ShapeDtypeStruct((9 * c, 2 * c), BF),
             jax.ShapeDtypeStruct((16, c), F32),
-            jax.ShapeDtypeStruct((3, c), F32),
+            jax.ShapeDtypeStruct((2, c), F32),
             jax.ShapeDtypeStruct((t, 2, 16, c), BF),
             jax.ShapeDtypeStruct((t, 2, sum(REACH), 16, c), BF),
         ),
-        in_specs=[HBM] * 6,
-        out_specs=(VMEM,) * 8,
+        in_specs=[HBM] * 5,
+        out_specs=(VMEM,) * 7,
         scratch_shapes=[
             pltpu.VMEM(x.shape, BF),
             pltpu.VMEM(w.shape, BF),
             pltpu.VMEM((1, c), F32),
             pltpu.VMEM((1, c), F32),
             pltpu.SMEM(near.shape, jnp.int32),
-            pltpu.SMEM((1,), jnp.int32),
-            pltpu.SemaphoreType.DMA((6,)),
+            pltpu.SemaphoreType.DMA((5,)),
         ],
         compiler_params=params(),
         cost_estimate=pl.CostEstimate(
             flops=9 * t * s * s * c * c, bytes_accessed=6 << 20, transcendentals=t * s * s * c // 2
         ),
         name="inner",
-    )(*in_hbm(x, w, near, bias, head), label)
+    )(*in_hbm(x, w, near, bias, head))
 
 
 def outer_kernel(
     mate_ref, other_ref, w_ref, small_ref, beside_ref, mask_ref, part_ref, u_in, win_in,
-    u_ref, win_ref, to_mate_ref, to_other_ref, sum_ref, both_ref,
+    u_ref, win_ref, to_mate_ref, to_other_ref, sum_ref, both_ref, corner_ref,
 ):
     del u_in, win_in
     t, s, _, c = u_ref.shape
-    fill_border(beside_ref, mask_ref, mate_ref, other_ref, win_ref, both_ref)
+    fill_border(beside_ref, mask_ref, mate_ref, other_ref, win_ref, both_ref, corner_ref)
     total = part_ref[...] + first_part(
         regions(t, s)[1], win_ref, w_ref, small_ref[1:2], u_ref
     )
@@ -317,10 +337,10 @@
     upper = total.astype(BF)
     rest = total - upper.astype(F32)
     middle = rest.astype(BF)
-    to_mate_ref[t + 1, 0, 0:16] = upper
-    to_mate_ref[t + 1, 0, 16:32] = middle
-    to_mate_ref[t + 1, 1, 0:16] = (rest - middle.astype(F32)).astype(BF)
-    to_mate_ref[t + 1, 1, 16:32] = jnp.zeros((16, c), BF)
+    to_mate_ref[t, 0, 0:16] = upper
+    to_mate_ref[t, 0, 16:32] = middle
+    to_mate_ref[t, 1, 0:16] = (rest - middle.astype(F32)).astype(BF)
+    to_mate_ref[t, 1, 16:32] = jnp.zeros((16, c), BF)
 
 
 def outer_stage(mate, other, w, small, beside, mask, part, u, win):
@@ -330,14 +350,14 @@
         out_shape=(
             jax.ShapeDtypeStruct(u.shape, BF),
             jax.ShapeDtypeStruct(win.shape, BF),
-            jax.ShapeDtypeStruct((t + 2, D, s, c), BF),
             jax.ShapeDtypeStruct((t + 1, D, s, c), BF),
+            jax.ShapeDtypeStruct((t, D, s, c), BF),
             jax.ShapeDtypeStruct((16, c), F32),
         ),
         in_specs=[VMEM] * 9,
         out_specs=(VMEM,) * 5,
         input_output_aliases={7: 0, 8: 1},
-        scratch_shapes=[pltpu.VMEM((2, t + 1, D, s, c), BF)],
+        scratch_shapes=[pltpu.VMEM((2, t, D, s, c), BF), pltpu.VMEM((2, D, 16, c), BF)],
         compiler_params=params(),
         cost_estimate=pl.CostEstimate(
             flops=9 * t * s * s * c * c, bytes_accessed=4 << 20, transcendentals=t * s * s * c // 2
@@ -346,8 +366,20 @@
     )(mate, other, w, small, beside, mask, part, u, win)
 
 
-def back_inner_kernel(tiles, u_ref, w_ref, beside_ref, *refs):
-    win_ref, v_ref = refs[-2:]
+def turn(first_ref, small_ref, second_ref):
+    c = first_ref.shape[1] // 2
+    head = small_ref[0:1] * (1.0 / KEPT)
+    for a in range(3):
+        for b in range(3):
+            rows = pl.ds((a * 3 + b) * c, c)
+            weight = first_ref[pl.ds(((2 - a) * 3 + 2 - b) * c, c), 0:c]
+            turned = (weight.astype(F32) * head).T
+            upper = turned.astype(BF)
+            second_ref[rows, 0:c] = upper
+            second_ref[rows, c : 2 * c] = (turned - upper.astype(F32)).astype(BF)
+
+
+def back_tiles(tiles, u_ref, w_ref, beside_ref, win_ref, v_ref):
     t, s = u_ref.shape[:2]
     fill_own(tiles, u_ref, win_ref)
     fill_beside(tiles, beside_ref, u_ref, win_ref)
@@ -355,29 +387,55 @@
     second_part(places, win_ref, w_ref, v_ref)
 
 
-def back_inner(tiles, u, w, beside, held=()):
+def back_inner_kernel(
+    u_ref, first_ref, small_ref, beside_ref, label_ref, win_ref, v_ref, w_ref, row_ref
+):
+    row_ref[...] = jnp.full(row_ref.shape, label_ref[0], jnp.int32).astype(F32)
+    turn(first_ref, small_ref, w_ref)
+    back_tiles(range(u_ref.shape[0]), u_ref, w_ref, beside_ref, win_ref, v_ref)
+
+
+def back_inner(u, first, small, beside, label):
     t, s, _, c = u.shape
     return pl.pallas_call(
-        functools.partial(back_inner_kernel, tiles),
+        back_inner_kernel,
         out_shape=(
             jax.ShapeDtypeStruct((3, t, s + 2 * D, s, c), BF),
             jax.ShapeDtypeStruct(u.shape, F32),
-        ),
-        in_specs=[VMEM] * (3 + len(held)),
-        out_specs=(VMEM, VMEM),
-        input_output_aliases={3: 0, 4: 1} if held else {},
+            jax.ShapeDtypeStruct((9 * c, 2 * c), BF),
+            jax.ShapeDtypeStruct((8, c), F32),
+        ),
+        in_specs=[VMEM] * 4 + [SMEM],
+        out_specs=(VMEM,) * 4,
         compiler_params=params(),
         cost_estimate=pl.CostEstimate(
-            flops=5 * t * s * s * c * c, bytes_accessed=2 << 20, transcendentals=0
+            flops=16 * t * s * s * c * c, bytes_accessed=8 << 20, transcendentals=0
         ),
         name="back_inner",
-    )(u, w, beside, *held)
-
-
-def back_outer_kernel(mate_ref, other_ref, w_ref, beside_ref, mask_ref, win_in, v_in, win_ref, v_ref, both_ref):
+    )(u, first, small, beside, label)
+
+
+def gate_kernel(strip_ref, sum_ref, out_ref):
+    del sum_ref
+    out_ref[...] = strip_ref[...]
+
+
+def gate(strip, total):
+    return pl.pallas_call(
+        gate_kernel,
+        out_shape=jax.ShapeDtypeStruct(strip.shape, strip.dtype),
+        in_specs=[VMEM, VMEM],
+        out_specs=VMEM,
+        compiler_params=params(),
+        cost_estimate=pl.CostEstimate(flops=1 << 31, bytes_accessed=1 << 20, transcendentals=0),
+        name="gate",
+    )(strip, total)
+
+
+def back_outer_kernel(mate_ref, other_ref, w_ref, beside_ref, mask_ref, win_in, v_in, win_ref, v_ref, both_ref, corner_ref):
     del win_in, v_in
     t, s = v_ref.shape[:2]
-    fill_border(beside_ref, mask_ref, mate_ref, other_ref, win_ref, both_ref)
+    fill_border(beside_ref, mask_ref, mate_ref, other_ref, win_ref, both_ref, corner_ref)
     second_part(regions(t, s)[1], win_ref, w_ref, v_ref)
 
 
@@ -392,7 +450,7 @@
         in_specs=[VMEM] * 7,
         out_specs=(VMEM, VMEM),
         input_output_aliases={5: 0, 6: 1},
-        scratch_shapes=[pltpu.VMEM((2, t + 1, D, s, c), BF)],
+        scratch_shapes=[pltpu.VMEM((2, t, D, s, c), BF), pltpu.VMEM((2, D, 16, c), BF)],
         compiler_params=params(),
         cost_estimate=pl.CostEstimate(
             flops=8 * t * s * s * c * c, bytes_accessed=2 << 20, transcendentals=0
@@ -401,9 +459,9 @@
     )(mate, other, w, beside, mask, win, v)[1]
 
 
-def scale_kernel(count, small_ref, mine_ref, theirs_ref, v_ref, o_ref, stage_ref, sems):
+def scale_kernel(count, label_ref, mine_ref, theirs_ref, v_ref, o_ref, stage_ref, sems):
     score = jnp.sum(mine_ref[...] + theirs_ref[...], axis=(0, 1), keepdims=True) / count
-    slope = jax.nn.sigmoid(score) - small_ref[2:3, 0:1] / 100.0
+    slope = jax.nn.sigmoid(score) - label_ref[0:1, 0:1] / 100.0
     t, s = v_ref.shape[:2]
     copies = []
     for i in range(t):
@@ -417,7 +475,7 @@
         copy.wait()
 
 
-def scale(small, mine, theirs, v, count):
+def scale(label, mine, theirs, v, count):
     return pl.pallas_call(
         functools.partial(scale_kernel, count),
         out_shape=jax.ShapeDtypeStruct(v.shape, F32),
@@ -426,34 +484,35 @@
         scratch_shapes=[pltpu.VMEM(v.shape, F32), pltpu.SemaphoreType.DMA((v.shape[0], 2))],
         compiler_params=params(),
         name="scale",
-    )(small, mine, theirs, v)
+    )(label, mine, theirs, v)
 
 
 def body(tissue_tiles, neighbours, conv_weight, conv_bias, head_weight, slide_label):
     t, s, _, c = tissue_tiles.shape
     size = lax.axis_size(GROUP)
     mate, other = swap(*make_strips(tissue_tiles))
-    u, win, w_first, w_second, part, small, beside, mask = inner_stage(
-        tissue_tiles, conv_weight, neighbours, conv_bias.reshape(1, c), head_weight.reshape(1, c),
-        slide_label,
+    u, win, w_first, part, small, beside, mask = inner_stage(
+        tissue_tiles, conv_weight, neighbours, conv_bias.reshape(1, c), head_weight.reshape(1, c)
     )
     u, _, mate, other, mine = outer_stage(
         mate, other, w_first, small, beside, mask, part, u, win
     )
-    mate, other = swap(mate, other)
-    got = mate[t + 1].astype(F32)
+    mate, _ = swap(mate, None)
+    got = mate[t].astype(F32)
     theirs = got[0, 0:16] + got[0, 16:32] + got[1, 0:16]
     if size & (size - 1):
         mine, theirs = lax.psum(mine, GROUP), jnp.zeros_like(mine)
     step = 2
     while step < size and not size & (size - 1):
         mine = mine + theirs
+        if step == 2:
+            other = gate(other, mine)
         theirs = lax.ppermute(mine, GROUP, [(i, i ^ step) for i in range(size)])
         step *= 2
-    held = back_inner(tuple(range(1, t - 1)), u, w_second, beside)
-    held = back_inner((0, t - 1), u, w_second, beside, held)
-    v = back_outer(mate, other, w_second, beside, mask, *held)
-    return scale(small, mine, theirs, v, float(t * size * s * s * c))
+    _, other = swap(None, other)
+    win, v, w_second, label = back_inner(u, w_first, small, beside, slide_label)
+    v = back_outer(mate, other, w_second, beside, mask, win, v)
+    return scale(label, mine, theirs, v, float(t * size * s * s * c))
 
 
 def solution(mesh):

time: 28.3 us -> 25.5 us (0.901)
  starting transfers between devices: 14.4 us -> 12.2 us
  waiting for transfers between devices: 2.52 us -> 2.01 us
    ppermute x3, starting transfers between devices: 8.62 us -> 6.42 us  [body(): theirs = lax.ppermute(mine, GROUP, [(i, i ^ step) for i in range(size)])]
    ppermute x3, waiting for transfers between devices: 2.23 us -> 1.73 us  [body(): theirs = lax.ppermute(mine, GROUP, [(i, i ^ step) for i in range(size)])]
  transfers between devices with their start and end apart: 7 -> 7, of which waited for: 4 -> 4; matrix products, arithmetic and copies ran while one was open for 0% -> 0% of each run, Pallas kernels for 24% -> 26%
where the time goes in v4:
time: 25.5 us; the launch traced here: 25.3 us
  starting transfers between devices  12.2 us (48%)
  Pallas kernels  10.4 us (41%)
  waiting for transfers between devices  2.01 us (8%)
  between operations  0.72 us (3%)
    ppermute x3, starting transfers between devices, body(): theirs = lax.ppermute(mine, GROUP, [(i, i ^ step) for i in range(size)])  6.42 us
    ppermute x2, starting transfers between devices, swap(): lax.ppermute(mate, GROUP, mates)  4.49 us
    pallas_call x1, Pallas kernels, inner_stage(): pl.pallas_call(inner_kernel, out_shape=(jax.ShapeDtypeStruct(x.shape, BF)...  3.05 us
    pallas_call x1, Pallas kernels, back_inner(): pl.pallas_call(back_inner_kernel, out_shape=(jax.ShapeDtypeStruct((3, t,...  2.12 us
    ppermute x3, waiting for transfers between devices, body(): theirs = lax.ppermute(mine, GROUP, [(i, i ^ step) for i in range(size)])  1.73 us
    pallas_call x1, Pallas kernels, scale(): pl.pallas_call(functools.partial(scale_kernel, count), out_shape=jax.Shap...  1.55 us
    pallas_call x1, Pallas kernels, back_outer(): pl.pallas_call(back_outer_kernel, out_shape=(jax.ShapeDtypeStruct(win.sha...  1.42 us
    ppermute x2, starting transfers between devices, swap(): lax.ppermute(other, GROUP, others)  1.31 us
  transfers between devices with their start and end apart: 7, of which 4 were waited for; matrix products, arithmetic and copies ran while one was open for 0% of the time, Pallas kernels for 26%

profile of v4, /device:TPU:0, one launch (start us, length us, event | category | flops | bytes accessed | tf_op | source)
XLA Modules:
  0.0 25.3 jit_solution(11939936529767758905)
XLA Ops:
  0.0 1.1 %strips.1 = (bf16[4,2,32,128]{3,2,1,0:T(8,128)(2,1)S(1)}, bf16[4,2,32,128]{3,2,1,0:T(8,128)(2,1)S(1)}) custom-call(bf16[4,32,32,128]{3,2,1,0:T(8,128)(2,1)} %x_hbm.1), custom_call_target="tpu_custom_call" | custom-call | tf_op jit(solution)/shard_map/strips/pallas_call | solution.py:83
  1.1 0.6 %collective-permute-start = (bf16[4,2,32,128]{3,2,1,0:T(8,128)(2,1)S(1)}, bf16[4,2,32,128]{3,2,1,0:T(8,128)(2,1)S(1)}, u32[]{:S(2)}, u32[]{:S(2)}) collective-permute-start(bf16[4,2,32,128]{3,2,1,0:T(8,128)(2,1)S(1)} %get-tuple-element.23), channel_id=1, source_target_pairs={{0,1},{1,0},{2,3},{3,2},{4,5},{5,4},{6,7},{7,6},{8,9},{9,8},{10,11... | collective-permute-start | bytes 196616 | tf_op jit(solution)/shard_map/ppermute | solution.py:101
  1.6 0.7 %collective-permute-start.1 = (bf16[4,2,32,128]{3,2,1,0:T(8,128)(2,1)S(1)}, bf16[4,2,32,128]{3,2,1,0:T(8,128)(2,1)S(1)}, u32[]{:S(2)}, u32[]{:S(2)}) collective-permute-start(bf16[4,2,32,128]{3,2,1,0:T(8,128)(2,1)S(1)} %get-tuple-element.24), channel_id=1, source_target_pairs={{1,2},{2,1},{3,4},{4,3},{5,6},{6,5},{7,8},{8,7},{9,10},{10,9},{11,... | collective-permute-start | bytes 196616 | tf_op jit(solution)/shard_map/ppermute | solution.py:102
  2.3 3.1 %inner.1 = (bf16[4,32,32,128]{3,2,1,0:T(8,128)(2,1)S(1)}, bf16[3,4,36,32,128]{4,3,2,1,0:T(8,128)(2,1)S(1)}, bf16[1536,256]{1,0:T(8,128)(2,1)S(1)}, f32[16,128]{1...) custom-call(bf16[4,32,32,128]{3,2,1,0:T(8,128)(2,1)} %x_hbm.1, ...), custom_call_target="tpu_custom_call" | custom-call | flops 603979776 | bytes 6291456 | tf_op jit(solution)/shard_map/inner/pallas_call | solution.py:292
  5.4 0.0 collective-permute-done.mate_ref
  5.4 0.0 collective-permute-done.1.other_ref
  5.4 1.1 %outer.1 = (bf16[4,32,32,128]{3,2,1,0:T(8,128)(2,1)S(1)}, bf16[3,4,36,32,128]{4,3,2,1,0:T(8,128)(2,1)S(1)}, bf16[5,2,32,128]{3,2,1,0:T(8,128)(2,1)S(1)}, bf16[4,...) custom-call(bf16[4,2,32,128]{3,2,1,0:T(8,128)(2,1)S(1)} %collective-permute-done.mate_ref, ...), custom_call_target="tpu_custom_call", output_to_operand_aliasing={{0}: (7, {}), {1}: (8, {})} | custom-call | flops 603979776 | bytes 4194304 | tf_op jit(solution)/shard_map/outer/pallas_call | solution.py:348
  6.5 3.9 %collective-permute-start.2 = (bf16[5,2,32,128]{3,2,1,0:T(8,128)(2,1)S(1)}, bf16[5,2,32,128]{3,2,1,0:T(8,128)(2,1)S(1)}, u32[]{:S(2)}, u32[]{:S(2)}) collective-permute-start(bf16[5,2,32,128]{3,2,1,0:T(8,128)(2,1)S(1)} %get-tuple-element.35), channel_id=1, source_target_pairs={{0,1},{1,0},{2,3},{3,2},{4,5},{5,4},{6,7},{7,6},{8,9},{9,8},{10,11... | collective-permute-start | bytes 245768 | tf_op jit(solution)/shard_map/ppermute | solution.py:101
  11.1 0.3 %collective-permute-done.2.mate_ref = bf16[5,2,32,128]{3,2,1,0:T(8,128)(2,1)S(1)} collective-permute-done((bf16[5,2,32,128]{3,2,1,0:T(8,128)(2,1)S(1)}, bf16[5,2,32,128]{3,2,1,0:T(8,128)(2,1)S(1)}, u32[]{:S(2)}, u32[]{:S(2)}) %collective-permute-start.2) | collective-permute-done | bytes 81952 | tf_op jit(solution)/shard_map/ppermute | solution.py:101
  11.4 1.9 %collective-permute-start.3 = (f32[16,128]{1,0:T(8,128)S(1)}, f32[16,128]{1,0:T(8,128)S(1)}, u32[]{:S(2)}, u32[]{:S(2)}) collective-permute-start(f32[16,128]{1,0:T(8,128)S(1)} %fusion.2.sum_ref), channel_id=1, source_target_pairs={{0,2},{1,3},{2,0},{3,1},{4,6},{5,7},{6,4},{7,5},{8,10},{9,11},{10,... | collective-permute-start | bytes 24584 | tf_op jit(solution)/shard_map/ppermute | solution.py:510
  13.3 0.7 %collective-permute-start.6 = (bf16[4,2,32,128]{3,2,1,0:T(8,128)(2,1)S(1)}, bf16[4,2,32,128]{3,2,1,0:T(8,128)(2,1)S(1)}, u32[]{:S(2)}, u32[]{:S(2)}) collective-permute-start(bf16[4,2,32,128]{3,2,1,0:T(8,128)(2,1)S(1)} %gate.1), channel_id=1, source_target_pairs={{1,2},{2,1},{3,4},{4,3},{5,6},{6,5},{7,8},{8,7},{9,10},{10,9},{11,... | collective-permute-start | bytes 196616 | tf_op jit(solution)/shard_map/ppermute | solution.py:102
  14.0 1.1 %collective-permute-done.3 = f32[16,128]{1,0:T(8,128)S(1)} collective-permute-done((f32[16,128]{1,0:T(8,128)S(1)}, f32[16,128]{1,0:T(8,128)S(1)}, u32[]{:S(2)}, u32[]{:S(2)}) %collective-permute-start.3) | collective-permute-done | bytes 8224 | tf_op jit(solution)/shard_map/ppermute | solution.py:510
  15.1 1.9 %collective-permute-start.4 = (f32[16,128]{1,0:T(8,128)S(1)}, f32[16,128]{1,0:T(8,128)S(1)}, u32[]{:S(2)}, u32[]{:S(2)}) collective-permute-start(f32[16,128]{1,0:T(8,128)S(1)} %add.23), channel_id=1, source_target_pairs={{0,4},{1,5},{2,6},{3,7},{4,0},{5,1},{6,2},{7,3},{8,12},{9,13},{10,... | collective-permute-start | bytes 24584 | tf_op jit(solution)/shard_map/ppermute | solution.py:510
  17.0 2.1 %back_inner.1 = (bf16[3,4,36,32,128]{4,3,2,1,0:T(8,128)(2,1)S(1)}, f32[4,32,32,128]{3,2,1,0:T(8,128)S(1)}, bf16[1152,256]{1,0:T(8,128)(2,1)S(1)}, f32[8,128]{1,0:T(8,128)S(1)}) custom-call(bf16[4,32,32,128]{3,2,1,0:T(8,128)(2,1)S(1)} %get-tuple-element.32.u_ref, bf16[1536,256]{1,0:T(8,128)(2,1)S(1)} %get-tuple-element.25.w_ref.first_ref, ...), custom_call_target="tpu_custom_call" | custom-call | flops 1073741824 | bytes 8388608 | tf_op jit(solution)/shard_map/back_inner/pallas_call | solution.py:400
  19.1 0.1 collective-permute-done.4
  19.2 2.6 %collective-permute-start.5 = (f32[16,128]{1,0:T(8,128)S(1)}, f32[16,128]{1,0:T(8,128)S(1)}, u32[]{:S(2)}, u32[]{:S(2)}) collective-permute-start(f32[16,128]{1,0:T(8,128)S(1)} %add.24.mine_ref), channel_id=1, source_target_pairs={{0,8},{1,9},{2,10},{3,11},{4,12},{5,13},{6,14},{7,15},{8,0},{9,1},... | collective-permute-start | bytes 24584 | tf_op jit(solution)/shard_map/ppermute | solution.py:510
  21.8 0.0 collective-permute-done.6.other_ref
  21.8 1.4 %back_outer.1 = (bf16[3,4,36,32,128]{4,3,2,1,0:T(8,128)(2,1)S(1)}, f32[4,32,32,128]{3,2,1,0:T(8,128)S(1)}) custom-call(bf16[5,2,32,128]{3,2,1,0:T(8,128)(2,1)S(1)} %collective-permute-done.2.mate_ref, bf16[4,2,32,128]{3,2,1,0:T(8,128)(2,1)S(1)} %collective-permute-done.6.other_ref, ...), custom_call_target="tpu_custom_call", output_to_operand_aliasing={{0}: (5, {}), {1}: (6, {})} | custom-call | flops 536870912 | bytes 2097152 | tf_op jit(solution)/shard_map/back_outer/pallas_call | solution.py:444
  23.2 0.5 %collective-permute-done.5.theirs_ref = f32[16,128]{1,0:T(8,128)S(1)} collective-permute-done((f32[16,128]{1,0:T(8,128)S(1)}, f32[16,128]{1,0:T(8,128)S(1)}, u32[]{:S(2)}, u32[]{:S(2)}) %collective-permute-start.5) | collective-permute-done | bytes 8224 | tf_op jit(solution)/shard_map/ppermute | solution.py:510
  23.8 1.6 %scale.1 = f32[4,32,32,128]{3,2,1,0:T(8,128)} custom-call(f32[8,128]{1,0:T(8,128)S(1)} %get-tuple-element.33.label_ref, f32[16,128]{1,0:T(8,128)S(1)} %add.24.mine_ref, f32[16,128]{1,0:T(8,128)S(1)} %collective-permute-done.5.theirs_ref, f32[4,32,32,128]{3,2,1,0:T(8,128)S(1)} %get-tuple-element.40.v_ref), custom_call_target="tpu_custom_call" | custom-call | tf_op jit(solution)/shard_map/scale/pallas_call | solution.py:479
  (5 shorter events, 0.0 us)
Async XLA Ops:
  1.1 4.3 %collective-permute-start = (bf16[4,2,32,128]{3,2,1,0:T(8,128)(2,1)S(1)}, bf16[4,2,32,128]{3,2,1,0:T(8,128)(2,1)S(1)}, u32[]{:S(2)}, u32[]{:S(2)}) collective-permute-start(bf16[4,2,32,128]{3,2,1,0:T(8,128)(2,1)S(1)} %get-tuple-element.23), channel_id=1, source_target_pairs={{0,1},{1,0},{2,3},{3,2},{4,5},{5,4},{6,7},{7,6},{8,9},{9,8},{10,11... | collective-permute-start | bytes 196616 | tf_op jit(solution)/shard_map/ppermute | solution.py:101
  1.6 3.7 %collective-permute-start.1 = (bf16[4,2,32,128]{3,2,1,0:T(8,128)(2,1)S(1)}, bf16[4,2,32,128]{3,2,1,0:T(8,128)(2,1)S(1)}, u32[]{:S(2)}, u32[]{:S(2)}) collective-permute-start(bf16[4,2,32,128]{3,2,1,0:T(8,128)(2,1)S(1)} %get-tuple-element.24), channel_id=1, source_target_pairs={{1,2},{2,1},{3,4},{4,3},{5,6},{6,5},{7,8},{8,7},{9,10},{10,9},{11,... | collective-permute-start | bytes 196616 | tf_op jit(solution)/shard_map/ppermute | solution.py:102
  6.5 4.9 %collective-permute-start.2 = (bf16[5,2,32,128]{3,2,1,0:T(8,128)(2,1)S(1)}, bf16[5,2,32,128]{3,2,1,0:T(8,128)(2,1)S(1)}, u32[]{:S(2)}, u32[]{:S(2)}) collective-permute-start(bf16[5,2,32,128]{3,2,1,0:T(8,128)(2,1)S(1)} %get-tuple-element.35), channel_id=1, source_target_pairs={{0,1},{1,0},{2,3},{3,2},{4,5},{5,4},{6,7},{7,6},{8,9},{9,8},{10,11... | collective-permute-start | bytes 245768 | tf_op jit(solution)/shard_map/ppermute | solution.py:101
  11.4 3.7 %collective-permute-start.3 = (f32[16,128]{1,0:T(8,128)S(1)}, f32[16,128]{1,0:T(8,128)S(1)}, u32[]{:S(2)}, u32[]{:S(2)}) collective-permute-start(f32[16,128]{1,0:T(8,128)S(1)} %fusion.2.sum_ref), channel_id=1, source_target_pairs={{0,2},{1,3},{2,0},{3,1},{4,6},{5,7},{6,4},{7,5},{8,10},{9,11},{10,... | collective-permute-start | bytes 24584 | tf_op jit(solution)/shard_map/ppermute | solution.py:510
  13.3 8.5 %collective-permute-start.6 = (bf16[4,2,32,128]{3,2,1,0:T(8,128)(2,1)S(1)}, bf16[4,2,32,128]{3,2,1,0:T(8,128)(2,1)S(1)}, u32[]{:S(2)}, u32[]{:S(2)}) collective-permute-start(bf16[4,2,32,128]{3,2,1,0:T(8,128)(2,1)S(1)} %gate.1), channel_id=1, source_target_pairs={{1,2},{2,1},{3,4},{4,3},{5,6},{6,5},{7,8},{8,7},{9,10},{10,9},{11,... | collective-permute-start | bytes 196616 | tf_op jit(solution)/shard_map/ppermute | solution.py:102
  15.1 4.1 %collective-permute-start.4 = (f32[16,128]{1,0:T(8,128)S(1)}, f32[16,128]{1,0:T(8,128)S(1)}, u32[]{:S(2)}, u32[]{:S(2)}) collective-permute-start(f32[16,128]{1,0:T(8,128)S(1)} %add.23), channel_id=1, source_target_pairs={{0,4},{1,5},{2,6},{3,7},{4,0},{5,1},{6,2},{7,3},{8,12},{9,13},{10,... | collective-permute-start | bytes 24584 | tf_op jit(solution)/shard_map/ppermute | solution.py:510
  19.2 4.6 %collective-permute-start.5 = (f32[16,128]{1,0:T(8,128)S(1)}, f32[16,128]{1,0:T(8,128)S(1)}, u32[]{:S(2)}, u32[]{:S(2)}) collective-permute-start(f32[16,128]{1,0:T(8,128)S(1)} %add.24.mine_ref), channel_id=1, source_target_pairs={{0,8},{1,9},{2,10},{3,11},{4,12},{5,13},{6,14},{7,15},{8,0},{9,1},... | collective-permute-start | bytes 24584 | tf_op jit(solution)/shard_map/ppermute | solution.py:510

commit v5 on v4

--- a/solution.py
+++ b/solution.py
@@ -89,6 +89,7 @@
         + [pltpu.VMEM((s, 16, c), BF)] * 2
         + [pltpu.SemaphoreType.DMA((4,))],
         compiler_params=params(),
+        cost_estimate=pl.CostEstimate(flops=1 << 32, bytes_accessed=8 << 20, transcendentals=0),
         name="strips",
     )(*in_hbm(x))
 
@@ -135,45 +136,37 @@
             win_ref[2, i, D : D + s, s - D :] = src_ref[i + 1, :, :D] * there
 
 
-def fill_border(beside_ref, mask_ref, mate_ref, other_ref, win_ref, both_ref, corner_ref):
+def fill_side(side, beside_ref, mask_ref, strip_ref, win_ref, corner_ref):
     t, s, c = win_ref.shape[1], win_ref.shape[3], win_ref.shape[4]
-    parity = my_index() % 2
-    both_ref[0] = mate_ref[0:t]
-    both_ref[1] = other_ref[0:t]
-    prev_ref, next_ref = both_ref.at[1 - parity], both_ref.at[parity]
     per = s // D
+    far, near = (0, t - 1) if side == 0 else (t - 1, 0)
+    shared = range(s - D, s) if side == 0 else range(D)
+    inside = slice(s - D, s) if side == 0 else slice(0, D)
     corner_ref[...] = jnp.zeros(corner_ref.shape, BF)
-    for r in range(D):
-        at = pl.ds((per - D + r) * D, D)
-        corner_ref[0, r, 16 - D :] = prev_ref[0, D - 1, at, :]
-        corner_ref[1, r, :D] = next_ref[t - 1, 0, pl.ds(r * D, D), :]
-
-    def low(i, columns):
-        if i == -t:
-            return corner_ref[0]
-        return prev_ref[t + i, :, columns] if i < 0 else win_ref[1, i, s : s + D, columns]
-
-    def high(i, columns):
-        if i == 2 * t - 1:
-            return corner_ref[1]
-        return next_ref[i - t, :, columns] if i >= t else win_ref[1, i, D : 2 * D, columns]
-
-    has_left = beside_ref[0, 0, 0:D]
-    has_right = beside_ref[t - 1, 1, 0:D]
+    there = beside_ref[0, 0, 0:D] if side == 0 else beside_ref[t - 1, 1, 0:D]
     for r in range(s):
         at = pl.ds((r % per) * D, D)
-        if r < s - D:
-            pixels = prev_ref[0, r // per, at, :]
+        pixels = strip_ref[far, r // per, at, :]
+        if r in shared:
+            edge = slice(16 - D, 16) if side == 0 else slice(0, D)
+            corner_ref[r - shared[0], edge] = pixels
+            pixels = strip_ref[near, r - shared[0], inside, :]
+        if side == 0:
+            win_ref[0, 0, D + r, :D] = pixels * there
         else:
-            pixels = prev_ref[t - 1, r - s + D, s - D :, :]
-        win_ref[0, 0, D + r, :D] = pixels * has_left
-        if r >= D:
-            pixels = next_ref[t - 1, r // per, at, :]
-        else:
-            pixels = next_ref[0, r, :D, :]
-        win_ref[2, t - 1, D + r, s - D :] = pixels * has_right
-
-    def pick(strip, i, side, kind, columns):
+            win_ref[2, t - 1, D + r, s - D :] = pixels * there
+
+    def strip(i, columns):
+        if i in (-t, 2 * t - 1):
+            return corner_ref[...]
+        if i < 0:
+            return strip_ref[t + i, :, columns]
+        if i >= t:
+            return strip_ref[i - t, :, columns]
+        row = s if side == 0 else D
+        return win_ref[1, i, row : row + D, columns]
+
+    def pick(i, kind, columns):
         total = None
         for step in range(1, REACH[kind] + 1):
             rows = strip(i - step if side == 0 else i + step, columns)
@@ -183,17 +176,32 @@
             total = term if total is None else total + term
         return total.reshape(D, n * 16, c)
 
+    row = 0 if side == 0 else D + s
     for i in range(t):
-        for side, strip, row in ((0, low, 0), (1, high, D + s)):
-            rows = slice(row, row + D)
-            middle = pick(strip, i, side, 1, slice(0, s))
-            left = pick(strip, i, side, 2 * side, slice(s - 16, s))
-            right = pick(strip, i, side, 2 - 2 * side, slice(0, 16))
-            win_ref[0, i, rows, D:] = middle[:, : s - D]
-            win_ref[0, i, rows, :D] = left[:, 16 - D :]
-            win_ref[1, i, rows] = middle
-            win_ref[2, i, rows, : s - D] = middle[:, D:]
-            win_ref[2, i, rows, s - D :] = right[:, :D]
+        rows = slice(row, row + D)
+        middle = pick(i, 1, slice(0, s))
+        left = pick(i, 2 * side, slice(s - 16, s))
+        right = pick(i, 2 - 2 * side, slice(0, 16))
+        win_ref[0, i, rows, D:] = middle[:, : s - D]
+        win_ref[0, i, rows, :D] = left[:, 16 - D :]
+        win_ref[1, i, rows] = middle
+        win_ref[2, i, rows, : s - D] = middle[:, D:]
+        win_ref[2, i, rows, s - D :] = right[:, :D]
+
+
+def side_regions(t, s, side, last):
+    h = s // 2
+    top = [(i, 0, 4, 0, s) for i in range(t)]
+    bottom = [(i, s - 4, 4, 0, s) for i in range(t)]
+    if side == 0:
+        places = top + [(0, 4, s - 8, 0, h)]
+        if last:
+            return places + [(0, s - 4, 4, 0, h)]
+        return places[: t - 1] + [(t - 1, 0, 4, 0, h)] + places[t:]
+    places = bottom + [(t - 1, 4, s - 8, h, h)]
+    if last:
+        return places + [(t - 1, 0, 4, h, h)]
+    return [(0, s - 4, 4, h, h)] + places[1:]
 
 
 def first_part(places, win_ref, w_ref, bias, u_ref):
@@ -242,22 +250,21 @@
 
 
 def inner_kernel(
-    x_hbm, w_hbm, near_hbm, bias_hbm, head_hbm,
-    u_ref, win_ref, first_ref, sum_ref, small_ref, beside_ref, mask_ref,
-    x_ref, w_ref, bias_ref, head_ref, near_ref, sems,
+    x_ref, w_ref, bias_ref, near_vmem,
+    u_ref, win_ref, first_ref, sum_ref, beside_ref, mask_ref, near_ref, sem,
 ):
     t, s, _, c = x_ref.shape
-    moves = [
-        (x_hbm, x_ref), (w_hbm, w_ref), (head_hbm, head_ref), (bias_hbm, bias_ref),
-        (near_hbm, near_ref),
-    ]
-    copies = [pltpu.make_async_copy(a, b, sems.at[i]) for i, (a, b) in enumerate(moves)]
-    for copy in copies:
-        copy.start()
-    for copy in copies[1:]:
-        copy.wait()
-    small_ref[0:1] = head_ref[...]
-    small_ref[1:2] = bias_ref[...]
+    copy = pltpu.make_async_copy(near_vmem, near_ref, sem)
+    copy.start()
+    blank = jnp.zeros((c, c), BF)
+    for b in range(3):
+        for m in range(4):
+            rows = pl.ds((m * 3 + b) * c, c)
+            for half in range(2):
+                a = m - half
+                first_ref[rows, pl.ds(half * c, c)] = w_ref[a, b] if 0 <= a < 3 else blank
+    fill_own(range(t), x_ref, win_ref)
+    copy.wait()
     start = my_index() * t
 
     def flag(yes):
@@ -274,20 +281,11 @@
                     there = start + (i - step if side == 0 else i + step)
                     mask_ref[i, side, at] = flag((near_ref[i, k] == there) & (there >= 0))
                     at += 1
-    blank = jnp.zeros((c, c), BF)
-    for b in range(3):
-        for m in range(4):
-            rows = pl.ds((m * 3 + b) * c, c)
-            for half in range(2):
-                a = m - half
-                first_ref[rows, pl.ds(half * c, c)] = w_ref[a, b] if 0 <= a < 3 else blank
-    copies[0].wait()
-    fill_own(range(t), x_ref, win_ref)
     fill_beside(range(t), beside_ref, x_ref, win_ref)
     sum_ref[...] = first_part(regions(t, s)[0], win_ref, first_ref, bias_ref[...], u_ref)
 
 
-def inner_stage(x, w, near, bias, head):
+def inner_stage(x, w, bias, near):
     t, s, _, c = x.shape
     return pl.pallas_call(
         inner_kernel,
@@ -296,39 +294,57 @@
             jax.ShapeDtypeStruct((3, t, s + 2 * D, s, c), BF),
             jax.ShapeDtypeStruct((12 * c, 2 * c), BF),
             jax.ShapeDtypeStruct((16, c), F32),
-            jax.ShapeDtypeStruct((2, c), F32),
             jax.ShapeDtypeStruct((t, 2, 16, c), BF),
             jax.ShapeDtypeStruct((t, 2, sum(REACH), 16, c), BF),
         ),
-        in_specs=[HBM] * 5,
-        out_specs=(VMEM,) * 7,
-        scratch_shapes=[
-            pltpu.VMEM(x.shape, BF),
-            pltpu.VMEM(w.shape, BF),
-            pltpu.VMEM((1, c), F32),
-            pltpu.VMEM((1, c), F32),
-            pltpu.SMEM(near.shape, jnp.int32),
-            pltpu.SemaphoreType.DMA((5,)),
-        ],
+        in_specs=[VMEM] * 4,
+        out_specs=(VMEM,) * 6,
+        scratch_shapes=[pltpu.SMEM(near.shape, jnp.int32), pltpu.SemaphoreType.DMA(())],
         compiler_params=params(),
         cost_estimate=pl.CostEstimate(
             flops=9 * t * s * s * c * c, bytes_accessed=6 << 20, transcendentals=t * s * s * c // 2
         ),
         name="inner",
-    )(*in_hbm(x, w, near, bias, head))
+    )(x, w, bias, near)
 
 
 def outer_kernel(
-    mate_ref, other_ref, w_ref, small_ref, beside_ref, mask_ref, part_ref, u_in, win_in,
-    u_ref, win_ref, to_mate_ref, to_other_ref, sum_ref, both_ref, corner_ref,
+    last, strip_ref, w_ref, bias_ref, beside_ref, mask_ref, part_ref, u_in, win_in, u_ref, win_ref, sum_ref, corner_ref,
 ):
     del u_in, win_in
+    t, s = u_ref.shape[:2]
+    parity = my_index() % 2
+
+    def run(side):
+        fill_side(side, beside_ref, mask_ref, strip_ref, win_ref, corner_ref)
+        places = side_regions(t, s, side, last)
+        sum_ref[...] = part_ref[...] + first_part(places, win_ref, w_ref, bias_ref[...], u_ref)
+
+    first = parity if last else 1 - parity
+
+    @pl.when(first == 0)
+    def _():
+        run(0)
+
+    @pl.when(first == 1)
+    def _():
+        run(1)
+
+
+def outer_mate_kernel(*refs):
+    outer_kernel(False, *refs)
+
+
+def outer_other_kernel(
+    strip_ref, w_ref, bias_ref, head_ref, beside_ref, mask_ref, part_ref, u_in, win_in,
+    u_ref, win_ref, to_mate_ref, to_other_ref, sum_ref, corner_ref,
+):
     t, s, _, c = u_ref.shape
-    fill_border(beside_ref, mask_ref, mate_ref, other_ref, win_ref, both_ref, corner_ref)
-    total = part_ref[...] + first_part(
-        regions(t, s)[1], win_ref, w_ref, small_ref[1:2], u_ref
+    outer_kernel(
+        True, strip_ref, w_ref, bias_ref, beside_ref, mask_ref, part_ref, u_in, win_in,
+        u_ref, win_ref, sum_ref, corner_ref,
     )
-    total = total * small_ref[0:1]
+    total = sum_ref[...] * head_ref[...]
     sum_ref[...] = total
     put_strips(
         u_ref.at[:, 0:D], u_ref.at[:, s - D : s],
@@ -343,10 +359,31 @@
     to_mate_ref[t, 1, 16:32] = jnp.zeros((16, c), BF)
 
 
-def outer_stage(mate, other, w, small, beside, mask, part, u, win):
+def outer_mate(strip, w, bias, beside, mask, part, u, win):
     t, s, _, c = u.shape
     return pl.pallas_call(
-        outer_kernel,
+        outer_mate_kernel,
+        out_shape=(
+            jax.ShapeDtypeStruct(u.shape, BF),
+            jax.ShapeDtypeStruct(win.shape, BF),
+            jax.ShapeDtypeStruct((16, c), F32),
+        ),
+        in_specs=[VMEM] * 8,
+        out_specs=(VMEM,) * 3,
+        input_output_aliases={6: 0, 7: 1},
+        scratch_shapes=[pltpu.VMEM((D, 16, c), BF)],
+        compiler_params=params(),
+        cost_estimate=pl.CostEstimate(
+            flops=4 * t * s * s * c * c, bytes_accessed=4 << 20, transcendentals=t * s * s * c // 4
+        ),
+        name="outer_mate",
+    )(strip, w, bias, beside, mask, part, u, win)
+
+
+def outer_other(strip, w, bias, head, beside, mask, part, u, win):
+    t, s, _, c = u.shape
+    return pl.pallas_call(
+        outer_other_kernel,
         out_shape=(
             jax.ShapeDtypeStruct(u.shape, BF),
             jax.ShapeDtypeStruct(win.shape, BF),
@@ -357,18 +394,18 @@
         in_specs=[VMEM] * 9,
         out_specs=(VMEM,) * 5,
         input_output_aliases={7: 0, 8: 1},
-        scratch_shapes=[pltpu.VMEM((2, t, D, s, c), BF), pltpu.VMEM((2, D, 16, c), BF)],
+        scratch_shapes=[pltpu.VMEM((D, 16, c), BF)],
         compiler_params=params(),
         cost_estimate=pl.CostEstimate(
-            flops=9 * t * s * s * c * c, bytes_accessed=4 << 20, transcendentals=t * s * s * c // 2
-        ),
-        name="outer",
-    )(mate, other, w, small, beside, mask, part, u, win)
-
-
-def turn(first_ref, small_ref, second_ref):
+            flops=4 * t * s * s * c * c, bytes_accessed=4 << 20, transcendentals=t * s * s * c // 4
+        ),
+        name="outer_other",
+    )(strip, w, bias, head, beside, mask, part, u, win)
+
+
+def turn(first_ref, head_ref, second_ref):
     c = first_ref.shape[1] // 2
-    head = small_ref[0:1] * (1.0 / KEPT)
+    head = head_ref[...] * (1.0 / KEPT)
     for a in range(3):
         for b in range(3):
             rows = pl.ds((a * 3 + b) * c, c)
@@ -387,32 +424,41 @@
     second_part(places, win_ref, w_ref, v_ref)
 
 
-def back_inner_kernel(
-    u_ref, first_ref, small_ref, beside_ref, label_ref, win_ref, v_ref, w_ref, row_ref
-):
+def turned(first, head):
+    c = head.shape[1]
+    return pl.pallas_call(
+        turn,
+        out_shape=jax.ShapeDtypeStruct((9 * c, 2 * c), BF),
+        in_specs=[VMEM, VMEM],
+        out_specs=VMEM,
+        compiler_params=params(),
+        cost_estimate=pl.CostEstimate(flops=0, bytes_accessed=1 << 20, transcendentals=0),
+        name="turn",
+    )(first, head)
+
+
+def back_inner_kernel(u_ref, w_ref, beside_ref, label_ref, win_ref, v_ref, row_ref):
     row_ref[...] = jnp.full(row_ref.shape, label_ref[0], jnp.int32).astype(F32)
-    turn(first_ref, small_ref, w_ref)
     back_tiles(range(u_ref.shape[0]), u_ref, w_ref, beside_ref, win_ref, v_ref)
 
 
-def back_inner(u, first, small, beside, label):
+def back_inner(u, w, beside, label):
     t, s, _, c = u.shape
     return pl.pallas_call(
         back_inner_kernel,
         out_shape=(
             jax.ShapeDtypeStruct((3, t, s + 2 * D, s, c), BF),
             jax.ShapeDtypeStruct(u.shape, F32),
-            jax.ShapeDtypeStruct((9 * c, 2 * c), BF),
             jax.ShapeDtypeStruct((8, c), F32),
         ),
-        in_specs=[VMEM] * 4 + [SMEM],
-        out_specs=(VMEM,) * 4,
+        in_specs=[VMEM] * 3 + [SMEM],
+        out_specs=(VMEM,) * 3,
         compiler_params=params(),
         cost_estimate=pl.CostEstimate(
             flops=16 * t * s * s * c * c, bytes_accessed=8 << 20, transcendentals=0
         ),
         name="back_inner",
-    )(u, first, small, beside, label)
+    )(u, w, beside, label)
 
 
 def gate_kernel(strip_ref, sum_ref, out_ref):
@@ -435,7 +481,11 @@
 def back_outer_kernel(mate_ref, other_ref, w_ref, beside_ref, mask_ref, win_in, v_in, win_ref, v_ref, both_ref, corner_ref):
     del win_in, v_in
     t, s = v_ref.shape[:2]
-    fill_border(beside_ref, mask_ref, mate_ref, other_ref, win_ref, both_ref, corner_ref)
+    parity = my_index() % 2
+    both_ref[0] = mate_ref[0:t]
+    both_ref[1] = other_ref[0:t]
+    for side, strip_ref in enumerate((both_ref.at[1 - parity], both_ref.at[parity])):
+        fill_side(side, beside_ref, mask_ref, strip_ref, win_ref, corner_ref.at[side])
     second_part(regions(t, s)[1], win_ref, w_ref, v_ref)
 
 
@@ -491,11 +541,11 @@
     t, s, _, c = tissue_tiles.shape
     size = lax.axis_size(GROUP)
     mate, other = swap(*make_strips(tissue_tiles))
-    u, win, w_first, part, small, beside, mask = inner_stage(
-        tissue_tiles, conv_weight, neighbours, conv_bias.reshape(1, c), head_weight.reshape(1, c)
-    )
-    u, _, mate, other, mine = outer_stage(
-        mate, other, w_first, small, beside, mask, part, u, win
+    bias, head = conv_bias.reshape(1, c), head_weight.reshape(1, c)
+    u, win, w_first, part, beside, mask = inner_stage(tissue_tiles, conv_weight, bias, neighbours)
+    u, win, part = outer_mate(mate, w_first, bias, beside, mask, part, u, win)
+    u, _, mate, other, mine = outer_other(
+        other, w_first, bias, head, beside, mask, part, u, win
     )
     mate, _ = swap(mate, None)
     got = mate[t].astype(F32)
@@ -510,7 +560,8 @@
         theirs = lax.ppermute(mine, GROUP, [(i, i ^ step) for i in range(size)])
         step *= 2
     _, other = swap(None, other)
-    win, v, w_second, label = back_inner(u, w_first, small, beside, slide_label)
+    w_second = turned(w_first, head)
+    win, v, label = back_inner(u, w_second, beside, slide_label)
     v = back_outer(mate, other, w_second, beside, mask, win, v)
     return scale(label, mine, theirs, v, float(t * size * s * s * c))
 

time: 25.5 us -> 25.2 us (0.988)
  Pallas kernels: 10.4 us -> 9.8 us
    pallas_call x1, Pallas kernels: 3.05 us -> 2.21 us  [inner_stage(): pl.pallas_call(inner_kernel, out_shape=(jax.ShapeDtypeStruct(x.shape, BF)...]
    pallas_call x1 -> x3, Pallas kernels: 1.15 us -> 1.58 us  [the longest x1 0.73 us: outer_other(): pl.pallas_call(outer_other_kernel, out_shape=(jax.ShapeDtypeStruct(u.shap...]
  transfers between devices with their start and end apart: 7 -> 7, of which waited for: 4 -> 3; matrix products, arithmetic and copies ran while one was open for 0% -> 0% of each run, Pallas kernels for 26% -> 25%
where the time goes in v5:
time: 25.2 us; the launch traced here: 25 us
  starting transfers between devices  12.4 us (49%)
  Pallas kernels  9.8 us (39%)
  waiting for transfers between devices  2 us (8%)
  between operations  0.79 us (3%)
    ppermute x3, starting transfers between devices, body(): theirs = lax.ppermute(mine, GROUP, [(i, i ^ step) for i in range(size)])  6.55 us
    ppermute x2, starting transfers between devices, swap(): lax.ppermute(mate, GROUP, mates)  4.52 us
    pallas_call x1, Pallas kernels, inner_stage(): pl.pallas_call(inner_kernel, out_shape=(jax.ShapeDtypeStruct(x.shape, BF)...  2.21 us
    ppermute x3, waiting for transfers between devices, body(): theirs = lax.ppermute(mine, GROUP, [(i, i ^ step) for i in range(size)])  1.97 us
    pallas_call x1, Pallas kernels, back_inner(): pl.pallas_call(back_inner_kernel, out_shape=(jax.ShapeDtypeStruct((3, t,...  1.89 us
    pallas_call x1, Pallas kernels, scale(): pl.pallas_call(functools.partial(scale_kernel, count), out_shape=jax.Shap...  1.55 us
    pallas_call x1, Pallas kernels, back_outer(): pl.pallas_call(back_outer_kernel, out_shape=(jax.ShapeDtypeStruct(win.sha...  1.4 us
    ppermute x2, starting transfers between devices, swap(): lax.ppermute(other, GROUP, others)  1.31 us
  transfers between devices with their start and end apart: 7, of which 3 were waited for; matrix products, arithmetic and copies ran while one was open for 0% of the time, Pallas kernels for 25%

profile of v5, /device:TPU:0, one launch (start us, length us, event | category | flops | bytes accessed | tf_op | source)
XLA Modules:
  0.0 25.0 jit_solution(17127774475300484370)
XLA Ops:
  0.0 0.0 copy-start.2
  0.0 0.0 copy-start.1
  0.0 0.0 copy-start.4
  0.0 0.0 copy-start.3
  0.0 1.2 %strips.1 = (bf16[4,2,32,128]{3,2,1,0:T(8,128)(2,1)S(1)}, bf16[4,2,32,128]{3,2,1,0:T(8,128)(2,1)S(1)}) custom-call(bf16[4,32,32,128]{3,2,1,0:T(8,128)(2,1)} %x_ref.3), custom_call_target="tpu_custom_call" | custom-call | flops 4294967296 | bytes 8388608 | tf_op jit(solution)/shard_map/strips/pallas_call | solution.py:83
  1.2 0.6 %collective-permute-start.1 = (bf16[4,2,32,128]{3,2,1,0:T(8,128)(2,1)S(1)}, bf16[4,2,32,128]{3,2,1,0:T(8,128)(2,1)S(1)}, u32[]{:S(2)}, u32[]{:S(2)}) collective-permute-start(bf16[4,2,32,128]{3,2,1,0:T(8,128)(2,1)S(1)} %get-tuple-element.28), channel_id=1, source_target_pairs={{0,1},{1,0},{2,3},{3,2},{4,5},{5,4},{6,7},{7,6},{8,9},{9,8},{10,11... | collective-permute-start | bytes 196616 | tf_op jit(solution)/shard_map/ppermute | solution.py:102
  1.8 0.7 %collective-permute-start = (bf16[4,2,32,128]{3,2,1,0:T(8,128)(2,1)S(1)}, bf16[4,2,32,128]{3,2,1,0:T(8,128)(2,1)S(1)}, u32[]{:S(2)}, u32[]{:S(2)}) collective-permute-start(bf16[4,2,32,128]{3,2,1,0:T(8,128)(2,1)S(1)} %get-tuple-element.24), channel_id=1, source_target_pairs={{1,2},{2,1},{3,4},{4,3},{5,6},{6,5},{7,8},{8,7},{9,10},{10,9},{11,... | collective-permute-start | bytes 196616 | tf_op jit(solution)/shard_map/ppermute | solution.py:103
  2.4 0.0 copy-done.2
  2.4 0.0 copy-done.1
  2.4 0.0 copy-done.4
  2.4 0.0 copy-done.3
  2.5 0.0 copy-start
  2.5 2.2 %inner.1 = (bf16[4,32,32,128]{3,2,1,0:T(8,128)(2,1)S(1)}, bf16[3,4,36,32,128]{4,3,2,1,0:T(8,128)(2,1)S(1)}, bf16[1536,256]{1,0:T(8,128)(2,1)S(1)}, f32[16,128]{1...) custom-call(bf16[4,32,32,128]{3,2,1,0:T(8,128)(2,1)S(1)} %copy-done.2, ...), custom_call_target="tpu_custom_call" | custom-call | flops 603979776 | bytes 6291456 | tf_op jit(solution)/shard_map/inner/pallas_call | solution.py:290
  4.7 0.0 collective-permute-done.1.refs_0_
  4.7 0.6 %outer_mate.1 = (bf16[4,32,32,128]{3,2,1,0:T(8,128)(2,1)S(1)}, bf16[3,4,36,32,128]{4,3,2,1,0:T(8,128)(2,1)S(1)}, f32[16,128]{1,0:T(8,128)S(1)}) custom-call(bf16[4,2,32,128]{3,2,1,0:T(8,128)(2,1)S(1)} %collective-permute-done.1.refs_0_, ...), custom_call_target="tpu_custom_call", output_to_operand_aliasing={{0}: (6, {}), {1}: (7, {})} | custom-call | flops 268435456 | bytes 4194304 | tf_op jit(solution)/shard_map/outer_mate/pallas_call | solution.py:364
  5.3 0.0 collective-permute-done.strip_ref
  5.3 0.0 copy-done
  5.3 0.7 %outer_other.1 = (bf16[4,32,32,128]{3,2,1,0:T(8,128)(2,1)S(1)}, bf16[3,4,36,32,128]{4,3,2,1,0:T(8,128)(2,1)S(1)}, bf16[5,2,32,128]{3,2,1,0:T(8,128)(2,1)S(1)}, b...) custom-call(bf16[4,2,32,128]{3,2,1,0:T(8,128)(2,1)S(1)} %collective-permute-done.stri, ...), custom_call_target="tpu_custom_call", output_to_operand_aliasing={{0}: (7, {}), {1}: (8, {})} | custom-call | flops 268435456 | bytes 4194304 | tf_op jit(solution)/shard_map/outer_other/pallas_call | solution.py:385
  6.1 4.0 %collective-permute-start.2 = (bf16[5,2,32,128]{3,2,1,0:T(8,128)(2,1)S(1)}, bf16[5,2,32,128]{3,2,1,0:T(8,128)(2,1)S(1)}, u32[]{:S(2)}, u32[]{:S(2)}) collective-permute-start(bf16[5,2,32,128]{3,2,1,0:T(8,128)(2,1)S(1)} %get-tuple-element.38), channel_id=1, source_target_pairs={{0,1},{1,0},{2,3},{3,2},{4,5},{5,4},{6,7},{7,6},{8,9},{9,8},{10,11... | collective-permute-start | bytes 245768 | tf_op jit(solution)/shard_map/ppermute | solution.py:102
  10.0 0.2 turn.1.w_ref
  10.9 0.0 collective-permute-done.2.mate_ref
  11.0 2.0 %collective-permute-start.3 = (f32[16,128]{1,0:T(8,128)S(1)}, f32[16,128]{1,0:T(8,128)S(1)}, u32[]{:S(2)}, u32[]{:S(2)}) collective-permute-start(f32[16,128]{1,0:T(8,128)S(1)} %fusion.2.sum_ref), channel_id=1, source_target_pairs={{0,2},{1,3},{2,0},{3,1},{4,6},{5,7},{6,4},{7,5},{8,10},{9,11},{10,... | collective-permute-start | bytes 24584 | tf_op jit(solution)/shard_map/ppermute | solution.py:560
  13.0 0.7 %collective-permute-start.6 = (bf16[4,2,32,128]{3,2,1,0:T(8,128)(2,1)S(1)}, bf16[4,2,32,128]{3,2,1,0:T(8,128)(2,1)S(1)}, u32[]{:S(2)}, u32[]{:S(2)}) collective-permute-start(bf16[4,2,32,128]{3,2,1,0:T(8,128)(2,1)S(1)} %gate.1), channel_id=1, source_target_pairs={{1,2},{2,1},{3,4},{4,3},{5,6},{6,5},{7,8},{8,7},{9,10},{10,9},{11,... | collective-permute-start | bytes 196616 | tf_op jit(solution)/shard_map/ppermute | solution.py:103
  13.7 1.0 %collective-permute-done.3 = f32[16,128]{1,0:T(8,128)S(1)} collective-permute-done((f32[16,128]{1,0:T(8,128)S(1)}, f32[16,128]{1,0:T(8,128)S(1)}, u32[]{:S(2)}, u32[]{:S(2)}) %collective-permute-start.3) | collective-permute-done | bytes 8224 | tf_op jit(solution)/shard_map/ppermute | solution.py:560
  14.7 2.0 %collective-permute-start.4 = (f32[16,128]{1,0:T(8,128)S(1)}, f32[16,128]{1,0:T(8,128)S(1)}, u32[]{:S(2)}, u32[]{:S(2)}) collective-permute-start(f32[16,128]{1,0:T(8,128)S(1)} %add.23), channel_id=1, source_target_pairs={{0,4},{1,5},{2,6},{3,7},{4,0},{5,1},{6,2},{7,3},{8,12},{9,13},{10,... | collective-permute-start | bytes 24584 | tf_op jit(solution)/shard_map/ppermute | solution.py:560
  16.7 1.9 %back_inner.1 = (bf16[3,4,36,32,128]{4,3,2,1,0:T(8,128)(2,1)S(1)}, f32[4,32,32,128]{3,2,1,0:T(8,128)S(1)}, f32[8,128]{1,0:T(8,128)S(1)}) custom-call(bf16[4,32,32,128]{3,2,1,0:T(8,128)(2,1)S(1)} %get-tuple-element.35.u_ref, bf16[1152,256]{1,0:T(8,128)(2,1)S(1)} %turn.1.w_ref, bf16[4,2,16,128]{3,2,1,0:T(8,128)(2,1)S(1)} %get-tuple-element.26.refs_3_.beside_ref, ...), custom_call_target="tpu_custom_call" | custom-call | flops 1073741824 | bytes 8388608 | tf_op jit(solution)/shard_map/back_inner/pallas_call | solution.py:447
  18.6 0.3 %collective-permute-done.4 = f32[16,128]{1,0:T(8,128)S(1)} collective-permute-done((f32[16,128]{1,0:T(8,128)S(1)}, f32[16,128]{1,0:T(8,128)S(1)}, u32[]{:S(2)}, u32[]{:S(2)}) %collective-permute-start.4) | collective-permute-done | bytes 8224 | tf_op jit(solution)/shard_map/ppermute | solution.py:560
  18.9 2.5 %collective-permute-start.5 = (f32[16,128]{1,0:T(8,128)S(1)}, f32[16,128]{1,0:T(8,128)S(1)}, u32[]{:S(2)}, u32[]{:S(2)}) collective-permute-start(f32[16,128]{1,0:T(8,128)S(1)} %add.24.mine_ref), channel_id=1, source_target_pairs={{0,8},{1,9},{2,10},{3,11},{4,12},{5,13},{6,14},{7,15},{8,0},{9,1},... | collective-permute-start | bytes 24584 | tf_op jit(solution)/shard_map/ppermute | solution.py:560
  21.4 0.0 collective-permute-done.6.other_ref
  21.4 1.4 %back_outer.1 = (bf16[3,4,36,32,128]{4,3,2,1,0:T(8,128)(2,1)S(1)}, f32[4,32,32,128]{3,2,1,0:T(8,128)S(1)}) custom-call(bf16[5,2,32,128]{3,2,1,0:T(8,128)(2,1)S(1)} %collective-permute-done.2.mate_ref, bf16[4,2,32,128]{3,2,1,0:T(8,128)(2,1)S(1)} %collective-permute-done.6.other_ref, ...), custom_call_target="tpu_custom_call", output_to_operand_aliasing={{0}: (5, {}), {1}: (6, {})} | custom-call | flops 536870912 | bytes 2097152 | tf_op jit(solution)/shard_map/back_outer/pallas_call | solution.py:494
  22.8 0.7 %collective-permute-done.5.theirs_ref = f32[16,128]{1,0:T(8,128)S(1)} collective-permute-done((f32[16,128]{1,0:T(8,128)S(1)}, f32[16,128]{1,0:T(8,128)S(1)}, u32[]{:S(2)}, u32[]{:S(2)}) %collective-permute-start.5) | collective-permute-done | bytes 8224 | tf_op jit(solution)/shard_map/ppermute | solution.py:560
  23.4 1.6 %scale.1 = f32[4,32,32,128]{3,2,1,0:T(8,128)} custom-call(f32[8,128]{1,0:T(8,128)S(1)} %get-tuple-element.36.label_ref, f32[16,128]{1,0:T(8,128)S(1)} %add.24.mine_ref, f32[16,128]{1,0:T(8,128)S(1)} %collective-permute-done.5.theirs_ref, f32[4,32,32,128]{3,2,1,0:T(8,128)S(1)} %get-tuple-element.42.v_ref), custom_call_target="tpu_custom_call" | custom-call | tf_op jit(solution)/shard_map/scale/pallas_call | solution.py:529
  (5 shorter events, 0.0 us)
Async XLA Ops:
  0.0 2.4 %copy-start.2 = (bf16[4,32,32,128]{3,2,1,0:T(8,128)(2,1)S(1)}, bf16[4,32,32,128]{3,2,1,0:T(8,128)(2,1)}, u32[]{:S(2)}) copy-start(bf16[4,32,32,128]{3,2,1,0:T(8,128)(2,1)} %x_ref.3) | copy-start | bytes 3145732
  0.0 2.4 %copy-start.1 = (f32[128]{0:T(128)S(1)}, f32[128]{0:T(128)}, u32[]{:S(2)}) copy-start(f32[128]{0:T(128)} %param.9) | copy-start | bytes 1540
  0.0 2.4 %copy-start.4 = (s32[4,8]{1,0:T(4,128)S(1)}, s32[4,8]{1,0:T(4,128)}, u32[]{:S(2)}) copy-start(s32[4,8]{1,0:T(4,128)} %near_vmem.1) | copy-start | bytes 388
  0.0 2.4 %copy-start.3 = (bf16[3,3,128,128]{3,2,1,0:T(8,128)(2,1)S(1)}, bf16[3,3,128,128]{3,2,1,0:T(8,128)(2,1)}, u32[]{:S(2)}) copy-start(bf16[3,3,128,128]{3,2,1,0:T(8,128)(2,1)} %w_ref.1) | copy-start | bytes 884740
  1.2 3.5 %collective-permute-start.1 = (bf16[4,2,32,128]{3,2,1,0:T(8,128)(2,1)S(1)}, bf16[4,2,32,128]{3,2,1,0:T(8,128)(2,1)S(1)}, u32[]{:S(2)}, u32[]{:S(2)}) collective-permute-start(bf16[4,2,32,128]{3,2,1,0:T(8,128)(2,1)S(1)} %get-tuple-element.28), channel_id=1, source_target_pairs={{0,1},{1,0},{2,3},{3,2},{4,5},{5,4},{6,7},{7,6},{8,9},{9,8},{10,11... | collective-permute-start | bytes 196616 | tf_op jit(solution)/shard_map/ppermute | solution.py:102
  1.8 3.6 %collective-permute-start = (bf16[4,2,32,128]{3,2,1,0:T(8,128)(2,1)S(1)}, bf16[4,2,32,128]{3,2,1,0:T(8,128)(2,1)S(1)}, u32[]{:S(2)}, u32[]{:S(2)}) collective-permute-start(bf16[4,2,32,128]{3,2,1,0:T(8,128)(2,1)S(1)} %get-tuple-element.24), channel_id=1, source_target_pairs={{1,2},{2,1},{3,4},{4,3},{5,6},{6,5},{7,8},{8,7},{9,10},{10,9},{11,... | collective-permute-start | bytes 196616 | tf_op jit(solution)/shard_map/ppermute | solution.py:103
  2.5 2.9 %copy-start = (f32[128]{0:T(128)S(1)}, f32[128]{0:T(128)}, u32[]{:S(2)}) copy-start(f32[128]{0:T(128)} %param.10) | copy-start | bytes 1540
  6.1 4.9 %collective-permute-start.2 = (bf16[5,2,32,128]{3,2,1,0:T(8,128)(2,1)S(1)}, bf16[5,2,32,128]{3,2,1,0:T(8,128)(2,1)S(1)}, u32[]{:S(2)}, u32[]{:S(2)}) collective-permute-start(bf16[5,2,32,128]{3,2,1,0:T(8,128)(2,1)S(1)} %get-tuple-element.38), channel_id=1, source_target_pairs={{0,1},{1,0},{2,3},{3,2},{4,5},{5,4},{6,7},{7,6},{8,9},{9,8},{10,11... | collective-permute-start | bytes 245768 | tf_op jit(solution)/shard_map/ppermute | solution.py:102
  11.0 3.7 %collective-permute-start.3 = (f32[16,128]{1,0:T(8,128)S(1)}, f32[16,128]{1,0:T(8,128)S(1)}, u32[]{:S(2)}, u32[]{:S(2)}) collective-permute-start(f32[16,128]{1,0:T(8,128)S(1)} %fusion.2.sum_ref), channel_id=1, source_target_pairs={{0,2},{1,3},{2,0},{3,1},{4,6},{5,7},{6,4},{7,5},{8,10},{9,11},{10,... | collective-permute-start | bytes 24584 | tf_op jit(solution)/shard_map/ppermute | solution.py:560
  13.0 8.4 %collective-permute-start.6 = (bf16[4,2,32,128]{3,2,1,0:T(8,128)(2,1)S(1)}, bf16[4,2,32,128]{3,2,1,0:T(8,128)(2,1)S(1)}, u32[]{:S(2)}, u32[]{:S(2)}) collective-permute-start(bf16[4,2,32,128]{3,2,1,0:T(8,128)(2,1)S(1)} %gate.1), channel_id=1, source_target_pairs={{1,2},{2,1},{3,4},{4,3},{5,6},{6,5},{7,8},{8,7},{9,10},{10,9},{11,... | collective-permute-start | bytes 196616 | tf_op jit(solution)/shard_map/ppermute | solution.py:103
  14.7 4.2 %collective-permute-start.4 = (f32[16,128]{1,0:T(8,128)S(1)}, f32[16,128]{1,0:T(8,128)S(1)}, u32[]{:S(2)}, u32[]{:S(2)}) collective-permute-start(f32[16,128]{1,0:T(8,128)S(1)} %add.23), channel_id=1, source_target_pairs={{0,4},{1,5},{2,6},{3,7},{4,0},{5,1},{6,2},{7,3},{8,12},{9,13},{10,... | collective-permute-start | bytes 24584 | tf_op jit(solution)/shard_map/ppermute | solution.py:560
  18.9 4.5 %collective-permute-start.5 = (f32[16,128]{1,0:T(8,128)S(1)}, f32[16,128]{1,0:T(8,128)S(1)}, u32[]{:S(2)}, u32[]{:S(2)}) collective-permute-start(f32[16,128]{1,0:T(8,128)S(1)} %add.24.mine_ref), channel_id=1, source_target_pairs={{0,8},{1,9},{2,10},{3,11},{4,12},{5,13},{6,14},{7,15},{8,0},{9,1},... | collective-permute-start | bytes 24584 | tf_op jit(solution)/shard_map/ppermute | solution.py:560
